TPU v7x, 256 devices: a whole 4x4x8 slice. The times are simulated.
256 devices in a mesh: tm: 32 (over x, z), freq: 2 (over core), rec: 4 (over y).
Axes of the slice: x: 4, y: 4, z: 8, core: 2. Of those that a mesh axis runs over, the one named last changes fastest.
Arguments:
- tokens: bfloat16 [10240, 768], P(('rec', 'tm', 'freq')), parts along dimension 0, may hold values from -6 to 6
- placement: int32 [2, 10240], P(None, ('rec', 'tm', 'freq')), parts along dimension 1, may hold values from 0 to 1599, as said below
- patch_mask: int32 [6400, 8], P(('rec', 'tm'), 'freq'), parts along dimension 0, may hold values from 0 to 1, as said below
- targets: bfloat16 [6400, 8, 256], P(('rec', 'tm'), 'freq'), parts along dimension 0, may hold values from -6 to 6
- in_weight: bfloat16 [768, 384], replicated, may hold values from -0.21875 to 0.21875
- mask_token: bfloat16 [384], replicated, may hold values from -5 to 5
- conv_weight: bfloat16 [2, 3456, 384], replicated, may hold values from -0.109375 to 0.109375
- head_weight: bfloat16 [384, 256], replicated, may hold values from -0.3125 to 0.3125
Outputs:
- prediction: bfloat16 [6400, 8, 256], P(('rec', 'tm'), 'freq'), parts along dimension 0
- token_grad: float32 [10240, 768], P(('rec', 'tm', 'freq')), parts along dimension 0
- conv_grad: float32 [8, 3456, 384], P('rec', ('tm', 'freq')), parts along dimension 0
There are 4 independent parts, one for each index of `rec`. A program takes and returns all parts, laid end to end along the dimension named above; an argument that names none is the same for every part. Nothing has to cross between parts.
Inputs may be any that keep to these rules, and one draw needn't show every extreme that they name: `patch_mask`: exactly 2560 patches are visible; each tile of 50 x 4 patches (tile index = time tile times 2 plus frequency tile) holds at most 80 visible ones, a bound reached in every draw. `placement`: every visible patch is named by exactly one token, no masked patch by any; the first row stays below 1600 and the second below 8; the 40 tokens of one shard name at most 2 patches of any one tile, a bound reached in every draw.
All inputs are finite; a program needn't handle non-finite values.
Results may differ from a plain program's by a relative error of at most 0.0085.
Values may be sent and summed in bfloat16 or wider, within the bound.
No kernel may reach another device: no remote copies, remote signals or barrier semaphores. Data moves between devices by JAX's collectives and lax.ppermute only.
A program may use at most 64 MiB of HBM per device.

v0:
```python
import jax
import jax.numpy as jnp
from jax import lax
from jax.experimental import pallas as pl
from jax.experimental.pallas import tpu as pltpu
from jax.sharding import Mesh
from jax.sharding import PartitionSpec as P

TM = ("tm_0", "tm_1")
TM_FREQ = ("tm_0", "tm_1", "freq")
REC_TM_FREQ = ("rec", "tm_0", "tm_1", "freq")
REC_TM = ("rec", "tm_0", "tm_1")

F32 = jnp.float32
BF16 = jnp.bfloat16
ROWS = 50
COLS = 8
CELLS = ROWS * COLS
CHANNELS = 384
DEPTH = 3 * CHANNELS
PIX = 256
SLOTS = 4
ERF_SCALE = 0.7071067811865476
PDF_SCALE = 0.3989422804014327
ERF_TOP = (
    0.00022905065861350646,
    0.0034082910107109506,
    0.050955695062380861,
    0.18520832239976145,
    1.128379143519084,
)
ERF_BOTTOM = (
    -1.1791602954361697e-7,
    0.000023547966471313185,
    0.0010179625278914885,
    0.014070470171167667,
    0.11098505178285362,
    0.49746925110067538,
    1.0,
)


def horner(value, factors):
    total = jnp.full_like(value, factors[0])
    for factor in factors[1:]:
        total = total * value + factor
    return total


def erf(value):
    bounded = jnp.clip(value, -3.7439211627767994, 3.7439211627767994)
    square = bounded * bounded
    return bounded * horner(square, ERF_TOP) / horner(square, ERF_BOTTOM)


def half_erf(unit):
    return 0.5 * (1.0 + erf(unit * ERF_SCALE))


def column_shifted(value):
    cells, channels = value.shape
    grid = value.reshape(cells // 8, 8, channels)
    column = lax.broadcasted_iota(jnp.int32, grid.shape, 1)
    lower = jnp.where(column == 0, 0.0, pltpu.roll(grid, 1, axis=1))
    upper = jnp.where(column == 7, 0.0, pltpu.roll(grid, 7, axis=1))
    return lower.reshape(value.shape), value, upper.reshape(value.shape)


def store_columns(value, even, odd):
    cells, channels = value.shape
    for part, shifted in enumerate(column_shifted(value)):
        lanes = slice(part * channels, (part + 1) * channels)
        even[0:cells, lanes] = shifted.astype(BF16)
        odd[0 : cells - 8, lanes] = shifted[8:].astype(BF16)


def conv_taps(even, odd, weight, cells):
    summed = jnp.dot(even[0:cells], weight[0, 0:DEPTH], preferred_element_type=F32)
    summed += jnp.dot(odd[0:cells], weight[0, DEPTH : 2 * DEPTH], preferred_element_type=F32)
    summed += jnp.dot(
        even[16 : 16 + cells], weight[0, 2 * DEPTH : 3 * DEPTH], preferred_element_type=F32
    )
    return summed


def conv_back(grad, weight, cells):
    summed = None
    for row_off in range(3):
        term = lax.dot_general(
            grad,
            weight[0, row_off * DEPTH : (row_off + 1) * DEPTH],
            (((1,), (1,)), ((), ())),
            preferred_element_type=F32,
        )
        term = term[8 * (2 - row_off) : 8 * (2 - row_off) + cells]
        summed = term if summed is None else summed + term
    grid = (cells // 8, 8, CHANNELS)
    column = lax.broadcasted_iota(jnp.int32, grid, 1)
    first = summed[:, 0:CHANNELS].reshape(grid)
    last = summed[:, 2 * CHANNELS :].reshape(grid)
    total = jnp.where(column == 7, 0.0, pltpu.roll(first, 7, axis=1))
    total += jnp.where(column == 0, 0.0, pltpu.roll(last, 1, axis=1))
    return summed[:, CHANNELS : 2 * CHANNELS] + total.reshape(cells, CHANNELS)


def normed(conv_out):
    center = conv_out - jnp.mean(conv_out, axis=-1, keepdims=True)
    scale = lax.rsqrt(jnp.mean(center * center, axis=-1, keepdims=True) + 1e-05)
    return center * scale, scale


def pull_back(unit, scale, gradient):
    slope = half_erf(unit) + unit * (PDF_SCALE * jnp.exp(-0.5 * unit * unit))
    grad = gradient * slope
    mean = jnp.mean(grad, axis=-1, keepdims=True)
    along = jnp.mean(grad * unit, axis=-1, keepdims=True)
    return scale * (grad - mean - unit * along)


def rows_valid(place_ref, cells, before):
    row = lax.shift_right_logical(lax.broadcasted_iota(jnp.int32, (cells, 1), 0), 3)
    row = row + place_ref[0] * ROWS - before
    return (row >= 0) & (row < place_ref[2] * ROWS)


def place_kernel(arrived, aim, token, x_out, chosen_out):
    notes = arrived[:, CHANNELS : CHANNELS + 128].astype(F32)
    cell = notes[:, 0:1] * 8.0 + notes[:, 1:2]
    cell = jnp.where(notes[:, 2:3] == 1.0, cell, -1.0).astype(jnp.int32)
    slots = arrived.shape[0]
    chosen = jnp.where(lax.broadcasted_iota(jnp.int32, (slots, CELLS), 1) == cell, 1.0, 0.0)
    chosen = chosen.astype(BF16)
    chosen_out[...] = chosen
    placed = lax.dot_general(
        chosen, arrived[:, 0:CHANNELS], (((0,), (0,)), ((), ())), preferred_element_type=F32
    )
    masked = aim[16 : 16 + CELLS, PIX : PIX + 1] == 1.0
    x_out[...] = jnp.where(masked, token[...].astype(F32), placed).astype(BF16)


def first_kernel(
    place_ref, above, own, below, weight, active_out, unit_out, scale_out, share_out, even, odd
):
    source = jnp.concatenate(
        [above[...].astype(F32), own[...].astype(F32), below[...].astype(F32)], axis=0
    )
    store_columns(source, even, odd)
    unit, scale = normed(conv_taps(even, odd, weight, 448))
    unit_out[...] = unit[16:432]
    scale_out[...] = jnp.broadcast_to(scale[16:432], (416, 128))
    active = source[8:456] + unit * half_erf(unit)
    active = jnp.where(rows_valid(place_ref, 448, 3), active, 0.0)
    active_out[...] = active.astype(BF16)
    share_out[...] = jnp.where(place_ref[1] == 1, active[16:432], source[24:440]).astype(BF16)


def second_kernel(
    place_ref, active_ref, unit_ref, scale_ref, weight, head, aim,
    pred, share_out, mid_out, grad_out, even, odd,
):
    active = active_ref[...].astype(F32)
    store_columns(active, even, odd)
    unit, scale = normed(conv_taps(even, odd, weight, 432))
    top = (active[8:440] + unit * half_erf(unit)).astype(BF16)
    guess = jnp.dot(top, head[...], preferred_element_type=F32)
    pred[...] = guess[16:416].astype(BF16)
    misfit = jnp.where(
        aim[:, PIX : PIX + 1] == 1.0, (guess - aim[:, 0:PIX].astype(F32)) * 0.0625, 0.0
    ).astype(BF16)
    grad_top = lax.dot_general(
        misfit, head[...], (((1,), (1,)), ((), ())), preferred_element_type=F32
    )
    grad_two = pull_back(unit, scale, grad_top).astype(BF16)
    grad_mid = grad_top[8:424] + conv_back(grad_two, weight, 416)
    grad_one = pull_back(unit_ref[...], scale_ref[:, 0:1], grad_mid)
    grad_one = jnp.where(rows_valid(place_ref, 416, 1), grad_one, 0.0)
    grad_out[...] = grad_one.astype(BF16)
    mid_out[...] = grad_mid[8:408]
    share_out[...] = jnp.where(
        place_ref[1] == 1, grad_two.astype(F32)[16:416], grad_one[8:408]
    ).astype(BF16)


def tail_kernel(grad_ref, mid_ref, weight, chosen, out):
    grad_cells = mid_ref[...] + conv_back(grad_ref[...], weight, CELLS)
    out[...] = jnp.dot(chosen[...], grad_cells.astype(BF16), preferred_element_type=F32).astype(
        BF16
    )


def weight_kernel(place_ref, *refs):
    inner, outer = refs[0:4], refs[4:8]
    out, turned, moved, total = refs[8:]
    first_tap = place_ref[3] * 2
    for part in range(4):
        turned[part] = inner[part][...].astype(F32).T.astype(BF16)
    moved[...] = jnp.zeros_like(moved)
    for step in range(3):
        tap = first_tap + step
        row_off = jnp.where(tap >= 6, 2, jnp.where(tap >= 3, 1, 0))
        col_off = tap - 3 * row_off
        start = pl.multiple_of(row_off * 8, 8)
        summed = None
        for part in range(4):
            low, middle, high = column_shifted(outer[part][...].astype(F32))
            piece = jnp.where(col_off == 0, high, jnp.where(col_off == 1, middle, low))
            slot = 4 * step + part
            moved[slot, pl.ds(start, CELLS), :] = piece
            term = jnp.dot(
                turned[part], moved[slot].astype(BF16), preferred_element_type=F32
            )
            summed = term if summed is None else summed + term
        total[step * CHANNELS : (step + 1) * CHANNELS] = summed
    base = pl.multiple_of(place_ref[3] * 96, 8)
    kept = total[pl.ds(base, 864), :]
    for block in range(16):
        out[block] = kept[54 * block : 54 * (block + 1)].astype(BF16)


VMEM = pl.BlockSpec(memory_space=pltpu.VMEM)
SMEM = pl.BlockSpec(memory_space=pltpu.SMEM)


def call(kernel, name, shapes, scratch, cost, *operands, scalars=True, specs=None):
    in_specs = [SMEM] + [VMEM] * (len(operands) - 1) if scalars else [VMEM] * len(operands)
    return pl.pallas_call(
        kernel,
        out_shape=shapes,
        in_specs=specs or in_specs,
        out_specs=jax.tree.map(lambda _: VMEM, shapes),
        scratch_shapes=scratch,
        compiler_params=pltpu.CompilerParams(vmem_limit_bytes=56 << 20),
        cost_estimate=pl.CostEstimate(
            flops=cost, bytes_accessed=cost // 400, transcendentals=0
        ),
        name=name,
    )(*operands)


def shape(dims, dtype=BF16):
    return jax.ShapeDtypeStruct(dims, dtype)


def send(value, axis, step, wrap):
    count = lax.axis_size(axis)
    pairs = [(i, (i + step) % count) for i in range(count)]
    if not wrap:
        pairs = [(i, i + step) for i in range(count) if 0 <= i + step < count]
    return lax.ppermute(value, axis, pairs)


def per_device(
    tokens, placement, patch_mask, targets, in_weight, mask_token, conv_weight, head_weight
):
    time_tiles = lax.axis_size(TM)
    shards = time_tiles * lax.axis_size("freq")
    core = lax.axis_index("freq")
    place = jnp.stack(
        [lax.axis_index(TM), core, jnp.int32(time_tiles), lax.axis_index("tm_0")]
    ).astype(jnp.int32)
    half = patch_mask.shape[1]

    grid_rows, grid_cols = placement[0], placement[1]
    target = grid_rows // ROWS * 2 + grid_cols // half
    same = target[:, None] == target[None, :]
    order = jnp.arange(target.shape[0])
    slot = jnp.sum(same & (order[None, :] < order[:, None]), axis=1)
    where_to = target * 2 + slot
    proj = jnp.dot(tokens, in_weight, preferred_element_type=F32).astype(BF16)
    lane = jnp.arange(128)[None, :]
    notes = jnp.where(
        lane == 0,
        (grid_rows % ROWS)[:, None],
        jnp.where(lane == 1, grid_cols[:, None], jnp.where(lane == 2, 1, 0)),
    ).astype(BF16)
    payload = jnp.concatenate([proj, notes], axis=1)
    index = jnp.arange(shards * SLOTS)
    wanted = index // (2 * SLOTS) * SLOTS + index % SLOTS
    sender = (wanted[:, None] == where_to[None, :]).astype(BF16)
    packed = jnp.dot(sender, payload, preferred_element_type=F32).astype(BF16)
    arrived = lax.all_to_all(
        packed.reshape(shards, SLOTS, -1), TM_FREQ, split_axis=0, concat_axis=0, tiled=True
    ).reshape(shards * SLOTS, -1)

    flags = jnp.broadcast_to((patch_mask == 1)[:, :, None], (*patch_mask.shape, 128))
    aim = jnp.concatenate([targets, flags.astype(BF16)], axis=2)
    other = send(aim, "freq", 1, True)
    aim = jnp.where(
        core == 0, jnp.concatenate([aim, other], axis=1), jnp.concatenate([other, aim], axis=1)
    )
    aim = jnp.concatenate(
        [send(aim[-2:], TM, 1, False), aim, send(aim[:2], TM, -1, False)], axis=0
    ).reshape(-1, PIX + 128)

    own, chosen = call(
        place_kernel,
        "place",
        (shape((CELLS, CHANNELS)), shape((shards * SLOTS, CELLS))),
        [],
        80_000_000,
        arrived,
        aim,
        mask_token[None, :],
        scalars=False,
    )
    above = send(own[-32:], TM, 1, False)
    below = send(own[:32], TM, -1, False)
    weights = [conv_weight[layer : layer + 1] for layer in range(2)]
    columns = [pltpu.VMEM((464, DEPTH), BF16), pltpu.VMEM((464, DEPTH), BF16)]
    active, unit, scale, inner = call(
        first_kernel,
        "first",
        (shape((448, CHANNELS)), shape((416, CHANNELS), F32), shape((416, 128), F32), shape((416, CHANNELS))),
        columns,
        1_500_000_000,
        place,
        above,
        own,
        below,
        weights[0],
    )
    inners = [inner] + [send(inner, "tm_0", step, True) for step in (1, 2, 3)]
    pred, outer, mid, grad = call(
        second_kernel,
        "second",
        (shape((CELLS, PIX)), shape((CELLS, CHANNELS)), shape((CELLS, CHANNELS), F32), shape((416, CHANNELS))),
        columns,
        3_500_000_000,
        place,
        active,
        unit,
        scale,
        weights[1],
        head_weight,
        aim,
    )
    outers = [outer] + [send(outer, "tm_0", step, True) for step in (1, 2, 3)]

    outgoing = call(
        tail_kernel,
        "tail",
        shape((shards * SLOTS, CHANNELS)),
        [],
        1_200_000_000,
        grad,
        mid,
        weights[0],
        chosen,
        scalars=False,
    )
    outgoing = lax.dynamic_index_in_dim(
        outgoing.reshape(shards, 2, 2, CHANNELS), core, axis=1, keepdims=False
    )
    returned = lax.all_to_all(outgoing, TM_FREQ, split_axis=0, concat_axis=0, tiled=True)
    taken = (jnp.arange(shards * 2)[None, :] == where_to[:, None]).astype(BF16)
    grad_proj = jnp.dot(
        taken, returned.reshape(shards * 2, -1), preferred_element_type=F32
    ).astype(BF16)
    token_grad = lax.dot_general(
        grad_proj, in_weight, (((1,), (1,)), ((), ())), preferred_element_type=F32
    )

    terms = call(
        weight_kernel,
        "weight",
        shape((16, 54, CHANNELS)),
        [
            pltpu.VMEM((4, CHANNELS, 416), BF16),
            pltpu.VMEM((12, 416, CHANNELS), F32),
            pltpu.VMEM((DEPTH, CHANNELS), F32),
        ],
        1_500_000_000,
        place,
        *inners,
        *outers,
    )
    terms = lax.all_to_all(terms, ("tm_1", "freq"), split_axis=0, concat_axis=0, tiled=True)
    conv_grad = terms.reshape(-1, 2, 54, CHANNELS).astype(F32).sum(axis=0)
    pred = lax.dynamic_slice_in_dim(pred.reshape(ROWS, COLS, PIX), core * half, half, axis=1)
    return (pred, token_grad, conv_grad)


def solution(mesh):
    split = Mesh(
        mesh.devices.reshape(4, 8, mesh.shape["freq"], mesh.shape["rec"]),
        ("tm_0", "tm_1", "freq", "rec"),
    )
    placed = (
        P(REC_TM_FREQ, None),
        P(None, REC_TM_FREQ),
        P(REC_TM, "freq"),
        P(REC_TM, "freq", None),
        P(),
        P(),
        P(),
        P(),
    )
    return jax.shard_map(
        per_device,
        mesh=split,
        in_specs=placed,
        out_specs=(P(REC_TM, "freq", None), P(REC_TM_FREQ, None), P("rec", TM_FREQ, None)),
        check_vma=False,
    )
```

profile of v0, /device:TPU:1, one launch (start us, length us, event | category | flops | bytes accessed | tf_op | source)
XLA Modules:
  0.0 133.7 jit_solution(10537199150599494495)
XLA Ops:
  0.6 0.0 copy-start
  0.6 0.7 compare_convert_fusion
  1.4 0.1 copy.14
  1.5 0.1 broadcast_in_dim.68
  1.6 1.0 pad_maximum_fusion
  2.6 3.3 %collective-permute-start = (bf16[50,4,384]{2,1,0:T(4,128)(2,1)S(1)}, bf16[50,4,384]{2,1,0:T(4,128)(2,1)S(1)}, u32[]{:S(2)}, u32[]{:S(2)}) collective-permute-start(bf16[50,4,384]{2,1,0:T(4,128)(2,1)S(1)} %pad_maximum_fusion), channel_id=1, source_target_pairs={{0,4},{4,0},{1,5},{5,1},{2,6},{6,2},{3,7},{7,3},{8,12},{12,8},{9,1... | collective-permute-start | bytes 460808 | tf_op jit(solution)/shard_map/ppermute | solution.py:249
  5.9 0.8 fusion.14
  6.7 0.8 slice_bitcast_fusion
  7.5 0.2 convert_reduce_fusion.1
  7.7 1.0 convolution_convert_fusion.1
  8.7 0.1 select_convert_fusion
  8.8 0.3 convolution_convert_fusion
  9.1 0.8 reshape.151
  9.8 9.9 %all-to-all-start = ((bf16[64,4,512]{2,1,0:T(4,128)(2,1)}), bf16[64,4,512]{2,1,0:T(4,128)(2,1)S(1)}, u32[]{:S(2)}, u32[]{:S(2)}) async-start(bf16[64,4,512]{2,1,0:T(4,128)(2,1)} %reshape.151), calls=%async_computation | async-start | bytes 524288 | tf_op jit(solution)/shard_map/all_to_all | solution.py:281
  19.7 0.0 collective-permute-done
  19.7 1.3 maximum_select_fusion
  21.0 3.3 %collective-permute-start.1 = (bf16[2,8,384]{2,1,0:T(8,128)(2,1)S(1)}, bf16[2,8,384]{2,1,0:T(8,128)(2,1)S(1)}, u32[]{:S(2)}, u32[]{:S(2)}) collective-permute-start(bf16[2,8,384]{2,1,0:T(8,128)(2,1)S(1)} %get-tuple-element.35), channel_id=1, source_target_pairs={{0,8},{8,16},{16,24},{24,32},{32,40},{40,48},{48,56},{56,64},{64,7... | collective-permute-start | bytes 36872 | tf_op jit(solution)/shard_map/ppermute | solution.py:249
  24.3 0.0 copy-start.2
  24.3 1.3 collective-permute-start.2
  25.6 5.4 %fusion.17 = (bf16[1,3456,384]{2,1,0:T(8,128)(2,1)}, bf16[1,3456,384]{2,1,0:T(8,128)(2,1)}) fusion(bf16[2,3456,384]{2,1,0:T(8,128)(2,1)} %param.14), kind=kLoop, calls=%fused_computation.56 | loop fusion | bytes 10616832 | tf_op jit(solution)/shard_map/slice | solution.py:308
  31.0 0.6 broadcast_in_dim.69.token
  31.6 0.0 collective-permute-done.1
  31.6 0.0 collective-permute-done.2
  31.6 0.8 maximum_bitcast_fusion.aim
  32.3 0.0 all-to-all-done
  32.3 0.8 reshape.152.arrived
  33.1 2.3 %place.1 = (bf16[400,384]{1,0:T(8,128)(2,1)}, bf16[256,400]{1,0:T(8,128)(2,1)}) custom-call(bf16[256,512]{1,0:T(8,128)(2,1)} %reshape.152.arrived, bf16[432,384]{1,0:T(8,128)(2,1)} %maximum_bitcast_fusion.aim, bf16[1,384]{1,0:T(2,128)(2,1)} %broadcast_in_dim.69.token), custom_call_target="tpu_custom_call" | custom-call | flops 80000000 | bytes 200000 | tf_op jit(solution)/shard_map/place/pallas_call | solution.py:226
  35.4 0.8 fusion.18
  36.2 1.3 collective-permute-start.4
  37.5 4.6 %collective-permute-start.3 = (bf16[32,384]{1,0:T(8,128)(2,1)S(1)}, bf16[32,384]{1,0:T(8,128)(2,1)S(1)}, u32[]{:S(2)}, u32[]{:S(2)}) collective-permute-start(bf16[32,384]{1,0:T(8,128)(2,1)S(1)} %get-tuple-element.34), channel_id=1, source_target_pairs={{0,8},{8,16},{16,24},{24,32},{32,40},{40,48},{48,56},{56,64},{64,7... | collective-permute-start | bytes 73736 | tf_op jit(solution)/shard_map/ppermute | solution.py:249
  42.1 0.7 pad_add_fusion.place_ref
  42.8 0.0 collective-permute-done.4.below
  42.8 0.3 collective-permute-done.3.above
  43.0 0.3 copy-done.10
  43.4 0.3 copy-done.11
  43.7 5.9 %first.1 = (bf16[448,384]{1,0:T(8,128)(2,1)}, f32[416,384]{1,0:T(8,128)}, f32[416,128]{1,0:T(8,128)}, bf16[416,384]{1,0:T(8,128)(2,1)}) custom-call(s32[4]{0:T(128)} %pad_add_fusion.place_ref, bf16[32,384]{1,0:T(8,128)(2,1)} %copy-done.11, bf16[400,384]{1,0:T(8,128)(2,1)} %get-tuple-element.13.own, bf16[32,384]{1,0:T(8,128)(2,1)} %copy-done.10, ...), custom_call_target="tpu_custom_call" | custom-call | flops 1500000000 | bytes 3750000 | tf_op jit(solution)/shard_map/first/pallas_call | solution.py:226
  49.5 9.2 %second.1 = (bf16[400,256]{1,0:T(8,128)(2,1)}, bf16[400,384]{1,0:T(8,128)(2,1)}, f32[400,384]{1,0:T(8,128)}, bf16[416,384]{1,0:T(8,128)(2,1)}) custom-call(s32[4]{0:T(128)} %pad_add_fusion.place_ref, bf16[448,384]{1,0:T(8,128)(2,1)} %get-tuple-element.14.active_ref, f32[416,384]{1,0:T(8,128)} %get-tuple-element.15.unit_ref, ...), custom_call_target="tpu_custom_call" | custom-call | flops 3500000000 | bytes 8750000 | tf_op jit(solution)/shard_map/second/pallas_call | solution.py:226
  58.8 7.9 %collective-permute-start.10 = (bf16[400,384]{1,0:T(8,128)(2,1)}, bf16[400,384]{1,0:T(8,128)(2,1)S(1)}, u32[]{:S(2)}, u32[]{:S(2)}) collective-permute-start(bf16[400,384]{1,0:T(8,128)(2,1)} %get-tuple-element.22.refs_4_), channel_id=1, source_target_pairs={{0,192},{64,0},{128,64},{192,128},{1,193},{65,1},{129,65},{193,129... | collective-permute-start | bytes 921608 | tf_op jit(solution)/shard_map/ppermute | solution.py:249
  66.7 0.2 collective-permute-start.7
  66.9 0.0 collective-permute-start.6
  66.9 1.3 collective-permute-start.5
  68.2 3.6 %collective-permute-start.9 = (bf16[400,384]{1,0:T(8,128)(2,1)}, bf16[400,384]{1,0:T(8,128)(2,1)S(1)}, u32[]{:S(2)}, u32[]{:S(2)}) collective-permute-start(bf16[400,384]{1,0:T(8,128)(2,1)} %get-tuple-element.22.refs_4_), channel_id=1, source_target_pairs={{0,128},{64,192},{128,0},{192,64},{1,129},{65,193},{129,1},{193,65... | collective-permute-start | bytes 921608 | tf_op jit(solution)/shard_map/ppermute | solution.py:249
  71.7 0.0 collective-permute-done.10.refs_7_
  71.7 0.0 collective-permute-start.8
  71.7 4.9 %tail.1 = bf16[256,384]{1,0:T(8,128)(2,1)} custom-call(bf16[416,384]{1,0:T(8,128)(2,1)} %get-tuple-element.18.grad_ref, f32[400,384]{1,0:T(8,128)} %get-tuple-element.19.mid_ref, bf16[1,3456,384]{2,1,0:T(8,128)(2,1)} %get-tuple-element.32.weight, bf16[256,400]{1,0:T(8,128)(2,1)} %get-tuple-element.20.chosen), custom_call_target="tpu_custom_call" | custom-call | flops 1200000000 | bytes 3000000 | tf_op jit(solution)/shard_map/tail/pallas_call | solution.py:226
  76.6 1.0 reshape.155
  77.6 0.7 dynamic-slice_bitcast_fusion
  78.3 14.6 %all-to-all-start.1 = ((bf16[64,2,384]{2,1,0:T(2,128)(2,1)}), bf16[64,2,384]{2,1,0:T(2,128)(2,1)S(1)}, u32[]{:S(2)}, u32[]{:S(2)}) async-start(bf16[64,2,384]{2,1,0:T(2,128)(2,1)} %dynamic-slice_bitcast_fusion), calls=%async_computation.1 | async-start | bytes 196608 | tf_op jit(solution)/shard_map/all_to_all | solution.py:354
  92.9 0.0 collective-permute-done.9.refs_6_
  93.0 4.7 %collective-permute-done.8.refs_5_ = bf16[400,384]{1,0:T(8,128)(2,1)S(1)} collective-permute-done((bf16[400,384]{1,0:T(8,128)(2,1)}, bf16[400,384]{1,0:T(8,128)(2,1)S(1)}, u32[]{:S(2)}, u32[]{:S(2)}) %collective-permute-start.8) | collective-permute-done | bytes 307232 | tf_op jit(solution)/shard_map/ppermute | solution.py:249
  97.6 0.0 collective-permute-done.7.refs_3_
  97.6 0.0 collective-permute-done.6.refs_2_
  97.7 0.7 copy-done.9
  98.4 0.1 copy-done.4
  98.5 0.1 copy-done.5
  98.6 0.7 copy-done.6
  99.3 7.5 %weight.1 = bf16[16,54,384]{2,1,0:T(8,128)(2,1)} custom-call(s32[4]{0:T(128)} %pad_add_fusion.place_ref, bf16[416,384]{1,0:T(8,128)(2,1)} %get-tuple-element.21.refs_0_, bf16[416,384]{1,0:T(8,128)(2,1)} %copy-done.6, bf16[416,384]{1,0:T(8,128)(2,1)} %copy-done.5, bf16[416,384]{1,0:T(8,128)(2,1)} %copy-done.4, bf16[400,384]{1,0:T(8,128)(2,1)} %get-tuple-element.22.refs_4_, ...), custom_call_target="tpu_custom_call" | custom-call | flops 1500000000 | bytes 3750000 | tf_op jit(solution)/shard_map/weight/pallas_call | solution.py:226
  106.8 0.0 all-to-all-done.1
  106.8 5.4 %all-to-all-start.2 = ((bf16[16,54,384]{2,1,0:T(8,128)(2,1)}), bf16[16,54,384]{2,1,0:T(8,128)(2,1)S(1)}, u32[]{:S(2)}, u32[]{:S(2)}) async-start(bf16[16,54,384]{2,1,0:T(8,128)(2,1)} %weight.1), calls=%async_computation.2 | async-start | bytes 1376256 | tf_op jit(solution)/shard_map/all_to_all | solution.py:377
  112.2 0.7 constant_dynamic-slice_fusion
  113.0 1.1 fusion
  114.1 18.8 %all-to-all-done.2 = bf16[16,54,384]{2,1,0:T(8,128)(2,1)S(1)} async-done(((bf16[16,54,384]{2,1,0:T(8,128)(2,1)}), bf16[16,54,384]{2,1,0:T(8,128)(2,1)S(1)}, u32[]{:S(2)}, u32[]{:S(2)}) %all-to-all-start.2) | async-done | bytes 663584 | tf_op jit(solution)/shard_map/all_to_all | solution.py:377
  132.8 0.1 convert_reduce_fusion
  132.9 0.8 copy.15
  (24 shorter events, 0.1 us)
Async XLA Ops:
  0.6 7.0 %copy-start = (bf16[768,384]{1,0:T(8,128)(2,1)S(1)}, bf16[768,384]{1,0:T(8,128)(2,1)}, u32[]{:S(2)}) copy-start(bf16[768,384]{1,0:T(8,128)(2,1)} %param.12) | copy-start | bytes 1769476
  2.6 17.1 %collective-permute-start = (bf16[50,4,384]{2,1,0:T(4,128)(2,1)S(1)}, bf16[50,4,384]{2,1,0:T(4,128)(2,1)S(1)}, u32[]{:S(2)}, u32[]{:S(2)}) collective-permute-start(bf16[50,4,384]{2,1,0:T(4,128)(2,1)S(1)} %pad_maximum_fusion), channel_id=1, source_target_pairs={{0,4},{4,0},{1,5},{5,1},{2,6},{6,2},{3,7},{7,3},{8,12},{12,8},{9,1... | collective-permute-start | bytes 460808 | tf_op jit(solution)/shard_map/ppermute | solution.py:249
  9.8 22.5 %all-to-all-start = ((bf16[64,4,512]{2,1,0:T(4,128)(2,1)}), bf16[64,4,512]{2,1,0:T(4,128)(2,1)S(1)}, u32[]{:S(2)}, u32[]{:S(2)}) async-start(bf16[64,4,512]{2,1,0:T(4,128)(2,1)} %reshape.151), calls=%async_computation | async-start | bytes 524288 | tf_op jit(solution)/shard_map/all_to_all | solution.py:281
  21.0 10.5 %collective-permute-start.1 = (bf16[2,8,384]{2,1,0:T(8,128)(2,1)S(1)}, bf16[2,8,384]{2,1,0:T(8,128)(2,1)S(1)}, u32[]{:S(2)}, u32[]{:S(2)}) collective-permute-start(bf16[2,8,384]{2,1,0:T(8,128)(2,1)S(1)} %get-tuple-element.35), channel_id=1, source_target_pairs={{0,8},{8,16},{16,24},{24,32},{32,40},{40,48},{48,56},{56,64},{64,7... | collective-permute-start | bytes 36872 | tf_op jit(solution)/shard_map/ppermute | solution.py:249
  24.3 6.7 %copy-start.2 = (bf16[384]{0:T(512)(128)(2,1)S(1)}, bf16[384]{0:T(512)(128)(2,1)}, u32[]{:S(2)}) copy-start(bf16[384]{0:T(512)(128)(2,1)} %param.13) | copy-start | bytes 2308
  24.3 7.3 %collective-permute-start.2 = (bf16[2,8,384]{2,1,0:T(8,128)(2,1)S(1)}, bf16[2,8,384]{2,1,0:T(8,128)(2,1)S(1)}, u32[]{:S(2)}, u32[]{:S(2)}) collective-permute-start(bf16[2,8,384]{2,1,0:T(8,128)(2,1)S(1)} %get-tuple-element.36), channel_id=1, source_target_pairs={{8,0},{16,8},{24,16},{32,24},{40,32},{48,40},{56,48},{64,56},{72,6... | collective-permute-start | bytes 36872 | tf_op jit(solution)/shard_map/ppermute | solution.py:249
  36.2 6.6 %collective-permute-start.4 = (bf16[32,384]{1,0:T(8,128)(2,1)S(1)}, bf16[32,384]{1,0:T(8,128)(2,1)S(1)}, u32[]{:S(2)}, u32[]{:S(2)}) collective-permute-start(bf16[32,384]{1,0:T(8,128)(2,1)S(1)} %get-tuple-element.33), channel_id=1, source_target_pairs={{8,0},{16,8},{24,16},{32,24},{40,32},{48,40},{56,48},{64,56},{72,6... | collective-permute-start | bytes 73736 | tf_op jit(solution)/shard_map/ppermute | solution.py:249
  37.5 5.6 %collective-permute-start.3 = (bf16[32,384]{1,0:T(8,128)(2,1)S(1)}, bf16[32,384]{1,0:T(8,128)(2,1)S(1)}, u32[]{:S(2)}, u32[]{:S(2)}) collective-permute-start(bf16[32,384]{1,0:T(8,128)(2,1)S(1)} %get-tuple-element.34), channel_id=1, source_target_pairs={{0,8},{8,16},{16,24},{24,32},{32,40},{40,48},{48,56},{56,64},{64,7... | collective-permute-start | bytes 73736 | tf_op jit(solution)/shard_map/ppermute | solution.py:249
  42.8 0.6 copy-start.10
  43.0 0.6 copy-start.11
  49.5 17.2 %copy-start.3 = (bf16[416,384]{1,0:T(8,128)(2,1)S(1)}, bf16[416,384]{1,0:T(8,128)(2,1)}, u32[]{:S(2)}) copy-start(bf16[416,384]{1,0:T(8,128)(2,1)} %get-tuple-element.21.refs_0_) | copy-start | bytes 958468
  58.8 13.0 %collective-permute-start.10 = (bf16[400,384]{1,0:T(8,128)(2,1)}, bf16[400,384]{1,0:T(8,128)(2,1)S(1)}, u32[]{:S(2)}, u32[]{:S(2)}) collective-permute-start(bf16[400,384]{1,0:T(8,128)(2,1)} %get-tuple-element.22.refs_4_), channel_id=1, source_target_pairs={{0,192},{64,0},{128,64},{192,128},{1,193},{65,1},{129,65},{193,129... | collective-permute-start | bytes 921608 | tf_op jit(solution)/shard_map/ppermute | solution.py:249
  66.7 30.9 %collective-permute-start.7 = (bf16[416,384]{1,0:T(8,128)(2,1)S(1)}, bf16[416,384]{1,0:T(8,128)(2,1)S(1)}, u32[]{:S(2)}, u32[]{:S(2)}) collective-permute-start(bf16[416,384]{1,0:T(8,128)(2,1)S(1)} %copy-done.3), channel_id=1, source_target_pairs={{0,192},{64,0},{128,64},{192,128},{1,193},{65,1},{129,65},{193,129... | collective-permute-start | bytes 958472 | tf_op jit(solution)/shard_map/ppermute | solution.py:249
  66.9 30.8 %collective-permute-start.6 = (bf16[416,384]{1,0:T(8,128)(2,1)S(1)}, bf16[416,384]{1,0:T(8,128)(2,1)S(1)}, u32[]{:S(2)}, u32[]{:S(2)}) collective-permute-start(bf16[416,384]{1,0:T(8,128)(2,1)S(1)} %copy-done.3), channel_id=1, source_target_pairs={{0,128},{64,192},{128,0},{192,64},{1,129},{65,193},{129,1},{193,65... | collective-permute-start | bytes 958472 | tf_op jit(solution)/shard_map/ppermute | solution.py:249
  66.9 30.8 %collective-permute-start.5 = (bf16[416,384]{1,0:T(8,128)(2,1)S(1)}, bf16[416,384]{1,0:T(8,128)(2,1)S(1)}, u32[]{:S(2)}, u32[]{:S(2)}) collective-permute-start(bf16[416,384]{1,0:T(8,128)(2,1)S(1)} %copy-done.3), channel_id=1, source_target_pairs={{0,64},{64,128},{128,192},{192,0},{1,65},{65,129},{129,193},{193,1... | collective-permute-start | bytes 958472 | tf_op jit(solution)/shard_map/ppermute | solution.py:249
  68.2 24.8 %collective-permute-start.9 = (bf16[400,384]{1,0:T(8,128)(2,1)}, bf16[400,384]{1,0:T(8,128)(2,1)S(1)}, u32[]{:S(2)}, u32[]{:S(2)}) collective-permute-start(bf16[400,384]{1,0:T(8,128)(2,1)} %get-tuple-element.22.refs_4_), channel_id=1, source_target_pairs={{0,128},{64,192},{128,0},{192,64},{1,129},{65,193},{129,1},{193,65... | collective-permute-start | bytes 921608 | tf_op jit(solution)/shard_map/ppermute | solution.py:249
  71.7 25.9 %copy-start.7 = (bf16[400,384]{1,0:T(8,128)(2,1)}, bf16[400,384]{1,0:T(8,128)(2,1)S(1)}, u32[]{:S(2)}) copy-start(bf16[400,384]{1,0:T(8,128)(2,1)S(1)} %collective-permute-done.10.refs_7_) | copy-start | bytes 921604
  71.7 25.9 %collective-permute-start.8 = (bf16[400,384]{1,0:T(8,128)(2,1)}, bf16[400,384]{1,0:T(8,128)(2,1)S(1)}, u32[]{:S(2)}, u32[]{:S(2)}) collective-permute-start(bf16[400,384]{1,0:T(8,128)(2,1)} %get-tuple-element.22.refs_4_), channel_id=1, source_target_pairs={{0,64},{64,128},{128,192},{192,0},{1,65},{65,129},{129,193},{193,1... | collective-permute-start | bytes 921608 | tf_op jit(solution)/shard_map/ppermute | solution.py:249
  78.3 28.5 %all-to-all-start.1 = ((bf16[64,2,384]{2,1,0:T(2,128)(2,1)}), bf16[64,2,384]{2,1,0:T(2,128)(2,1)S(1)}, u32[]{:S(2)}, u32[]{:S(2)}) async-start(bf16[64,2,384]{2,1,0:T(2,128)(2,1)} %dynamic-slice_bitcast_fusion), calls=%async_computation.1 | async-start | bytes 196608 | tf_op jit(solution)/shard_map/all_to_all | solution.py:354
  92.9 19.3 %copy-start.1 = (bf16[400,256]{1,0:T(8,128)(2,1)S(1)}, bf16[400,256]{1,0:T(8,128)(2,1)}, u32[]{:S(2)}) copy-start(bf16[400,256]{1,0:T(8,128)(2,1)} %get-tuple-element.17) | copy-start | bytes 614404
  92.9 4.7 %copy-start.8 = (bf16[400,384]{1,0:T(8,128)(2,1)}, bf16[400,384]{1,0:T(8,128)(2,1)S(1)}, u32[]{:S(2)}) copy-start(bf16[400,384]{1,0:T(8,128)(2,1)S(1)} %collective-permute-done.9.refs_6_) | copy-start | bytes 921604
  97.6 0.8 copy-start.9
  97.6 0.9 copy-start.4
  97.6 0.9 copy-start.5
  98.6 0.7 copy-start.6
  106.8 26.0 %all-to-all-start.2 = ((bf16[16,54,384]{2,1,0:T(8,128)(2,1)}), bf16[16,54,384]{2,1,0:T(8,128)(2,1)S(1)}, u32[]{:S(2)}, u32[]{:S(2)}) async-start(bf16[16,54,384]{2,1,0:T(8,128)(2,1)} %weight.1), calls=%async_computation.2 | async-start | bytes 1376256 | tf_op jit(solution)/shard_map/all_to_all | solution.py:377
where the time goes:
time: 134 us
  starting transfers between devices  56.6 us (42%)
  Pallas kernels  29.8 us (22%)
  waiting for transfers between devices  23.7 us (18%)
  local copies, waits for them, and re-layouts  14 us (10%)
  other arithmetic  6.33 us (5%)
  matrix products  2.43 us (2%)
    pallas_call x5, Pallas kernels, call(): pl.pallas_call(kernel, out_shape=shapes, in_specs=specs or in_specs, out_...  29.8 us
    ppermute x11, starting transfers between devices, send(): return lax.ppermute(value, axis, pairs)  26.7 us
    all_to_all x1, waiting for transfers between devices, per_device(): lax.all_to_all(terms, ('tm_1', 'freq'), split_axis=0, concat_axis=0, tile...  18.8 us
    all_to_all x1, starting transfers between devices, per_device(): lax.all_to_all(outgoing, TM_FREQ, split_axis=0, concat_axis=0, tiled=True)  14.6 us
    all_to_all x1, starting transfers between devices, per_device(): lax.all_to_all(packed.reshape(shards, SLOTS, -1), TM_FREQ, split_axis=0,...  9.89 us
    slice x1, local copies, waits for them, and re-layouts, per_device(): weights = [conv_weight[layer:layer + 1] for layer in range(2)]  5.38 us
    all_to_all x1, starting transfers between devices, per_device(): lax.all_to_all(terms, ('tm_1', 'freq'), split_axis=0, concat_axis=0, tile...  5.36 us
    ppermute x11, waiting for transfers between devices, send(): return lax.ppermute(value, axis, pairs)  4.96 us
  transfers between devices with their start and end apart: 14, of which 3 were waited for; matrix products, arithmetic and copies ran while one was open for 12% of the time, Pallas kernels for 9%

commit v1 on v0

v1 whole, which is shorter than its diff:
```python
import jax
import jax.numpy as jnp
from jax import lax
from jax.experimental import pallas as pl
from jax.experimental.pallas import tpu as pltpu
from jax.sharding import Mesh
from jax.sharding import PartitionSpec as P


TM = ("tm_0", "tm_1")
TM_FREQ = ("tm_0", "tm_1", "freq")
REC_TM_FREQ = ("rec", "tm_0", "tm_1", "freq")
REC_TM = ("rec", "tm_0", "tm_1")

F32 = jnp.float32
BF16 = jnp.bfloat16
ROWS = 50
COLS = 8
CELLS = ROWS * COLS
CHANNELS = 384
DEPTH = 3 * CHANNELS
PIX = 256
ERF_SCALE = 0.7071067811865476
PDF_SCALE = 0.3989422804014327
ERF_TOP = (
    0.00022905065861350646,
    0.0034082910107109506,
    0.050955695062380861,
    0.18520832239976145,
    1.128379143519084,
)
ERF_BOTTOM = (
    -1.1791602954361697e-7,
    0.000023547966471313185,
    0.0010179625278914885,
    0.014070470171167667,
    0.11098505178285362,
    0.49746925110067538,
    1.0,
)


def horner(value, factors):
    total = jnp.full_like(value, factors[0])
    for factor in factors[1:]:
        total = total * value + factor
    return total


def erf(value):
    bounded = jnp.clip(value, -3.7439211627767994, 3.7439211627767994)
    square = bounded * bounded
    return bounded * horner(square, ERF_TOP) / horner(square, ERF_BOTTOM)


def half_erf(unit):
    return 0.5 * (1.0 + erf(unit * ERF_SCALE))


def column_shifted(value):
    cells, channels = value.shape
    grid = value.reshape(cells // 8, 8, channels)
    column = lax.broadcasted_iota(jnp.int32, grid.shape, 1)
    lower = jnp.where(column == 0, 0.0, pltpu.roll(grid, 1, axis=1))
    upper = jnp.where(column == 7, 0.0, pltpu.roll(grid, 7, axis=1))
    return lower.reshape(value.shape), value, upper.reshape(value.shape)


def store_columns(value, even, odd):
    cells, channels = value.shape
    for part, shifted in enumerate(column_shifted(value)):
        lanes = slice(part * channels, (part + 1) * channels)
        even[0:cells, lanes] = shifted.astype(BF16)
        odd[0 : cells - 8, lanes] = shifted[8:].astype(BF16)


def conv_taps(even, odd, weight, cells):
    summed = jnp.dot(even[0:cells], weight[0, 0:DEPTH], preferred_element_type=F32)
    summed += jnp.dot(odd[0:cells], weight[0, DEPTH : 2 * DEPTH], preferred_element_type=F32)
    summed += jnp.dot(
        even[16 : 16 + cells], weight[0, 2 * DEPTH : 3 * DEPTH], preferred_element_type=F32
    )
    return summed


def conv_back(grad, weight, cells):
    summed = None
    for row_off in range(3):
        term = lax.dot_general(
            grad,
            weight[0, row_off * DEPTH : (row_off + 1) * DEPTH],
            (((1,), (1,)), ((), ())),
            preferred_element_type=F32,
        )
        term = term[8 * (2 - row_off) : 8 * (2 - row_off) + cells]
        summed = term if summed is None else summed + term
    grid = (cells // 8, 8, CHANNELS)
    column = lax.broadcasted_iota(jnp.int32, grid, 1)
    first = summed[:, 0:CHANNELS].reshape(grid)
    last = summed[:, 2 * CHANNELS :].reshape(grid)
    total = jnp.where(column == 7, 0.0, pltpu.roll(first, 7, axis=1))
    total += jnp.where(column == 0, 0.0, pltpu.roll(last, 1, axis=1))
    return summed[:, CHANNELS : 2 * CHANNELS] + total.reshape(cells, CHANNELS)


def normed(conv_out):
    center = conv_out - jnp.mean(conv_out, axis=-1, keepdims=True)
    scale = lax.rsqrt(jnp.mean(center * center, axis=-1, keepdims=True) + 1e-05)
    return center * scale, scale


def pull_back(unit, scale, gradient):
    slope = half_erf(unit) + unit * (PDF_SCALE * jnp.exp(-0.5 * unit * unit))
    grad = gradient * slope
    mean = jnp.mean(grad, axis=-1, keepdims=True)
    along = jnp.mean(grad * unit, axis=-1, keepdims=True)
    return scale * (grad - mean - unit * along)


def rows_valid(cells, before):
    row = lax.shift_right_logical(lax.broadcasted_iota(jnp.int32, (cells, 1), 0), 3)
    row = row + lax.axis_index(TM) * ROWS - before
    return (row >= 0) & (row < lax.axis_size(TM) * ROWS)


def pack_kernel(tokens, placement, in_weight, packed, where_out):
    count = tokens.shape[0]
    rows = placement[0:1, :].astype(F32)
    cols = placement[1:2, :].astype(F32)
    tile_row = jnp.floor((rows + 0.5) * (1.0 / ROWS))
    tile = tile_row * 2.0 + jnp.where(cols >= 4.0, 1.0, 0.0)
    down = lax.broadcasted_iota(jnp.int32, (count, count), 0)
    across = lax.broadcasted_iota(jnp.int32, (count, count), 1)

    def column(value):
        return jnp.sum(jnp.where(down == across, value, 0.0), axis=1, keepdims=True)

    earlier = jnp.where((column(tile) == tile) & (down < across), 1.0, 0.0)
    where_to = tile * 2.0 + jnp.sum(earlier, axis=0, keepdims=True)
    where_out[...] = jnp.broadcast_to(column(where_to), where_out.shape)
    index = lax.broadcasted_iota(jnp.int32, (packed.shape[0], 1), 0)
    wanted = lax.shift_right_logical(index, 4) * 4 + (index & 3)
    match = jnp.where(wanted.astype(F32) == where_to, 1.0, 0.0).astype(BF16)
    proj = jnp.dot(tokens[...], in_weight[...], preferred_element_type=F32).astype(BF16)
    lane = lax.broadcasted_iota(jnp.int32, (count, 128), 1)
    notes = jnp.where(lane == 1, column(cols), jnp.where(lane == 2, 1.0, 0.0))
    notes = jnp.where(lane == 0, column(rows - tile_row * ROWS), notes).astype(BF16)
    low = jnp.dot(match, proj[:, 0:256], preferred_element_type=F32)
    rest = jnp.concatenate([proj[:, 256:384], notes], axis=1)
    high = jnp.dot(match, rest, preferred_element_type=F32)
    packed[...] = jnp.where((index & 4) == 0, low, high).astype(BF16)


def place_kernel(arrived, own_aim, other_aim, token, x_out, aim_out, down_out, up_out, chosen_out):
    core = lax.axis_index("freq")
    slots = arrived.shape[0]
    notes = arrived[:, 128:256].astype(F32).reshape(slots // 8, 8, 128)
    within = lax.broadcasted_iota(jnp.int32, notes.shape, 1)
    notes = jnp.where(within >= 4, notes, pltpu.roll(notes, 4, axis=1)).reshape(slots, 128)
    cell = jnp.where(notes[:, 2:3] == 1.0, notes[:, 0:1] * 8.0 + notes[:, 1:2], -1.0)
    lane = lax.broadcasted_iota(jnp.int32, (slots, CELLS), 1)
    index = lax.broadcasted_iota(jnp.int32, (slots, CELLS), 0)
    hit = lane == cell.astype(jnp.int32)

    def pick(flag):
        return lax.dot_general(
            jnp.where(hit & flag, 1.0, 0.0).astype(BF16),
            arrived[...],
            (((0,), (0,)), ((), ())),
            preferred_element_type=F32,
        )

    placed = jnp.concatenate([pick((index & 4) == 0), pick((index & 4) == 4)[:, 0:128]], axis=1)
    number = lax.broadcasted_iota(jnp.int32, (CELLS, 1), 0)
    far = (lax.shift_right_logical(number, 2) & 1) != core
    source = lax.shift_right_logical(number, 3) * 4 + (number & 3) + jnp.where(far, CELLS // 2, 0)
    order = lax.broadcasted_iota(jnp.int32, (CELLS, CELLS), 1) == source
    aim = jnp.dot(
        jnp.where(order, 1.0, 0.0).astype(BF16),
        jnp.concatenate([own_aim[...].astype(F32), other_aim[...].astype(F32)], axis=0).astype(BF16),
        preferred_element_type=F32,
    )
    x = jnp.where(aim[:, PIX : PIX + 1] == 1.0, token[...].astype(F32), placed)
    x_out[...] = x.astype(BF16)
    aim_out[...] = aim.astype(BF16)
    down_out[...] = jnp.concatenate([x[CELLS - 32 :], aim[CELLS - 16 :]], axis=0).astype(BF16)
    up_out[...] = jnp.concatenate([x[0:32], aim[0:16]], axis=0).astype(BF16)
    spread = jnp.broadcast_to(cell, (slots, 128)).reshape(slots // 8, 8, 128)
    first = jnp.sum(jnp.where(within == 4 + 2 * core, spread, 0.0), axis=1, keepdims=True)
    second = jnp.sum(jnp.where(within == 5 + 2 * core, spread, 0.0), axis=1, keepdims=True)
    spread = jnp.where((within & 1) == 0, first, second)
    spread = jnp.where(within < 6, spread, -1.0).reshape(slots, 128)
    chosen_out[...] = jnp.where(lane == spread[:, 0:1].astype(jnp.int32), 1.0, 0.0).astype(BF16)


def first_kernel(
    above, own, below, weight, active_out, unit_out, scale_out, share_out, even, odd
):
    source = jnp.concatenate(
        [above[0:32].astype(F32), own[...].astype(F32), below[0:32].astype(F32)], axis=0
    )
    store_columns(source, even, odd)
    unit, scale = normed(conv_taps(even, odd, weight, 448))
    unit_out[...] = unit[16:432]
    scale_out[...] = jnp.broadcast_to(scale[16:432], (416, 128))
    active = source[8:456] + unit * half_erf(unit)
    active = jnp.where(rows_valid(448, 3), active, 0.0)
    active_out[...] = active.astype(BF16)
    share_out[...] = jnp.where(lax.axis_index("freq") == 1, active[16:432], source[24:440]).astype(BF16)


def second_kernel(
    active_ref, unit_ref, scale_ref, weight, head, above, aim_ref, below,
    pred, share_out, mid_out, grad_out, even, odd,
):
    active = active_ref[...].astype(F32)
    store_columns(active, even, odd)
    unit, scale = normed(conv_taps(even, odd, weight, 432))
    top = (active[8:440] + unit * half_erf(unit)).astype(BF16)
    guess = jnp.dot(top, head[...], preferred_element_type=F32)
    pred[...] = guess[16:416].astype(BF16)
    aim = jnp.concatenate([above[32:48], aim_ref[...], below[32:48]], axis=0)
    misfit = jnp.where(
        aim[:, PIX : PIX + 1] == 1.0, (guess - aim[:, 0:PIX].astype(F32)) * 0.0625, 0.0
    ).astype(BF16)
    grad_top = lax.dot_general(
        misfit, head[...], (((1,), (1,)), ((), ())), preferred_element_type=F32
    )
    grad_two = pull_back(unit, scale, grad_top).astype(BF16)
    grad_mid = grad_top[8:424] + conv_back(grad_two, weight, 416)
    grad_one = pull_back(unit_ref[...], scale_ref[:, 0:1], grad_mid)
    grad_one = jnp.where(rows_valid(416, 1), grad_one, 0.0)
    grad_out[...] = grad_one.astype(BF16)
    mid_out[...] = grad_mid[8:408]
    share_out[...] = jnp.where(
        lax.axis_index("freq") == 1, grad_two.astype(F32)[16:416], grad_one[8:408]
    ).astype(BF16)


def tail_kernel(grad_ref, mid_ref, weight, chosen, out):
    grad_cells = mid_ref[...] + conv_back(grad_ref[...], weight, CELLS)
    picked = jnp.dot(chosen[...], grad_cells.astype(BF16), preferred_element_type=F32)
    part = lax.broadcasted_iota(jnp.int32, out.shape, 0) & 6
    picked = jnp.where(
        part == 0, picked[:, 0:128], jnp.where(part == 2, picked[:, 128:256], picked[:, 256:384])
    )
    out[...] = picked.astype(BF16)


def finish_kernel(returned, where_ref, in_weight, out):
    count = where_ref.shape[0]
    slots = returned.shape[0]
    index = lax.broadcasted_iota(jnp.int32, (count, slots), 1)
    slot = lax.shift_right_logical(index, 3) * 2 + (index & 1)
    hit = where_ref[:, 0:1].astype(jnp.int32) == slot
    parts = []
    for part in range(3):
        taken = jnp.where(hit & ((index & 6) == 2 * part), 1.0, 0.0).astype(BF16)
        parts.append(jnp.dot(taken, returned[...], preferred_element_type=F32))
    grad_proj = jnp.concatenate(parts, axis=1).astype(BF16)
    out[...] = lax.dot_general(
        grad_proj, in_weight[...], (((1,), (1,)), ((), ())), preferred_element_type=F32
    )


def weight_kernel(*refs):
    inner, outer = refs[0:4], refs[4:8]
    out, turned, moved, total = refs[8:]
    first_tap = lax.axis_index("tm_0") * 2
    for part in range(4):
        turned[part] = inner[part][...].astype(F32).T.astype(BF16)
    moved[...] = jnp.zeros_like(moved)
    for step in range(3):
        tap = first_tap + step
        row_off = jnp.where(tap >= 6, 2, jnp.where(tap >= 3, 1, 0))
        col_off = tap - 3 * row_off
        start = pl.multiple_of(row_off * 8, 8)
        summed = None
        for part in range(4):
            low, middle, high = column_shifted(outer[part][...].astype(F32))
            piece = jnp.where(col_off == 0, high, jnp.where(col_off == 1, middle, low))
            slot = 4 * step + part
            moved[slot, pl.ds(start, CELLS), :] = piece
            term = jnp.dot(
                turned[part], moved[slot].astype(BF16), preferred_element_type=F32
            )
            summed = term if summed is None else summed + term
        total[step * CHANNELS : (step + 1) * CHANNELS] = summed
    base = pl.multiple_of(lax.axis_index("tm_0") * 96, 8)
    kept = total[pl.ds(base, 864), :]
    for block in range(16):
        out[block] = kept[54 * block : 54 * (block + 1)].astype(BF16)


VMEM = pl.BlockSpec(memory_space=pltpu.VMEM)


def call(kernel, shapes, scratch, cost, limit, *operands):
    return pl.pallas_call(
        kernel,
        out_shape=shapes,
        in_specs=[VMEM] * len(operands),
        out_specs=jax.tree.map(lambda _: VMEM, shapes),
        scratch_shapes=scratch,
        compiler_params=pltpu.CompilerParams(vmem_limit_bytes=limit << 20),
        cost_estimate=pl.CostEstimate(
            flops=cost, bytes_accessed=cost // 400, transcendentals=0
        ),
    )(*operands)


def shape(dims, dtype=BF16):
    return jax.ShapeDtypeStruct(dims, dtype)


def send(value, axis, step, wrap):
    count = lax.axis_size(axis)
    pairs = [(i, (i + step) % count) for i in range(count)]
    if not wrap:
        pairs = [(i, i + step) for i in range(count) if 0 <= i + step < count]
    return lax.ppermute(value, axis, pairs)


def per_device(
    tokens, placement, patch_mask, targets, in_weight, mask_token, conv_weight, head_weight
):
    shards = lax.axis_size(TM_FREQ)
    core = lax.axis_index("freq")
    visible = tokens.shape[0]
    half = patch_mask.shape[1]

    packed, where_to = call(
        pack_kernel,
        (shape((shards * 8, 256)), shape((visible, 128), F32)),
        [],
        80_000_000,
        4,
        tokens,
        placement,
        in_weight,
    )
    arrived = lax.all_to_all(packed, TM_FREQ, split_axis=0, concat_axis=0, tiled=True)

    flags = jnp.broadcast_to((patch_mask == 1)[:, :, None], (*patch_mask.shape, 128))
    aim = jnp.concatenate([targets, flags.astype(BF16)], axis=2).reshape(-1, PIX + 128)
    other = send(aim, "freq", 1, True)

    own, aim, down, up, chosen = call(
        place_kernel,
        (
            shape((CELLS, CHANNELS)),
            shape((CELLS, PIX + 128)),
            shape((48, CHANNELS)),
            shape((48, CHANNELS)),
            shape((shards * 8, CELLS)),
        ),
        [],
        300_000_000,
        8,
        arrived,
        aim,
        other,
        mask_token[None, :],
    )
    above = send(down, TM, 1, False)
    below = send(up, TM, -1, False)
    weights = [conv_weight[layer : layer + 1] for layer in range(2)]
    columns = [pltpu.VMEM((464, DEPTH), BF16), pltpu.VMEM((464, DEPTH), BF16)]
    active, unit, scale, inner = call(
        first_kernel,
        (
            shape((448, CHANNELS)),
            shape((416, CHANNELS), F32),
            shape((416, 128), F32),
            shape((416, CHANNELS)),
        ),
        columns,
        1_500_000_000,
        16,
        above,
        own,
        below,
        weights[0],
    )
    inners = [inner] + [send(inner, "tm_0", step, True) for step in (1, 2, 3)]
    pred, outer, mid, grad = call(
        second_kernel,
        (
            shape((CELLS, PIX)),
            shape((CELLS, CHANNELS)),
            shape((CELLS, CHANNELS), F32),
            shape((416, CHANNELS)),
        ),
        columns,
        3_500_000_000,
24,
        active,
        unit,
        scale,
        weights[1],
        head_weight,
        above,
        aim,
        below,
    )
    outers = [outer] + [send(outer, "tm_0", step, True) for step in (1, 2, 3)]

    outgoing = call(
        tail_kernel, shape((shards * 8, 128)), [], 1_200_000_000, 16, grad, mid, weights[0], chosen
    )
    returned = lax.all_to_all(
        outgoing, TM_FREQ, split_axis=0, concat_axis=0, tiled=True
    )
    terms = call(
        weight_kernel,
        shape((16, 54, CHANNELS)),
        [
            pltpu.VMEM((4, CHANNELS, 416), BF16),
            pltpu.VMEM((12, 416, CHANNELS), F32),
            pltpu.VMEM((DEPTH, CHANNELS), F32),
        ],
        1_500_000_000,
        24,
        *inners,
        *outers,
    )
    terms = lax.all_to_all(terms, ("tm_1", "freq"), split_axis=0, concat_axis=0, tiled=True)
    token_grad = call(
        finish_kernel,
        shape((visible, in_weight.shape[0]), F32),
        [],
        80_000_000,
        4,
        returned,
        where_to,
        in_weight,
    )
    conv_grad = terms.reshape(-1, 2, 54, CHANNELS).astype(F32).sum(axis=0)
    pred = lax.dynamic_slice_in_dim(pred.reshape(ROWS, COLS, PIX), core * half, half, axis=1)
    return (pred, token_grad, conv_grad)


def solution(mesh):
    split = Mesh(
        mesh.devices.reshape(4, 8, mesh.shape["freq"], mesh.shape["rec"]),
        ("tm_0", "tm_1", "freq", "rec"),
    )
    placed = (
        P(REC_TM_FREQ, None),
        P(None, REC_TM_FREQ),
        P(REC_TM, "freq"),
        P(REC_TM, "freq", None),
        P(),
        P(),
        P(),
        P(),
    )
    return jax.shard_map(
        per_device,
        mesh=split,
        in_specs=placed,
        out_specs=(P(REC_TM, "freq", None), P(REC_TM_FREQ, None), P("rec", TM_FREQ, None)),
        check_vma=False,
    )
```

time: 134 us -> 117 us (0.87)
  waiting for transfers between devices: 23.7 us -> 41.9 us
  starting transfers between devices: 56.6 us -> 41.5 us
  Pallas kernels: 29.8 us -> 22.1 us
  local copies, waits for them, and re-layouts: 14 us -> 8.08 us
  other arithmetic: 6.33 us -> 1.75 us
  matrix products: 2.43 us -> 0 us
    ppermute x11 -> x9, starting transfers between devices: 26.7 us -> 15.1 us  [send(): return lax.ppermute(value, axis, pairs)]
    ppermute x11 -> x9, waiting for transfers between devices: 4.96 us -> 14.6 us  [send(): return lax.ppermute(value, axis, pairs)]
    all_to_all x1, waiting for transfers between devices: 0.01 us -> 8.46 us  [per_device(): lax.all_to_all(packed, TM_FREQ, split_axis=0, concat_axis=0, tiled=True)]
    pallas_call x5 -> x7, Pallas kernels: 29.8 us -> 22.1 us  [call(): pl.pallas_call(kernel, out_shape=shapes, in_specs=[VMEM] * len(operands),...]
    all_to_all x1, starting transfers between devices: 14.6 us -> 8.42 us  [per_device(): lax.all_to_all(outgoing, TM_FREQ, split_axis=0, concat_axis=0, tiled=True)]
    all_to_all x1, starting transfers between devices: 9.89 us -> 13 us  [per_device(): lax.all_to_all(packed, TM_FREQ, split_axis=0, concat_axis=0, tiled=True)]
    reshape x4 -> x1, local copies, waits for them, and re-layouts: 2.58 us -> 0.04 us  [per_device(): jnp.concatenate([targets, flags.astype(BF16)], axis=2)]
    dot_general x3 -> x0, matrix products: 2.43 us -> none  [the longest x1 1.12 us: per_device(): lax.dot_general(grad_proj, in_weight, (((1,), (1,)), ((), ())), preferred...]
  transfers between devices with their start and end apart: 14 -> 12, of which waited for: 3 -> 7; matrix products, arithmetic and copies ran while one was open for 12% -> 6% of each run, Pallas kernels for 9% -> 9%
where the time goes in v1:
time: 117 us; the launch traced here: 116 us
  waiting for transfers between devices  41.9 us (36%)
  starting transfers between devices  41.5 us (35%)
  Pallas kernels  22.1 us (19%)
  local copies, waits for them, and re-layouts  8.08 us (7%)
  other arithmetic  1.75 us (1%)
    pallas_call x7, Pallas kernels, call(): pl.pallas_call(kernel, out_shape=shapes, in_specs=[VMEM] * len(operands),...  22.1 us
    all_to_all x1, waiting for transfers between devices, per_device(): lax.all_to_all(terms, ('tm_1', 'freq'), split_axis=0, concat_axis=0, tile...  18.9 us
    ppermute x9, starting transfers between devices, send(): return lax.ppermute(value, axis, pairs)  15.1 us
    ppermute x9, waiting for transfers between devices, send(): return lax.ppermute(value, axis, pairs)  14.6 us
    all_to_all x1, starting transfers between devices, per_device(): lax.all_to_all(packed, TM_FREQ, split_axis=0, concat_axis=0, tiled=True)  13 us
    all_to_all x1, waiting for transfers between devices, per_device(): lax.all_to_all(packed, TM_FREQ, split_axis=0, concat_axis=0, tiled=True)  8.46 us
    all_to_all x1, starting transfers between devices, per_device(): lax.all_to_all(outgoing, TM_FREQ, split_axis=0, concat_axis=0, tiled=True)  8.42 us
    all_to_all x1, starting transfers between devices, per_device(): lax.all_to_all(terms, ('tm_1', 'freq'), split_axis=0, concat_axis=0, tile...  5.06 us
  transfers between devices with their start and end apart: 12, of which 7 were waited for; matrix products, arithmetic and copies ran while one was open for 6% of the time, Pallas kernels for 9%

profile of v1, /device:TPU:1, one launch (start us, length us, event | category | flops | bytes accessed | tf_op | source)
XLA Modules:
  0.0 116.1 jit_solution(5561358956245218491)
XLA Ops:
  0.6 0.0 copy-start
  0.6 1.1 copy-done
  1.7 0.0 copy-start.2
  1.7 0.8 copy-done.2
  2.5 0.0 copy-start.3
  2.5 0.7 copy-done.3
  3.2 1.2 %shard_map.103 = (bf16[512,256]{1,0:T(8,128)(2,1)}, f32[40,128]{1,0:T(8,128)S(1)}) custom-call(bf16[40,768]{1,0:T(8,128)(2,1)S(1)} %copy-done.2, s32[2,40]{1,0:T(2,128)S(1)} %copy-done.3, bf16[768,384]{1,0:T(8,128)(2,1)S(1)} %copy-done), custom_call_target="tpu_custom_call" | custom-call | flops 80000000 | bytes 200000 | tf_op jit(solution)/shard_map/pallas_call | solution.py:299
  4.4 13.0 %all-to-all-start = ((bf16[64,8,256]{2,1,0:T(8,128)(2,1)}), bf16[64,8,256]{2,1,0:T(8,128)(2,1)S(1)}, u32[]{:S(2)}, u32[]{:S(2)}) async-start(bf16[64,8,256]{2,1,0:T(8,128)(2,1)} %bitcast), calls=%async_computation | async-start | bytes 524288 | tf_op jit(solution)/shard_map/all_to_all | solution.py:342
  17.4 0.7 compare_convert_fusion
  18.1 0.1 copy.12
  18.2 0.1 broadcast_in_dim.4
  18.3 1.0 pad_maximum_fusion
  19.3 0.5 collective-permute-start
  19.9 0.7 broadcast_in_dim.10.token
  20.6 0.3 collective-permute-done.other_aim
  20.9 8.5 %all-to-all-done = bf16[64,8,256]{2,1,0:T(8,128)(2,1)S(1)} async-done(((bf16[64,8,256]{2,1,0:T(8,128)(2,1)}), bf16[64,8,256]{2,1,0:T(8,128)(2,1)S(1)}, u32[]{:S(2)}, u32[]{:S(2)}) %all-to-all-start) | async-done | bytes 262176 | tf_op jit(solution)/shard_map/all_to_all | solution.py:342
  29.4 1.3 %shard_map.104 = (bf16[400,384]{1,0:T(8,128)(2,1)S(1)}, bf16[400,384]{1,0:T(8,128)(2,1)S(1)}, bf16[48,384]{1,0:T(8,128)(2,1)S(1)}, bf16[48,384]{1,0:T(8,128)(2,1)S(1)}, bf16[512,400]{1,0:T(8,128)(2,1)S(1)}) custom-call(bf16[512,256]{1,0:T(8,128)(2,1)S(1)} %bitcast.8, bf16[200,384]{1,0:T(8,128)(2,1)S(1)} %reshape.20.own_aim, ...), custom_call_target="tpu_custom_call" | custom-call | flops 300000000 | bytes 750000 | tf_op jit(solution)/shard_map/pallas_call | solution.py:299
  30.7 3.1 %collective-permute-start.1 = (bf16[48,384]{1,0:T(8,128)(2,1)S(1)}, bf16[48,384]{1,0:T(8,128)(2,1)S(1)}, u32[]{:S(2)}, u32[]{:S(2)}) collective-permute-start(bf16[48,384]{1,0:T(8,128)(2,1)S(1)} %get-tuple-element.19), channel_id=1, source_target_pairs={{0,8},{8,16},{16,24},{24,32},{32,40},{40,48},{48,56},{56,64},{64,7... | collective-permute-start | bytes 110600 | tf_op jit(solution)/shard_map/ppermute | solution.py:321
  33.7 1.3 %collective-permute-start.2 = (bf16[48,384]{1,0:T(8,128)(2,1)S(1)}, bf16[48,384]{1,0:T(8,128)(2,1)S(1)}, u32[]{:S(2)}, u32[]{:S(2)}) collective-permute-start(bf16[48,384]{1,0:T(8,128)(2,1)S(1)} %get-tuple-element.21), channel_id=1, source_target_pairs={{8,0},{16,8},{24,16},{32,24},{40,32},{48,40},{56,48},{64,56},{72,6... | collective-permute-start | bytes 110600 | tf_op jit(solution)/shard_map/ppermute | solution.py:321
  35.0 3.1 %fusion = (bf16[1,3456,384]{2,1,0:T(8,128)(2,1)S(1)}, bf16[1,3456,384]{2,1,0:T(8,128)(2,1)S(1)}) fusion(bf16[2,3456,384]{2,1,0:T(8,128)(2,1)} %param.14), kind=kLoop, calls=%fused_computation.4 | loop fusion | bytes 10616832 | tf_op jit(solution)/shard_map/slice | solution.py:367
  38.1 0.0 collective-permute-done.1.above
  38.1 0.3 collective-permute-done.2.below
  38.5 0.0 copy-start.4
  38.5 2.9 %shard_map.105 = (bf16[448,384]{1,0:T(8,128)(2,1)S(1)}, f32[416,384]{1,0:T(8,128)S(1)}, f32[416,128]{1,0:T(8,128)S(1)}, bf16[416,384]{1,0:T(8,128)(2,1)S(1)}) custom-call(bf16[48,384]{1,0:T(8,128)(2,1)S(1)} %collective-permute-done.1.above, bf16[400,384]{1,0:T(8,128)(2,1)S(1)} %get-tuple-element.20.own, bf16[48,384]{1,0:T(8,128)(2,1)S(1)} %collective-permute-done.2.below, ...), custom_call_target="tpu_custom_call" | custom-call | flops 1500000000 | bytes 3750000 | tf_op jit(solution)/shard_map/pallas_call | solution.py:299
  41.4 0.0 copy-done.4
  41.4 6.0 %shard_map.106 = (bf16[400,256]{1,0:T(8,128)(2,1)S(1)}, bf16[400,384]{1,0:T(8,128)(2,1)S(1)}, f32[400,384]{1,0:T(8,128)S(1)}, bf16[416,384]{1,0:T(8,128)(2,1)S(1)}) custom-call(bf16[448,384]{1,0:T(8,128)(2,1)S(1)} %get-tuple-element.22.active_ref, f32[416,384]{1,0:T(8,128)S(1)} %get-tuple-element.23.unit_ref, f32[416,128]{1,0:T(8,128)S(1)} %get-tuple-element.24.scale_ref, ...), custom_call_target="tpu_custom_call" | custom-call | flops 3500000000 | bytes 8750000 | tf_op jit(solution)/shard_map/pallas_call | solution.py:299
  47.4 4.0 %collective-permute-start.6 = (bf16[400,384]{1,0:T(8,128)(2,1)S(1)}, bf16[400,384]{1,0:T(8,128)(2,1)S(1)}, u32[]{:S(2)}, u32[]{:S(2)}) collective-permute-start(bf16[400,384]{1,0:T(8,128)(2,1)S(1)} %get-tuple-element.32.refs_4_), channel_id=1, source_target_pairs={{0,64},{64,128},{128,192},{192,0},{1,65},{65,129},{129,193},{193,1... | collective-permute-start | bytes 921608 | tf_op jit(solution)/shard_map/ppermute | solution.py:321
  51.4 1.3 %collective-permute-start.3 = (bf16[416,384]{1,0:T(8,128)(2,1)S(1)}, bf16[416,384]{1,0:T(8,128)(2,1)S(1)}, u32[]{:S(2)}, u32[]{:S(2)}) collective-permute-start(bf16[416,384]{1,0:T(8,128)(2,1)S(1)} %get-tuple-element.31.refs_0_), channel_id=1, source_target_pairs={{0,64},{64,128},{128,192},{192,0},{1,65},{65,129},{129,193},{193,1... | collective-permute-start | bytes 958472 | tf_op jit(solution)/shard_map/ppermute | solution.py:321
  52.6 1.4 %collective-permute-start.4 = (bf16[416,384]{1,0:T(8,128)(2,1)S(1)}, bf16[416,384]{1,0:T(8,128)(2,1)S(1)}, u32[]{:S(2)}, u32[]{:S(2)}) collective-permute-start(bf16[416,384]{1,0:T(8,128)(2,1)S(1)} %get-tuple-element.31.refs_0_), channel_id=1, source_target_pairs={{0,128},{64,192},{128,0},{192,64},{1,129},{65,193},{129,1},{193,65... | collective-permute-start | bytes 958472 | tf_op jit(solution)/shard_map/ppermute | solution.py:321
  54.0 2.0 %collective-permute-start.5 = (bf16[416,384]{1,0:T(8,128)(2,1)S(1)}, bf16[416,384]{1,0:T(8,128)(2,1)S(1)}, u32[]{:S(2)}, u32[]{:S(2)}) collective-permute-start(bf16[416,384]{1,0:T(8,128)(2,1)S(1)} %get-tuple-element.31.refs_0_), channel_id=1, source_target_pairs={{0,192},{64,0},{128,64},{192,128},{1,193},{65,1},{129,65},{193,129... | collective-permute-start | bytes 958472 | tf_op jit(solution)/shard_map/ppermute | solution.py:321
  56.0 0.4 collective-permute-start.7
  56.4 3.1 %collective-permute-done.6.refs_5_ = bf16[400,384]{1,0:T(8,128)(2,1)S(1)} collective-permute-done((bf16[400,384]{1,0:T(8,128)(2,1)S(1)}, bf16[400,384]{1,0:T(8,128)(2,1)S(1)}, u32[]{:S(2)}, u32[]{:S(2)}) %collective-permute-start.6) | collective-permute-done | bytes 307232 | tf_op jit(solution)/shard_map/ppermute | solution.py:321
  59.5 1.2 %collective-permute-start.8 = (bf16[400,384]{1,0:T(8,128)(2,1)S(1)}, bf16[400,384]{1,0:T(8,128)(2,1)S(1)}, u32[]{:S(2)}, u32[]{:S(2)}) collective-permute-start(bf16[400,384]{1,0:T(8,128)(2,1)S(1)} %get-tuple-element.32.refs_4_), channel_id=1, source_target_pairs={{0,192},{64,0},{128,64},{192,128},{1,193},{65,1},{129,65},{193,129... | collective-permute-start | bytes 921608 | tf_op jit(solution)/shard_map/ppermute | solution.py:321
  60.7 2.9 %shard_map.107 = bf16[512,128]{1,0:T(8,128)(2,1)} custom-call(bf16[416,384]{1,0:T(8,128)(2,1)S(1)} %get-tuple-element.27.grad_ref, f32[400,384]{1,0:T(8,128)S(1)} %get-tuple-element.28.mid_ref, bf16[1,3456,384]{2,1,0:T(8,128)(2,1)S(1)} %get-tuple-element.37.weight, bf16[512,400]{1,0:T(8,128)(2,1)S(1)} %get-tuple-element.29.chosen), custom_call_target="tpu_custom_call" | custom-call | flops 1200000000 | bytes 3000000 | tf_op jit(solution)/shard_map/pallas_call | solution.py:299
  63.6 8.4 %all-to-all-start.1 = ((bf16[64,8,128]{2,1,0:T(8,128)(2,1)}), bf16[64,8,128]{2,1,0:T(8,128)(2,1)S(1)}, u32[]{:S(2)}, u32[]{:S(2)}) async-start(bf16[64,8,128]{2,1,0:T(8,128)(2,1)} %bitcast.3), calls=%async_computation.1 | async-start | bytes 262144 | tf_op jit(solution)/shard_map/all_to_all | solution.py:411
  72.0 0.0 copy-start.1
  72.0 9.8 %collective-permute-done.7.refs_6_ = bf16[400,384]{1,0:T(8,128)(2,1)S(1)} collective-permute-done((bf16[400,384]{1,0:T(8,128)(2,1)S(1)}, bf16[400,384]{1,0:T(8,128)(2,1)S(1)}, u32[]{:S(2)}, u32[]{:S(2)}) %collective-permute-start.7) | collective-permute-done | bytes 307232 | tf_op jit(solution)/shard_map/ppermute | solution.py:321
  81.8 1.1 collective-permute-done.8.refs_7_
  82.9 0.0 collective-permute-done.3.refs_1_
  82.9 0.0 collective-permute-done.4.refs_2_
  82.9 0.0 collective-permute-done.5.refs_3_
  82.9 6.6 %shard_map.109 = bf16[16,54,384]{2,1,0:T(8,128)(2,1)} custom-call(bf16[416,384]{1,0:T(8,128)(2,1)S(1)} %get-tuple-element.31.refs_0_, bf16[416,384]{1,0:T(8,128)(2,1)S(1)} %collective-permute-done.3.refs_1_, bf16[416,384]{1,0:T(8,128)(2,1)S(1)} %collective-permute-done.4.refs_2_, bf16[416,384]{1,0:T(8,128)(2,1)S(1)} %collective-permute-done.5.refs_3_, ...), custom_call_target="tpu_custom_call" | custom-call | flops 1500000000 | bytes 3750000 | tf_op jit(solution)/shard_map/pallas_call | solution.py:299
  89.5 0.0 all-to-all-done.1
  89.5 5.1 %all-to-all-start.2 = ((bf16[16,54,384]{2,1,0:T(8,128)(2,1)}), bf16[16,54,384]{2,1,0:T(8,128)(2,1)S(1)}, u32[]{:S(2)}, u32[]{:S(2)}) async-start(bf16[16,54,384]{2,1,0:T(8,128)(2,1)} %shard_map.109), calls=%async_computation.2 | async-start | bytes 1376256 | tf_op jit(solution)/shard_map/all_to_all | solution.py:427
  94.6 0.7 constant_dynamic-slice_fusion
  95.3 0.0 copy-done.1
  95.3 1.1 shard_map.108
  96.4 18.9 %all-to-all-done.2 = bf16[16,54,384]{2,1,0:T(8,128)(2,1)S(1)} async-done(((bf16[16,54,384]{2,1,0:T(8,128)(2,1)}), bf16[16,54,384]{2,1,0:T(8,128)(2,1)S(1)}, u32[]{:S(2)}, u32[]{:S(2)}) %all-to-all-start.2) | async-done | bytes 663584 | tf_op jit(solution)/shard_map/all_to_all | solution.py:427
  115.3 0.1 convert_reduce_fusion
  115.4 0.8 copy.13
  (1 shorter events, 0.0 us)
Async XLA Ops:
  0.6 1.1 copy-start
  1.7 0.8 copy-start.2
  2.5 0.7 copy-start.3
  4.4 24.9 %all-to-all-start = ((bf16[64,8,256]{2,1,0:T(8,128)(2,1)}), bf16[64,8,256]{2,1,0:T(8,128)(2,1)S(1)}, u32[]{:S(2)}, u32[]{:S(2)}) async-start(bf16[64,8,256]{2,1,0:T(8,128)(2,1)} %bitcast), calls=%async_computation | async-start | bytes 524288 | tf_op jit(solution)/shard_map/all_to_all | solution.py:342
  19.3 1.6 %collective-permute-start = (bf16[200,384]{1,0:T(8,128)(2,1)S(1)}, bf16[200,384]{1,0:T(8,128)(2,1)S(1)}, u32[]{:S(2)}, u32[]{:S(2)}) collective-permute-start(bf16[200,384]{1,0:T(8,128)(2,1)S(1)} %reshape.20.own_aim), channel_id=1, source_target_pairs={{0,4},{4,0},{1,5},{5,1},{2,6},{6,2},{3,7},{7,3},{8,12},{12,8},{9,1... | collective-permute-start | bytes 460808 | tf_op jit(solution)/shard_map/ppermute | solution.py:321
  30.7 7.5 %collective-permute-start.1 = (bf16[48,384]{1,0:T(8,128)(2,1)S(1)}, bf16[48,384]{1,0:T(8,128)(2,1)S(1)}, u32[]{:S(2)}, u32[]{:S(2)}) collective-permute-start(bf16[48,384]{1,0:T(8,128)(2,1)S(1)} %get-tuple-element.19), channel_id=1, source_target_pairs={{0,8},{8,16},{16,24},{24,32},{32,40},{40,48},{48,56},{56,64},{64,7... | collective-permute-start | bytes 110600 | tf_op jit(solution)/shard_map/ppermute | solution.py:321
  33.7 4.7 %collective-permute-start.2 = (bf16[48,384]{1,0:T(8,128)(2,1)S(1)}, bf16[48,384]{1,0:T(8,128)(2,1)S(1)}, u32[]{:S(2)}, u32[]{:S(2)}) collective-permute-start(bf16[48,384]{1,0:T(8,128)(2,1)S(1)} %get-tuple-element.21), channel_id=1, source_target_pairs={{8,0},{16,8},{24,16},{32,24},{40,32},{48,40},{56,48},{64,56},{72,6... | collective-permute-start | bytes 110600 | tf_op jit(solution)/shard_map/ppermute | solution.py:321
  38.5 2.9 %copy-start.4 = (bf16[384,256]{1,0:T(8,128)(2,1)S(1)}, bf16[384,256]{1,0:T(8,128)(2,1)}, u32[]{:S(2)}) copy-start(bf16[384,256]{1,0:T(8,128)(2,1)} %head.1) | copy-start | bytes 589828
  47.4 12.1 %collective-permute-start.6 = (bf16[400,384]{1,0:T(8,128)(2,1)S(1)}, bf16[400,384]{1,0:T(8,128)(2,1)S(1)}, u32[]{:S(2)}, u32[]{:S(2)}) collective-permute-start(bf16[400,384]{1,0:T(8,128)(2,1)S(1)} %get-tuple-element.32.refs_4_), channel_id=1, source_target_pairs={{0,64},{64,128},{128,192},{192,0},{1,65},{65,129},{129,193},{193,1... | collective-permute-start | bytes 921608 | tf_op jit(solution)/shard_map/ppermute | solution.py:321
  51.4 31.5 %collective-permute-start.3 = (bf16[416,384]{1,0:T(8,128)(2,1)S(1)}, bf16[416,384]{1,0:T(8,128)(2,1)S(1)}, u32[]{:S(2)}, u32[]{:S(2)}) collective-permute-start(bf16[416,384]{1,0:T(8,128)(2,1)S(1)} %get-tuple-element.31.refs_0_), channel_id=1, source_target_pairs={{0,64},{64,128},{128,192},{192,0},{1,65},{65,129},{129,193},{193,1... | collective-permute-start | bytes 958472 | tf_op jit(solution)/shard_map/ppermute | solution.py:321
  52.6 30.2 %collective-permute-start.4 = (bf16[416,384]{1,0:T(8,128)(2,1)S(1)}, bf16[416,384]{1,0:T(8,128)(2,1)S(1)}, u32[]{:S(2)}, u32[]{:S(2)}) collective-permute-start(bf16[416,384]{1,0:T(8,128)(2,1)S(1)} %get-tuple-element.31.refs_0_), channel_id=1, source_target_pairs={{0,128},{64,192},{128,0},{192,64},{1,129},{65,193},{129,1},{193,65... | collective-permute-start | bytes 958472 | tf_op jit(solution)/shard_map/ppermute | solution.py:321
  54.0 28.8 %collective-permute-start.5 = (bf16[416,384]{1,0:T(8,128)(2,1)S(1)}, bf16[416,384]{1,0:T(8,128)(2,1)S(1)}, u32[]{:S(2)}, u32[]{:S(2)}) collective-permute-start(bf16[416,384]{1,0:T(8,128)(2,1)S(1)} %get-tuple-element.31.refs_0_), channel_id=1, source_target_pairs={{0,192},{64,0},{128,64},{192,128},{1,193},{65,1},{129,65},{193,129... | collective-permute-start | bytes 958472 | tf_op jit(solution)/shard_map/ppermute | solution.py:321
  56.0 25.8 %collective-permute-start.7 = (bf16[400,384]{1,0:T(8,128)(2,1)S(1)}, bf16[400,384]{1,0:T(8,128)(2,1)S(1)}, u32[]{:S(2)}, u32[]{:S(2)}) collective-permute-start(bf16[400,384]{1,0:T(8,128)(2,1)S(1)} %get-tuple-element.32.refs_4_), channel_id=1, source_target_pairs={{0,128},{64,192},{128,0},{192,64},{1,129},{65,193},{129,1},{193,65... | collective-permute-start | bytes 921608 | tf_op jit(solution)/shard_map/ppermute | solution.py:321
  59.5 23.4 %collective-permute-start.8 = (bf16[400,384]{1,0:T(8,128)(2,1)S(1)}, bf16[400,384]{1,0:T(8,128)(2,1)S(1)}, u32[]{:S(2)}, u32[]{:S(2)}) collective-permute-start(bf16[400,384]{1,0:T(8,128)(2,1)S(1)} %get-tuple-element.32.refs_4_), channel_id=1, source_target_pairs={{0,192},{64,0},{128,64},{192,128},{1,193},{65,1},{129,65},{193,129... | collective-permute-start | bytes 921608 | tf_op jit(solution)/shard_map/ppermute | solution.py:321
  63.6 25.9 %all-to-all-start.1 = ((bf16[64,8,128]{2,1,0:T(8,128)(2,1)}), bf16[64,8,128]{2,1,0:T(8,128)(2,1)S(1)}, u32[]{:S(2)}, u32[]{:S(2)}) async-start(bf16[64,8,128]{2,1,0:T(8,128)(2,1)} %bitcast.3), calls=%async_computation.1 | async-start | bytes 262144 | tf_op jit(solution)/shard_map/all_to_all | solution.py:411
  72.0 23.3 %copy-start.1 = (bf16[768,384]{1,0:T(8,128)(2,1)S(1)}, bf16[768,384]{1,0:T(8,128)(2,1)}, u32[]{:S(2)}) copy-start(bf16[768,384]{1,0:T(8,128)(2,1)} %in_weight.3) | copy-start | bytes 1769476
  89.5 25.8 %all-to-all-start.2 = ((bf16[16,54,384]{2,1,0:T(8,128)(2,1)}), bf16[16,54,384]{2,1,0:T(8,128)(2,1)S(1)}, u32[]{:S(2)}, u32[]{:S(2)}) async-start(bf16[16,54,384]{2,1,0:T(8,128)(2,1)} %shard_map.109), calls=%async_computation.2 | async-start | bytes 1376256 | tf_op jit(solution)/shard_map/all_to_all | solution.py:427

commit v2 on v1

--- a/solution.py
+++ b/solution.py
@@ -74,21 +74,37 @@
         odd[0 : cells - 8, lanes] = shifted[8:].astype(BF16)
 
 
-def conv_taps(even, odd, weight, cells):
-    summed = jnp.dot(even[0:cells], weight[0, 0:DEPTH], preferred_element_type=F32)
-    summed += jnp.dot(odd[0:cells], weight[0, DEPTH : 2 * DEPTH], preferred_element_type=F32)
-    summed += jnp.dot(
-        even[16 : 16 + cells], weight[0, 2 * DEPTH : 3 * DEPTH], preferred_element_type=F32
-    )
+def fetch(weight, layer, taps, arrivals):
+    copies = []
+    for part in range(3):
+        rows = pl.ds(part * DEPTH, DEPTH)
+        copies.append(
+            pltpu.make_async_copy(weight.at[layer, rows], taps.at[rows], arrivals.at[part])
+        )
+    for copy in copies:
+        copy.start()
+    return copies
+
+
+def conv_taps(even, odd, taps, copies, cells):
+    summed = None
+    for part, window in enumerate((even[0:cells], odd[0:cells], even[16 : 16 + cells])):
+        copies[part].wait()
+        term = jnp.dot(
+            window, taps[part * DEPTH : (part + 1) * DEPTH], preferred_element_type=F32
+        )
+        summed = term if summed is None else summed + term
     return summed
 
 
-def conv_back(grad, weight, cells):
+def conv_back(grad, taps, cells, copies=None):
     summed = None
     for row_off in range(3):
+        if copies:
+            copies[row_off].wait()
         term = lax.dot_general(
             grad,
-            weight[0, row_off * DEPTH : (row_off + 1) * DEPTH],
+            taps[row_off * DEPTH : (row_off + 1) * DEPTH],
             (((1,), (1,)), ((), ())),
             preferred_element_type=F32,
         )
@@ -194,28 +210,33 @@
 
 
 def first_kernel(
-    above, own, below, weight, active_out, unit_out, scale_out, share_out, even, odd
+    above, own, below, weight, active_out, unit_out, scale_out, share_out,
+    even, odd, taps, arrivals,
 ):
+    copies = fetch(weight, 0, taps, arrivals)
     source = jnp.concatenate(
         [above[0:32].astype(F32), own[...].astype(F32), below[0:32].astype(F32)], axis=0
     )
     store_columns(source, even, odd)
-    unit, scale = normed(conv_taps(even, odd, weight, 448))
+    unit, scale = normed(conv_taps(even, odd, taps, copies, 448))
     unit_out[...] = unit[16:432]
     scale_out[...] = jnp.broadcast_to(scale[16:432], (416, 128))
     active = source[8:456] + unit * half_erf(unit)
     active = jnp.where(rows_valid(448, 3), active, 0.0)
     active_out[...] = active.astype(BF16)
-    share_out[...] = jnp.where(lax.axis_index("freq") == 1, active[16:432], source[24:440]).astype(BF16)
+    share = jnp.where(lax.axis_index("freq") == 1, active[16:432], source[24:440]).astype(BF16)
+    for peer in range(4):
+        share_out[peer] = share
 
 
 def second_kernel(
     active_ref, unit_ref, scale_ref, weight, head, above, aim_ref, below,
-    pred, share_out, mid_out, grad_out, even, odd,
+    pred, share_out, mid_out, grad_out, even, odd, taps, arrivals,
 ):
+    copies = fetch(weight, 1, taps, arrivals)
     active = active_ref[...].astype(F32)
     store_columns(active, even, odd)
-    unit, scale = normed(conv_taps(even, odd, weight, 432))
+    unit, scale = normed(conv_taps(even, odd, taps, copies, 432))
     top = (active[8:440] + unit * half_erf(unit)).astype(BF16)
     guess = jnp.dot(top, head[...], preferred_element_type=F32)
     pred[...] = guess[16:416].astype(BF16)
@@ -227,7 +248,7 @@
         misfit, head[...], (((1,), (1,)), ((), ())), preferred_element_type=F32
     )
     grad_two = pull_back(unit, scale, grad_top).astype(BF16)
-    grad_mid = grad_top[8:424] + conv_back(grad_two, weight, 416)
+    grad_mid = grad_top[8:424] + conv_back(grad_two, taps, 416)
     grad_one = pull_back(unit_ref[...], scale_ref[:, 0:1], grad_mid)
     grad_one = jnp.where(rows_valid(416, 1), grad_one, 0.0)
     grad_out[...] = grad_one.astype(BF16)
@@ -237,8 +258,9 @@
     ).astype(BF16)
 
 
-def tail_kernel(grad_ref, mid_ref, weight, chosen, out):
-    grad_cells = mid_ref[...] + conv_back(grad_ref[...], weight, CELLS)
+def tail_kernel(grad_ref, mid_ref, weight, chosen, out, taps, arrivals):
+    copies = fetch(weight, 0, taps, arrivals)
+    grad_cells = mid_ref[...] + conv_back(grad_ref[...], taps, CELLS, copies)
     picked = jnp.dot(chosen[...], grad_cells.astype(BF16), preferred_element_type=F32)
     part = lax.broadcasted_iota(jnp.int32, out.shape, 0) & 6
     picked = jnp.where(
@@ -263,43 +285,49 @@
     )
 
 
-def weight_kernel(*refs):
-    inner, outer = refs[0:4], refs[4:8]
-    out, turned, moved, total = refs[8:]
-    first_tap = lax.axis_index("tm_0") * 2
+def weight_kernel(inner, own, back, early, late, front, out, turned, moved, total):
+    place = lax.axis_index("tm_0")
     for part in range(4):
-        turned[part] = inner[part][...].astype(F32).T.astype(BF16)
-    moved[...] = jnp.zeros_like(moved)
+        turned[part] = inner[(place - part) & 3].astype(F32).T.astype(BF16)
+    moved[:, 0:16] = jnp.zeros((12, 16, CHANNELS), F32)
+    moved[:, CELLS : CELLS + 16] = jnp.zeros((12, 16, CHANNELS), F32)
+    outers = (
+        own[...].astype(F32),
+        back[...].astype(F32),
+        jnp.concatenate([early[...].astype(F32), late[...].astype(F32)], axis=0),
+        front[...].astype(F32),
+    )
+    column = lax.broadcasted_iota(jnp.int32, (ROWS, COLS, CHANNELS), 1)
     for step in range(3):
-        tap = first_tap + step
+        tap = place * 2 + step
         row_off = jnp.where(tap >= 6, 2, jnp.where(tap >= 3, 1, 0))
-        col_off = tap - 3 * row_off
+        shift = tap - 3 * row_off - 1
         start = pl.multiple_of(row_off * 8, 8)
+        inside = (column >= shift) & (column < COLS + shift)
         summed = None
         for part in range(4):
-            low, middle, high = column_shifted(outer[part][...].astype(F32))
-            piece = jnp.where(col_off == 0, high, jnp.where(col_off == 1, middle, low))
+            piece = pltpu.roll(outers[part].reshape(ROWS, COLS, CHANNELS), shift & 7, axis=1)
+            piece = jnp.where(inside, piece, 0.0).reshape(CELLS, CHANNELS)
             slot = 4 * step + part
             moved[slot, pl.ds(start, CELLS), :] = piece
-            term = jnp.dot(
-                turned[part], moved[slot].astype(BF16), preferred_element_type=F32
-            )
+            term = jnp.dot(turned[part], moved[slot].astype(BF16), preferred_element_type=F32)
             summed = term if summed is None else summed + term
         total[step * CHANNELS : (step + 1) * CHANNELS] = summed
-    base = pl.multiple_of(lax.axis_index("tm_0") * 96, 8)
+    base = pl.multiple_of(place * 96, 8)
     kept = total[pl.ds(base, 864), :]
     for block in range(16):
         out[block] = kept[54 * block : 54 * (block + 1)].astype(BF16)
 
 
 VMEM = pl.BlockSpec(memory_space=pltpu.VMEM)
-
-
-def call(kernel, shapes, scratch, cost, limit, *operands):
+HBM = pl.BlockSpec(memory_space=pltpu.HBM)
+
+
+def call(kernel, shapes, scratch, cost, limit, *operands, far=-1):
     return pl.pallas_call(
         kernel,
         out_shape=shapes,
-        in_specs=[VMEM] * len(operands),
+        in_specs=[HBM if i == far else VMEM for i in range(len(operands))],
         out_specs=jax.tree.map(lambda _: VMEM, shapes),
         scratch_shapes=scratch,
         compiler_params=pltpu.CompilerParams(vmem_limit_bytes=limit << 20),
@@ -325,6 +353,7 @@
     tokens, placement, patch_mask, targets, in_weight, mask_token, conv_weight, head_weight
 ):
     shards = lax.axis_size(TM_FREQ)
+    conv_weight = pltpu.with_memory_space_constraint(conv_weight, pltpu.HBM)
     core = lax.axis_index("freq")
     visible = tokens.shape[0]
     half = patch_mask.shape[1]
@@ -334,7 +363,7 @@
         (shape((shards * 8, 256)), shape((visible, 128), F32)),
         [],
         80_000_000,
-        4,
+        62,
         tokens,
         placement,
         in_weight,
@@ -364,15 +393,15 @@
     )
     above = send(down, TM, 1, False)
     below = send(up, TM, -1, False)
-    weights = [conv_weight[layer : layer + 1] for layer in range(2)]
-    columns = [pltpu.VMEM((464, DEPTH), BF16), pltpu.VMEM((464, DEPTH), BF16)]
+    loaded = [pltpu.VMEM((9 * CHANNELS, CHANNELS), BF16), pltpu.SemaphoreType.DMA((3,))]
+    columns = [pltpu.VMEM((464, DEPTH), BF16), pltpu.VMEM((464, DEPTH), BF16), *loaded]
     active, unit, scale, inner = call(
         first_kernel,
         (
             shape((448, CHANNELS)),
             shape((416, CHANNELS), F32),
             shape((416, 128), F32),
-            shape((416, CHANNELS)),
+            shape((4, 416, CHANNELS)),
         ),
         columns,
         1_500_000_000,
@@ -380,9 +409,10 @@
         above,
         own,
         below,
-        weights[0],
-    )
-    inners = [inner] + [send(inner, "tm_0", step, True) for step in (1, 2, 3)]
+        conv_weight,
+        far=3,
+    )
+    inners = lax.all_to_all(inner, "tm_0", split_axis=0, concat_axis=0, tiled=True)
     pred, outer, mid, grad = call(
         second_kernel,
         (
@@ -397,16 +427,28 @@
         active,
         unit,
         scale,
-        weights[1],
+        conv_weight,
         head_weight,
         above,
         aim,
         below,
-    )
-    outers = [outer] + [send(outer, "tm_0", step, True) for step in (1, 2, 3)]
-
+        far=3,
+    )
+    back = send(outer, "tm_0", 1, True)
+    front = send(outer, "tm_0", -1, True)
+    early = send(back[: CELLS // 2], "tm_0", 1, True)
+    late = send(front[CELLS // 2 :], "tm_0", -1, True)
     outgoing = call(
-        tail_kernel, shape((shards * 8, 128)), [], 1_200_000_000, 16, grad, mid, weights[0], chosen
+        tail_kernel,
+        shape((shards * 8, 128)),
+        loaded,
+        1_200_000_000,
+        16,
+        grad,
+        mid,
+        conv_weight,
+        chosen,
+        far=2,
     )
     returned = lax.all_to_all(
         outgoing, TM_FREQ, split_axis=0, concat_axis=0, tiled=True
@@ -421,8 +463,12 @@
         ],
         1_500_000_000,
         24,
-        *inners,
-        *outers,
+        inners,
+        outer,
+        back,
+        early,
+        late,
+        front,
     )
     terms = lax.all_to_all(terms, ("tm_1", "freq"), split_axis=0, concat_axis=0, tiled=True)
     token_grad = call(

time: 117 us -> 122 us (1.043)
  waiting for transfers between devices: 41.9 us -> 49.1 us
  Pallas kernels: 22.1 us -> 27 us
  local copies, waits for them, and re-layouts: 8.08 us -> 3.72 us
  starting transfers between devices: 41.5 us -> 39.1 us
    pallas_call x7, Pallas kernels: 22.1 us -> 27 us  [call(): pl.pallas_call(kernel, out_shape=shapes, in_specs=[HBM if i == far else V...]
    all_to_all x0 -> x1, starting transfers between devices: none -> 4.63 us  [per_device(): lax.all_to_all(inner, 'tm_0', split_axis=0, concat_axis=0, tiled=True)]
    all_to_all x1, waiting for transfers between devices: 0.01 us -> 4.57 us  [per_device(): lax.all_to_all(outgoing, TM_FREQ, split_axis=0, concat_axis=0, tiled=True)]
    ppermute x9 -> x7, starting transfers between devices: 15.1 us -> 10.6 us  [send(): return lax.ppermute(value, axis, pairs)]
    slice x1 -> x2, local copies, waits for them, and re-layouts: 3.09 us -> 0.03 us  [the longest x1 0.02 us: per_device(): late = send(front[CELLS // 2:], 'tm_0', -1, True)]
    ppermute x9 -> x7, waiting for transfers between devices: 14.6 us -> 17.1 us  [send(): return lax.ppermute(value, axis, pairs)]
    all_to_all x1, starting transfers between devices: 5.06 us -> 3.78 us  [per_device(): lax.all_to_all(terms, ('tm_1', 'freq'), split_axis=0, concat_axis=0, tile...]
    all_to_all x1, starting transfers between devices: 8.42 us -> 7.15 us  [per_device(): lax.all_to_all(outgoing, TM_FREQ, split_axis=0, concat_axis=0, tiled=True)]
  transfers between devices with their start and end apart: 12 -> 11, of which waited for: 7 -> 6; matrix products, arithmetic and copies ran while one was open for 6% -> 2% of each run, Pallas kernels for 9% -> 15%
where the time goes in v2:
time: 122 us; the launch traced here: 121 us
  waiting for transfers between devices  49.1 us (40%)
  starting transfers between devices  39.1 us (32%)
  Pallas kernels  27 us (22%)
  local copies, waits for them, and re-layouts  3.72 us (3%)
  other arithmetic  1.75 us (1%)
    pallas_call x7, Pallas kernels, call(): pl.pallas_call(kernel, out_shape=shapes, in_specs=[HBM if i == far else V...  27 us
    all_to_all x1, waiting for transfers between devices, per_device(): lax.all_to_all(terms, ('tm_1', 'freq'), split_axis=0, concat_axis=0, tile...  18.9 us
    ppermute x7, waiting for transfers between devices, send(): return lax.ppermute(value, axis, pairs)  17.1 us
    all_to_all x1, starting transfers between devices, per_device(): lax.all_to_all(packed, TM_FREQ, split_axis=0, concat_axis=0, tiled=True)  13 us
    ppermute x7, starting transfers between devices, send(): return lax.ppermute(value, axis, pairs)  10.6 us
    all_to_all x1, waiting for transfers between devices, per_device(): lax.all_to_all(packed, TM_FREQ, split_axis=0, concat_axis=0, tiled=True)  8.46 us
    all_to_all x1, starting transfers between devices, per_device(): lax.all_to_all(outgoing, TM_FREQ, split_axis=0, concat_axis=0, tiled=True)  7.15 us
    all_to_all x1, starting transfers between devices, per_device(): lax.all_to_all(inner, 'tm_0', split_axis=0, concat_axis=0, tiled=True)  4.63 us
  transfers between devices with their start and end apart: 11, of which 6 were waited for; matrix products, arithmetic and copies ran while one was open for 2% of the time, Pallas kernels for 15%

profile of v2, /device:TPU:1, one launch (start us, length us, event | category | flops | bytes accessed | tf_op | source)
XLA Modules:
  0.0 121.5 jit_solution(12992592799073141623)
XLA Ops:
  0.6 0.0 copy-start.7
  0.6 2.3 %shard_map.103 = (bf16[512,256]{1,0:T(8,128)(2,1)}, f32[40,128]{1,0:T(8,128)}) custom-call(bf16[40,768]{1,0:T(8,128)(2,1)} %tokens.1, s32[2,40]{1,0:T(2,128)} %placement.1, bf16[768,384]{1,0:T(8,128)(2,1)} %in_weight.3), custom_call_target="tpu_custom_call" | custom-call | flops 80000000 | bytes 200000 | tf_op jit(solution)/shard_map/pallas_call | solution.py:327
  3.0 13.0 %all-to-all-start = ((bf16[64,8,256]{2,1,0:T(8,128)(2,1)}), bf16[64,8,256]{2,1,0:T(8,128)(2,1)S(1)}, u32[]{:S(2)}, u32[]{:S(2)}) async-start(bf16[64,8,256]{2,1,0:T(8,128)(2,1)} %bitcast.11), calls=%async_computation | async-start | bytes 524288 | tf_op jit(solution)/shard_map/all_to_all | solution.py:371
  16.0 0.7 compare_convert_fusion
  16.7 0.1 copy.12
  16.8 0.1 broadcast_in_dim.4
  16.9 1.0 pad_maximum_fusion
  17.9 0.5 collective-permute-start
  18.5 0.0 copy-done.7
  18.5 1.0 collective-permute-done.other_aim
  19.5 8.5 %all-to-all-done = bf16[64,8,256]{2,1,0:T(8,128)(2,1)S(1)} async-done(((bf16[64,8,256]{2,1,0:T(8,128)(2,1)}), bf16[64,8,256]{2,1,0:T(8,128)(2,1)S(1)}, u32[]{:S(2)}, u32[]{:S(2)}) %all-to-all-start) | async-done | bytes 262176 | tf_op jit(solution)/shard_map/all_to_all | solution.py:371
  27.9 1.3 %shard_map.104 = (bf16[400,384]{1,0:T(8,128)(2,1)S(1)}, bf16[400,384]{1,0:T(8,128)(2,1)S(1)}, bf16[48,384]{1,0:T(8,128)(2,1)S(1)}, bf16[48,384]{1,0:T(8,128)(2,1)S(1)}, bf16[512,400]{1,0:T(8,128)(2,1)S(1)}) custom-call(bf16[512,256]{1,0:T(8,128)(2,1)S(1)} %bitcast.8, bf16[200,384]{1,0:T(8,128)(2,1)S(1)} %reshape.20.own_aim, ...), custom_call_target="tpu_custom_call" | custom-call | flops 300000000 | bytes 750000 | tf_op jit(solution)/shard_map/pallas_call | solution.py:327
  29.3 0.0 copy-start.5
  29.3 3.1 %collective-permute-start.1 = (bf16[48,384]{1,0:T(8,128)(2,1)S(1)}, bf16[48,384]{1,0:T(8,128)(2,1)S(1)}, u32[]{:S(2)}, u32[]{:S(2)}) collective-permute-start(bf16[48,384]{1,0:T(8,128)(2,1)S(1)} %get-tuple-element.19), channel_id=1, source_target_pairs={{0,8},{8,16},{16,24},{24,32},{32,40},{40,48},{48,56},{56,64},{64,7... | collective-permute-start | bytes 110600 | tf_op jit(solution)/shard_map/ppermute | solution.py:349
  32.3 1.3 %collective-permute-start.2 = (bf16[48,384]{1,0:T(8,128)(2,1)S(1)}, bf16[48,384]{1,0:T(8,128)(2,1)S(1)}, u32[]{:S(2)}, u32[]{:S(2)}) collective-permute-start(bf16[48,384]{1,0:T(8,128)(2,1)S(1)} %get-tuple-element.21), channel_id=1, source_target_pairs={{8,0},{16,8},{24,16},{32,24},{40,32},{48,40},{56,48},{64,56},{72,6... | collective-permute-start | bytes 110600 | tf_op jit(solution)/shard_map/ppermute | solution.py:349
  33.6 0.0 collective-permute-done.1.above
  33.6 3.4 %collective-permute-done.2.below = bf16[48,384]{1,0:T(8,128)(2,1)S(1)} collective-permute-done((bf16[48,384]{1,0:T(8,128)(2,1)S(1)}, bf16[48,384]{1,0:T(8,128)(2,1)S(1)}, u32[]{:S(2)}, u32[]{:S(2)}) %collective-permute-start.2) | collective-permute-done | bytes 36896 | tf_op jit(solution)/shard_map/ppermute | solution.py:349
  37.0 5.6 %shard_map.105 = (bf16[448,384]{1,0:T(8,128)(2,1)S(1)}, f32[416,384]{1,0:T(8,128)S(1)}, f32[416,128]{1,0:T(8,128)S(1)}, bf16[4,416,384]{2,1,0:T(8,128)(2,1)}) custom-call(bf16[48,384]{1,0:T(8,128)(2,1)S(1)} %collective-permute-done.1.above, bf16[400,384]{1,0:T(8,128)(2,1)S(1)} %get-tuple-element.20.own, bf16[48,384]{1,0:T(8,128)(2,1)S(1)} %collective-permute-done.2.below, ...), custom_call_target="tpu_custom_call" | custom-call | flops 1500000000 | bytes 3750000 | tf_op jit(solution)/shard_map/pallas_call | solution.py:327
  42.6 0.0 copy-done.5
  42.6 0.0 copy-start.4
  42.6 4.6 %all-to-all-start.2 = ((bf16[4,416,384]{2,1,0:T(8,128)(2,1)}), bf16[4,416,384]{2,1,0:T(8,128)(2,1)S(1)}, u32[]{:S(2)}, u32[]{:S(2)}) async-start(bf16[4,416,384]{2,1,0:T(8,128)(2,1)} %get-tuple-element.31), calls=%async_computation.2 | async-start | bytes 2555904 | tf_op jit(solution)/shard_map/all_to_all | solution.py:415
  47.2 0.0 copy-done.4
  47.2 0.0 copy-start.6
  47.3 1.0 copy-done.6
  48.2 7.4 %shard_map.106 = (bf16[400,256]{1,0:T(8,128)(2,1)S(1)}, bf16[400,384]{1,0:T(8,128)(2,1)S(1)}, f32[400,384]{1,0:T(8,128)S(1)}, bf16[416,384]{1,0:T(8,128)(2,1)S(1)}) custom-call(bf16[448,384]{1,0:T(8,128)(2,1)S(1)} %get-tuple-element.22.active_ref, f32[416,384]{1,0:T(8,128)S(1)} %get-tuple-element.23.unit_ref, f32[416,128]{1,0:T(8,128)S(1)} %get-tuple-element.24.scale_ref, ...), custom_call_target="tpu_custom_call" | custom-call | flops 3500000000 | bytes 8750000 | tf_op jit(solution)/shard_map/pallas_call | solution.py:327
  55.7 0.0 copy-start.2
  55.7 1.6 %collective-permute-start.3 = (bf16[400,384]{1,0:T(8,128)(2,1)S(1)}, bf16[400,384]{1,0:T(8,128)(2,1)S(1)}, u32[]{:S(2)}, u32[]{:S(2)}) collective-permute-start(bf16[400,384]{1,0:T(8,128)(2,1)S(1)} %get-tuple-element.32.own), channel_id=1, source_target_pairs={{0,64},{64,128},{128,192},{192,0},{1,65},{65,129},{129,193},{193,1... | collective-permute-start | bytes 921608 | tf_op jit(solution)/shard_map/ppermute | solution.py:349
  57.2 1.3 %collective-permute-start.5 = (bf16[400,384]{1,0:T(8,128)(2,1)S(1)}, bf16[400,384]{1,0:T(8,128)(2,1)S(1)}, u32[]{:S(2)}, u32[]{:S(2)}) collective-permute-start(bf16[400,384]{1,0:T(8,128)(2,1)S(1)} %get-tuple-element.32.own), channel_id=1, source_target_pairs={{0,192},{64,0},{128,64},{192,128},{1,193},{65,1},{129,65},{193,129... | collective-permute-start | bytes 921608 | tf_op jit(solution)/shard_map/ppermute | solution.py:349
  58.5 12.7 %collective-permute-done.3.back = bf16[400,384]{1,0:T(8,128)(2,1)S(1)} collective-permute-done((bf16[400,384]{1,0:T(8,128)(2,1)S(1)}, bf16[400,384]{1,0:T(8,128)(2,1)S(1)}, u32[]{:S(2)}, u32[]{:S(2)}) %collective-permute-start.3) | collective-permute-done | bytes 307232 | tf_op jit(solution)/shard_map/ppermute | solution.py:349
  71.3 0.1 collective-permute-start.4
  71.4 0.0 collective-permute-done.5.front
  71.4 2.7 %collective-permute-start.6 = (bf16[200,384]{1,0:T(8,128)(2,1)S(1)}, bf16[200,384]{1,0:T(8,128)(2,1)S(1)}, u32[]{:S(2)}, u32[]{:S(2)}) collective-permute-start(bf16[200,384]{1,0:T(8,128)(2,1)S(1)} %slice.9), channel_id=1, source_target_pairs={{0,192},{64,0},{128,64},{192,128},{1,193},{65,1},{129,65},{193,129... | collective-permute-start | bytes 460808 | tf_op jit(solution)/shard_map/ppermute | solution.py:349
  74.1 0.0 copy-done.2
  74.1 4.4 %shard_map.107 = bf16[512,128]{1,0:T(8,128)(2,1)} custom-call(bf16[416,384]{1,0:T(8,128)(2,1)S(1)} %get-tuple-element.27.grad_ref, f32[400,384]{1,0:T(8,128)S(1)} %get-tuple-element.28.mid_ref, bf16[2,3456,384]{2,1,0:T(8,128)(2,1)} %weight.5, bf16[512,400]{1,0:T(8,128)(2,1)S(1)} %get-tuple-element.29.chosen), custom_call_target="tpu_custom_call" | custom-call | flops 1200000000 | bytes 3000000 | tf_op jit(solution)/shard_map/pallas_call | solution.py:327
  78.6 0.0 all-to-all-done.2.inner
  78.6 7.2 %all-to-all-start.1 = ((bf16[64,8,128]{2,1,0:T(8,128)(2,1)}), bf16[64,8,128]{2,1,0:T(8,128)(2,1)S(1)}, u32[]{:S(2)}, u32[]{:S(2)}) async-start(bf16[64,8,128]{2,1,0:T(8,128)(2,1)} %bitcast.3), calls=%async_computation.1 | async-start | bytes 262144 | tf_op jit(solution)/shard_map/all_to_all | solution.py:453
  85.7 0.0 collective-permute-done.4.early
  85.8 0.0 collective-permute-done.6.late
  85.8 0.0 copy-start.3
  85.8 1.0 copy-done.3
  86.7 4.8 %shard_map.109 = bf16[16,54,384]{2,1,0:T(8,128)(2,1)} custom-call(bf16[4,416,384]{2,1,0:T(8,128)(2,1)S(1)} %all-to-all-done.2.inner, bf16[400,384]{1,0:T(8,128)(2,1)S(1)} %copy-done.3, bf16[400,384]{1,0:T(8,128)(2,1)S(1)} %collective-permute-done.3.back, bf16[200,384]{1,0:T(8,128)(2,1)S(1)} %collective-permute-done.4.early, ...), custom_call_target="tpu_custom_call" | custom-call | flops 1500000000 | bytes 3750000 | tf_op jit(solution)/shard_map/pallas_call | solution.py:327
  91.5 0.0 copy-start
  91.5 0.0 copy-start.1
  91.5 4.6 %all-to-all-done.1 = bf16[64,8,128]{2,1,0:T(8,128)(2,1)S(1)} async-done(((bf16[64,8,128]{2,1,0:T(8,128)(2,1)}), bf16[64,8,128]{2,1,0:T(8,128)(2,1)S(1)}, u32[]{:S(2)}, u32[]{:S(2)}) %all-to-all-start.1) | async-done | bytes 131104 | tf_op jit(solution)/shard_map/all_to_all | solution.py:453
  96.1 3.8 %all-to-all-start.3 = ((bf16[16,54,384]{2,1,0:T(8,128)(2,1)}), bf16[16,54,384]{2,1,0:T(8,128)(2,1)S(1)}, u32[]{:S(2)}, u32[]{:S(2)}) async-start(bf16[16,54,384]{2,1,0:T(8,128)(2,1)} %shard_map.109), calls=%async_computation.3 | async-start | bytes 1376256 | tf_op jit(solution)/shard_map/all_to_all | solution.py:473
  99.9 0.7 constant_dynamic-slice_fusion
  100.5 0.0 copy-done
  100.6 0.0 copy-done.1
  100.6 1.1 shard_map.108
  101.7 18.9 %all-to-all-done.3 = bf16[16,54,384]{2,1,0:T(8,128)(2,1)S(1)} async-done(((bf16[16,54,384]{2,1,0:T(8,128)(2,1)}), bf16[16,54,384]{2,1,0:T(8,128)(2,1)S(1)}, u32[]{:S(2)}, u32[]{:S(2)}) %all-to-all-start.3) | async-done | bytes 663584 | tf_op jit(solution)/shard_map/all_to_all | solution.py:473
  120.6 0.1 convert_reduce_fusion
  120.7 0.8 copy.13
  (4 shorter events, 0.1 us)
Async XLA Ops:
  0.6 17.8 %copy-start.7 = (bf16[384]{0:T(512)(128)(2,1)S(1)}, bf16[384]{0:T(512)(128)(2,1)}, u32[]{:S(2)}) copy-start(bf16[384]{0:T(512)(128)(2,1)} %param.13) | copy-start | bytes 2308
  3.0 24.9 %all-to-all-start = ((bf16[64,8,256]{2,1,0:T(8,128)(2,1)}), bf16[64,8,256]{2,1,0:T(8,128)(2,1)S(1)}, u32[]{:S(2)}, u32[]{:S(2)}) async-start(bf16[64,8,256]{2,1,0:T(8,128)(2,1)} %bitcast.11), calls=%async_computation | async-start | bytes 524288 | tf_op jit(solution)/shard_map/all_to_all | solution.py:371
  17.9 1.6 %collective-permute-start = (bf16[200,384]{1,0:T(8,128)(2,1)S(1)}, bf16[200,384]{1,0:T(8,128)(2,1)S(1)}, u32[]{:S(2)}, u32[]{:S(2)}) collective-permute-start(bf16[200,384]{1,0:T(8,128)(2,1)S(1)} %reshape.20.own_aim), channel_id=1, source_target_pairs={{0,4},{4,0},{1,5},{5,1},{2,6},{6,2},{3,7},{7,3},{8,12},{12,8},{9,1... | collective-permute-start | bytes 460808 | tf_op jit(solution)/shard_map/ppermute | solution.py:349
  29.3 13.3 %copy-start.5 = (bf16[400,384]{1,0:T(8,128)(2,1)}, bf16[400,384]{1,0:T(8,128)(2,1)S(1)}, u32[]{:S(2)}) copy-start(bf16[400,384]{1,0:T(8,128)(2,1)S(1)} %get-tuple-element.25.aim_ref) | copy-start | bytes 921604
  29.3 4.4 %collective-permute-start.1 = (bf16[48,384]{1,0:T(8,128)(2,1)S(1)}, bf16[48,384]{1,0:T(8,128)(2,1)S(1)}, u32[]{:S(2)}, u32[]{:S(2)}) collective-permute-start(bf16[48,384]{1,0:T(8,128)(2,1)S(1)} %get-tuple-element.19), channel_id=1, source_target_pairs={{0,8},{8,16},{16,24},{24,32},{32,40},{40,48},{48,56},{56,64},{64,7... | collective-permute-start | bytes 110600 | tf_op jit(solution)/shard_map/ppermute | solution.py:349
  32.3 4.7 %collective-permute-start.2 = (bf16[48,384]{1,0:T(8,128)(2,1)S(1)}, bf16[48,384]{1,0:T(8,128)(2,1)S(1)}, u32[]{:S(2)}, u32[]{:S(2)}) collective-permute-start(bf16[48,384]{1,0:T(8,128)(2,1)S(1)} %get-tuple-element.21), channel_id=1, source_target_pairs={{8,0},{16,8},{24,16},{32,24},{40,32},{48,40},{56,48},{64,56},{72,6... | collective-permute-start | bytes 110600 | tf_op jit(solution)/shard_map/ppermute | solution.py:349
  42.6 4.6 %copy-start.4 = (bf16[384,256]{1,0:T(8,128)(2,1)S(1)}, bf16[384,256]{1,0:T(8,128)(2,1)}, u32[]{:S(2)}) copy-start(bf16[384,256]{1,0:T(8,128)(2,1)} %head.1) | copy-start | bytes 589828
  42.6 36.0 %all-to-all-start.2 = ((bf16[4,416,384]{2,1,0:T(8,128)(2,1)}), bf16[4,416,384]{2,1,0:T(8,128)(2,1)S(1)}, u32[]{:S(2)}, u32[]{:S(2)}) async-start(bf16[4,416,384]{2,1,0:T(8,128)(2,1)} %get-tuple-element.31), calls=%async_computation.2 | async-start | bytes 2555904 | tf_op jit(solution)/shard_map/all_to_all | solution.py:415
  47.2 1.0 copy-start.6
  55.7 18.5 %copy-start.2 = (bf16[400,384]{1,0:T(8,128)(2,1)}, bf16[400,384]{1,0:T(8,128)(2,1)S(1)}, u32[]{:S(2)}) copy-start(bf16[400,384]{1,0:T(8,128)(2,1)S(1)} %get-tuple-element.32.own) | copy-start | bytes 921604
  55.7 15.6 %collective-permute-start.3 = (bf16[400,384]{1,0:T(8,128)(2,1)S(1)}, bf16[400,384]{1,0:T(8,128)(2,1)S(1)}, u32[]{:S(2)}, u32[]{:S(2)}) collective-permute-start(bf16[400,384]{1,0:T(8,128)(2,1)S(1)} %get-tuple-element.32.own), channel_id=1, source_target_pairs={{0,64},{64,128},{128,192},{192,0},{1,65},{65,129},{129,193},{193,1... | collective-permute-start | bytes 921608 | tf_op jit(solution)/shard_map/ppermute | solution.py:349
  57.2 14.1 %collective-permute-start.5 = (bf16[400,384]{1,0:T(8,128)(2,1)S(1)}, bf16[400,384]{1,0:T(8,128)(2,1)S(1)}, u32[]{:S(2)}, u32[]{:S(2)}) collective-permute-start(bf16[400,384]{1,0:T(8,128)(2,1)S(1)} %get-tuple-element.32.own), channel_id=1, source_target_pairs={{0,192},{64,0},{128,64},{192,128},{1,193},{65,1},{129,65},{193,129... | collective-permute-start | bytes 921608 | tf_op jit(solution)/shard_map/ppermute | solution.py:349
  71.3 14.5 %collective-permute-start.4 = (bf16[200,384]{1,0:T(8,128)(2,1)S(1)}, bf16[200,384]{1,0:T(8,128)(2,1)S(1)}, u32[]{:S(2)}, u32[]{:S(2)}) collective-permute-start(bf16[200,384]{1,0:T(8,128)(2,1)S(1)} %slice.8), channel_id=1, source_target_pairs={{0,64},{64,128},{128,192},{192,0},{1,65},{65,129},{129,193},{193,1... | collective-permute-start | bytes 460808 | tf_op jit(solution)/shard_map/ppermute | solution.py:349
  71.4 14.4 %collective-permute-start.6 = (bf16[200,384]{1,0:T(8,128)(2,1)S(1)}, bf16[200,384]{1,0:T(8,128)(2,1)S(1)}, u32[]{:S(2)}, u32[]{:S(2)}) collective-permute-start(bf16[200,384]{1,0:T(8,128)(2,1)S(1)} %slice.9), channel_id=1, source_target_pairs={{0,192},{64,0},{128,64},{192,128},{1,193},{65,1},{129,65},{193,129... | collective-permute-start | bytes 460808 | tf_op jit(solution)/shard_map/ppermute | solution.py:349
  78.6 17.5 %all-to-all-start.1 = ((bf16[64,8,128]{2,1,0:T(8,128)(2,1)}), bf16[64,8,128]{2,1,0:T(8,128)(2,1)S(1)}, u32[]{:S(2)}, u32[]{:S(2)}) async-start(bf16[64,8,128]{2,1,0:T(8,128)(2,1)} %bitcast.3), calls=%async_computation.1 | async-start | bytes 262144 | tf_op jit(solution)/shard_map/all_to_all | solution.py:453
  85.8 1.0 copy-start.3
  91.5 9.1 %copy-start = (bf16[768,384]{1,0:T(8,128)(2,1)S(1)}, bf16[768,384]{1,0:T(8,128)(2,1)}, u32[]{:S(2)}) copy-start(bf16[768,384]{1,0:T(8,128)(2,1)} %in_weight.3) | copy-start | bytes 1769476
  91.5 9.1 %copy-start.1 = (f32[40,128]{1,0:T(8,128)S(1)}, f32[40,128]{1,0:T(8,128)}, u32[]{:S(2)}) copy-start(f32[40,128]{1,0:T(8,128)} %get-tuple-element.30.where_ref) | copy-start | bytes 61444
  96.1 24.5 %all-to-all-start.3 = ((bf16[16,54,384]{2,1,0:T(8,128)(2,1)}), bf16[16,54,384]{2,1,0:T(8,128)(2,1)S(1)}, u32[]{:S(2)}, u32[]{:S(2)}) async-start(bf16[16,54,384]{2,1,0:T(8,128)(2,1)} %shard_map.109), calls=%async_computation.3 | async-start | bytes 1376256 | tf_op jit(solution)/shard_map/all_to_all | solution.py:473

commit v3 on v1

--- a/solution.py
+++ b/solution.py
@@ -74,21 +74,22 @@
         odd[0 : cells - 8, lanes] = shifted[8:].astype(BF16)
 
 
-def conv_taps(even, odd, weight, cells):
-    summed = jnp.dot(even[0:cells], weight[0, 0:DEPTH], preferred_element_type=F32)
-    summed += jnp.dot(odd[0:cells], weight[0, DEPTH : 2 * DEPTH], preferred_element_type=F32)
-    summed += jnp.dot(
-        even[16 : 16 + cells], weight[0, 2 * DEPTH : 3 * DEPTH], preferred_element_type=F32
-    )
+def conv_taps(even, odd, taps, cells):
+    summed = None
+    for part, window in enumerate((even[0:cells], odd[0:cells], even[16 : 16 + cells])):
+        term = jnp.dot(
+            window, taps[0, part * DEPTH : (part + 1) * DEPTH], preferred_element_type=F32
+        )
+        summed = term if summed is None else summed + term
     return summed
 
 
-def conv_back(grad, weight, cells):
+def conv_back(grad, taps, cells):
     summed = None
     for row_off in range(3):
         term = lax.dot_general(
             grad,
-            weight[0, row_off * DEPTH : (row_off + 1) * DEPTH],
+            taps[0, row_off * DEPTH : (row_off + 1) * DEPTH],
             (((1,), (1,)), ((), ())),
             preferred_element_type=F32,
         )
@@ -206,7 +207,9 @@
     active = source[8:456] + unit * half_erf(unit)
     active = jnp.where(rows_valid(448, 3), active, 0.0)
     active_out[...] = active.astype(BF16)
-    share_out[...] = jnp.where(lax.axis_index("freq") == 1, active[16:432], source[24:440]).astype(BF16)
+    share_out[...] = jnp.where(
+        lax.axis_index("freq") == 1, active[16:432], source[24:440]
+    ).astype(BF16)
 
 
 def second_kernel(
@@ -264,29 +267,29 @@
 
 
 def weight_kernel(*refs):
-    inner, outer = refs[0:4], refs[4:8]
+    inners, outers = refs[0:4], [ref[...].astype(F32) for ref in refs[4:8]]
     out, turned, moved, total = refs[8:]
-    first_tap = lax.axis_index("tm_0") * 2
+    place = lax.axis_index("tm_0")
     for part in range(4):
-        turned[part] = inner[part][...].astype(F32).T.astype(BF16)
-    moved[...] = jnp.zeros_like(moved)
+        turned[part] = inners[part][...].astype(F32).T.astype(BF16)
+    column = lax.broadcasted_iota(jnp.int32, (ROWS, COLS, CHANNELS), 1)
     for step in range(3):
-        tap = first_tap + step
+        tap = place * 2 + step
         row_off = jnp.where(tap >= 6, 2, jnp.where(tap >= 3, 1, 0))
-        col_off = tap - 3 * row_off
+        shift = tap - 3 * row_off - 1
         start = pl.multiple_of(row_off * 8, 8)
+        inside = (column >= shift) & (column < COLS + shift)
         summed = None
         for part in range(4):
-            low, middle, high = column_shifted(outer[part][...].astype(F32))
-            piece = jnp.where(col_off == 0, high, jnp.where(col_off == 1, middle, low))
-            slot = 4 * step + part
-            moved[slot, pl.ds(start, CELLS), :] = piece
-            term = jnp.dot(
-                turned[part], moved[slot].astype(BF16), preferred_element_type=F32
-            )
+            piece = pltpu.roll(outers[part].reshape(ROWS, COLS, CHANNELS), shift & 7, axis=1)
+            piece = jnp.where(inside, piece, 0.0).reshape(CELLS, CHANNELS)
+            moved[part, 0:16] = jnp.zeros((16, CHANNELS), F32)
+            moved[part, CELLS : CELLS + 16] = jnp.zeros((16, CHANNELS), F32)
+            moved[part, pl.ds(start, CELLS), :] = piece
+            term = jnp.dot(turned[part], moved[part].astype(BF16), preferred_element_type=F32)
             summed = term if summed is None else summed + term
         total[step * CHANNELS : (step + 1) * CHANNELS] = summed
-    base = pl.multiple_of(lax.axis_index("tm_0") * 96, 8)
+    base = pl.multiple_of(place * 96, 8)
     kept = total[pl.ds(base, 864), :]
     for block in range(16):
         out[block] = kept[54 * block : 54 * (block + 1)].astype(BF16)
@@ -334,16 +337,17 @@
         (shape((shards * 8, 256)), shape((visible, 128), F32)),
         [],
         80_000_000,
-        4,
+        62,
         tokens,
         placement,
         in_weight,
     )
     arrived = lax.all_to_all(packed, TM_FREQ, split_axis=0, concat_axis=0, tiled=True)
-
     flags = jnp.broadcast_to((patch_mask == 1)[:, :, None], (*patch_mask.shape, 128))
     aim = jnp.concatenate([targets, flags.astype(BF16)], axis=2).reshape(-1, PIX + 128)
+
     other = send(aim, "freq", 1, True)
+    weights = [conv_weight[layer : layer + 1] for layer in range(2)]
 
     own, aim, down, up, chosen = call(
         place_kernel,
@@ -364,7 +368,6 @@
     )
     above = send(down, TM, 1, False)
     below = send(up, TM, -1, False)
-    weights = [conv_weight[layer : layer + 1] for layer in range(2)]
     columns = [pltpu.VMEM((464, DEPTH), BF16), pltpu.VMEM((464, DEPTH), BF16)]
     active, unit, scale, inner = call(
         first_kernel,
@@ -376,7 +379,7 @@
         ),
         columns,
         1_500_000_000,
-        16,
+        12,
         above,
         own,
         below,
@@ -393,7 +396,7 @@
         ),
         columns,
         3_500_000_000,
-24,
+18,
         active,
         unit,
         scale,
@@ -404,9 +407,8 @@
         below,
     )
     outers = [outer] + [send(outer, "tm_0", step, True) for step in (1, 2, 3)]
-
     outgoing = call(
-        tail_kernel, shape((shards * 8, 128)), [], 1_200_000_000, 16, grad, mid, weights[0], chosen
+        tail_kernel, shape((shards * 8, 128)), [], 1_200_000_000, 12, grad, mid, weights[0], chosen
     )
     returned = lax.all_to_all(
         outgoing, TM_FREQ, split_axis=0, concat_axis=0, tiled=True
@@ -416,11 +418,11 @@
         shape((16, 54, CHANNELS)),
         [
             pltpu.VMEM((4, CHANNELS, 416), BF16),
-            pltpu.VMEM((12, 416, CHANNELS), F32),
+            pltpu.VMEM((4, 416, CHANNELS), F32),
             pltpu.VMEM((DEPTH, CHANNELS), F32),
         ],
         1_500_000_000,
-        24,
+        16,
         *inners,
         *outers,
     )

time: 117 us -> 114 us (0.974)
  local copies, waits for them, and re-layouts: 8.08 us -> 5.52 us
    unnamed x11 -> x7, local copies, waits for them, and re-layouts: 3.33 us -> 0.77 us
  transfers between devices with their start and end apart: 12 -> 12, of which waited for: 7 -> 7; matrix products, arithmetic and copies ran while one was open for 6% -> 6% of each run, Pallas kernels for 9% -> 8%
where the time goes in v3:
time: 114 us
  waiting for transfers between devices  41.9 us (37%)
  starting transfers between devices  41.6 us (36%)
  Pallas kernels  22.1 us (19%)
  local copies, waits for them, and re-layouts  5.52 us (5%)
  other arithmetic  1.75 us (2%)
    pallas_call x7, Pallas kernels, call(): pl.pallas_call(kernel, out_shape=shapes, in_specs=[VMEM] * len(operands),...  22.1 us
    all_to_all x1, waiting for transfers between devices, per_device(): lax.all_to_all(terms, ('tm_1', 'freq'), split_axis=0, concat_axis=0, tile...  18.9 us
    ppermute x9, starting transfers between devices, send(): return lax.ppermute(value, axis, pairs)  15.1 us
    ppermute x9, waiting for transfers between devices, send(): return lax.ppermute(value, axis, pairs)  14.6 us
    all_to_all x1, starting transfers between devices, per_device(): lax.all_to_all(packed, TM_FREQ, split_axis=0, concat_axis=0, tiled=True)  13 us
    all_to_all x1, waiting for transfers between devices, per_device(): lax.all_to_all(packed, TM_FREQ, split_axis=0, concat_axis=0, tiled=True)  8.46 us
    all_to_all x1, starting transfers between devices, per_device(): lax.all_to_all(outgoing, TM_FREQ, split_axis=0, concat_axis=0, tiled=True)  8.45 us
    all_to_all x1, starting transfers between devices, per_device(): lax.all_to_all(terms, ('tm_1', 'freq'), split_axis=0, concat_axis=0, tile...  5.07 us
  transfers between devices with their start and end apart: 12, of which 7 were waited for; matrix products, arithmetic and copies ran while one was open for 6% of the time, Pallas kernels for 8%

profile of v3, /device:TPU:1, one launch (start us, length us, event | category | flops | bytes accessed | tf_op | source)
XLA Modules:
  0.0 113.6 jit_solution(2121368052082871911)
XLA Ops:
  0.6 2.3 %shard_map.103 = (bf16[512,256]{1,0:T(8,128)(2,1)}, f32[40,128]{1,0:T(8,128)}) custom-call(bf16[40,768]{1,0:T(8,128)(2,1)} %tokens.1, s32[2,40]{1,0:T(2,128)} %placement.1, bf16[768,384]{1,0:T(8,128)(2,1)} %in_weight.3), custom_call_target="tpu_custom_call" | custom-call | flops 80000000 | bytes 200000 | tf_op jit(solution)/shard_map/pallas_call | solution.py:302
  3.0 13.0 %all-to-all-start = ((bf16[64,8,256]{2,1,0:T(8,128)(2,1)}), bf16[64,8,256]{2,1,0:T(8,128)(2,1)S(1)}, u32[]{:S(2)}, u32[]{:S(2)}) async-start(bf16[64,8,256]{2,1,0:T(8,128)(2,1)} %bitcast.11), calls=%async_computation | async-start | bytes 524288 | tf_op jit(solution)/shard_map/all_to_all | solution.py:345
  15.9 0.7 compare_convert_fusion
  16.6 0.1 copy.12
  16.7 0.1 broadcast_in_dim.4
  16.9 1.0 pad_maximum_fusion
  17.9 0.5 collective-permute-start
  18.4 0.7 broadcast_in_dim.10.token
  19.1 0.3 collective-permute-done.other_aim
  19.4 8.5 %all-to-all-done = bf16[64,8,256]{2,1,0:T(8,128)(2,1)S(1)} async-done(((bf16[64,8,256]{2,1,0:T(8,128)(2,1)}), bf16[64,8,256]{2,1,0:T(8,128)(2,1)S(1)}, u32[]{:S(2)}, u32[]{:S(2)}) %all-to-all-start) | async-done | bytes 262176 | tf_op jit(solution)/shard_map/all_to_all | solution.py:345
  27.9 1.3 %shard_map.104 = (bf16[400,384]{1,0:T(8,128)(2,1)S(1)}, bf16[400,384]{1,0:T(8,128)(2,1)S(1)}, bf16[48,384]{1,0:T(8,128)(2,1)S(1)}, bf16[48,384]{1,0:T(8,128)(2,1)S(1)}, bf16[512,400]{1,0:T(8,128)(2,1)S(1)}) custom-call(bf16[512,256]{1,0:T(8,128)(2,1)S(1)} %bitcast.8, bf16[200,384]{1,0:T(8,128)(2,1)S(1)} %reshape.20.own_aim, ...), custom_call_target="tpu_custom_call" | custom-call | flops 300000000 | bytes 750000 | tf_op jit(solution)/shard_map/pallas_call | solution.py:302
  29.2 3.1 %collective-permute-start.1 = (bf16[48,384]{1,0:T(8,128)(2,1)S(1)}, bf16[48,384]{1,0:T(8,128)(2,1)S(1)}, u32[]{:S(2)}, u32[]{:S(2)}) collective-permute-start(bf16[48,384]{1,0:T(8,128)(2,1)S(1)} %get-tuple-element.19), channel_id=1, source_target_pairs={{0,8},{8,16},{16,24},{24,32},{32,40},{40,48},{48,56},{56,64},{64,7... | collective-permute-start | bytes 110600 | tf_op jit(solution)/shard_map/ppermute | solution.py:324
  32.3 1.3 %collective-permute-start.2 = (bf16[48,384]{1,0:T(8,128)(2,1)S(1)}, bf16[48,384]{1,0:T(8,128)(2,1)S(1)}, u32[]{:S(2)}, u32[]{:S(2)}) collective-permute-start(bf16[48,384]{1,0:T(8,128)(2,1)S(1)} %get-tuple-element.21), channel_id=1, source_target_pairs={{8,0},{16,8},{24,16},{32,24},{40,32},{48,40},{56,48},{64,56},{72,6... | collective-permute-start | bytes 110600 | tf_op jit(solution)/shard_map/ppermute | solution.py:324
  33.6 3.1 %fusion = (bf16[1,3456,384]{2,1,0:T(8,128)(2,1)S(1)}, bf16[1,3456,384]{2,1,0:T(8,128)(2,1)S(1)}) fusion(bf16[2,3456,384]{2,1,0:T(8,128)(2,1)} %param.14), kind=kLoop, calls=%fused_computation.4 | loop fusion | bytes 10616832 | tf_op jit(solution)/shard_map/slice | solution.py:350
  36.7 0.0 collective-permute-done.1.above
  36.7 0.3 collective-permute-done.2.below
  37.0 0.0 copy-start.2
  37.0 2.9 %shard_map.105 = (bf16[448,384]{1,0:T(8,128)(2,1)S(1)}, f32[416,384]{1,0:T(8,128)S(1)}, f32[416,128]{1,0:T(8,128)S(1)}, bf16[416,384]{1,0:T(8,128)(2,1)S(1)}) custom-call(bf16[48,384]{1,0:T(8,128)(2,1)S(1)} %collective-permute-done.1.above, bf16[400,384]{1,0:T(8,128)(2,1)S(1)} %get-tuple-element.20.own, bf16[48,384]{1,0:T(8,128)(2,1)S(1)} %collective-permute-done.2.below, ...), custom_call_target="tpu_custom_call" | custom-call | flops 1500000000 | bytes 3750000 | tf_op jit(solution)/shard_map/pallas_call | solution.py:302
  39.9 0.0 copy-done.2
  39.9 6.0 %shard_map.106 = (bf16[400,256]{1,0:T(8,128)(2,1)S(1)}, bf16[400,384]{1,0:T(8,128)(2,1)S(1)}, f32[400,384]{1,0:T(8,128)S(1)}, bf16[416,384]{1,0:T(8,128)(2,1)S(1)}) custom-call(bf16[448,384]{1,0:T(8,128)(2,1)S(1)} %get-tuple-element.22.active_ref, f32[416,384]{1,0:T(8,128)S(1)} %get-tuple-element.23.unit_ref, f32[416,128]{1,0:T(8,128)S(1)} %get-tuple-element.24.scale_ref, ...), custom_call_target="tpu_custom_call" | custom-call | flops 3500000000 | bytes 8750000 | tf_op jit(solution)/shard_map/pallas_call | solution.py:302
  46.0 4.0 %collective-permute-start.6 = (bf16[400,384]{1,0:T(8,128)(2,1)S(1)}, bf16[400,384]{1,0:T(8,128)(2,1)S(1)}, u32[]{:S(2)}, u32[]{:S(2)}) collective-permute-start(bf16[400,384]{1,0:T(8,128)(2,1)S(1)} %get-tuple-element.32.refs_4_), channel_id=1, source_target_pairs={{0,64},{64,128},{128,192},{192,0},{1,65},{65,129},{129,193},{193,1... | collective-permute-start | bytes 921608 | tf_op jit(solution)/shard_map/ppermute | solution.py:324
  49.9 1.3 %collective-permute-start.3 = (bf16[416,384]{1,0:T(8,128)(2,1)S(1)}, bf16[416,384]{1,0:T(8,128)(2,1)S(1)}, u32[]{:S(2)}, u32[]{:S(2)}) collective-permute-start(bf16[416,384]{1,0:T(8,128)(2,1)S(1)} %get-tuple-element.31.refs_0_), channel_id=1, source_target_pairs={{0,64},{64,128},{128,192},{192,0},{1,65},{65,129},{129,193},{193,1... | collective-permute-start | bytes 958472 | tf_op jit(solution)/shard_map/ppermute | solution.py:324
  51.2 1.4 %collective-permute-start.4 = (bf16[416,384]{1,0:T(8,128)(2,1)S(1)}, bf16[416,384]{1,0:T(8,128)(2,1)S(1)}, u32[]{:S(2)}, u32[]{:S(2)}) collective-permute-start(bf16[416,384]{1,0:T(8,128)(2,1)S(1)} %get-tuple-element.31.refs_0_), channel_id=1, source_target_pairs={{0,128},{64,192},{128,0},{192,64},{1,129},{65,193},{129,1},{193,65... | collective-permute-start | bytes 958472 | tf_op jit(solution)/shard_map/ppermute | solution.py:324
  52.6 2.0 %collective-permute-start.5 = (bf16[416,384]{1,0:T(8,128)(2,1)S(1)}, bf16[416,384]{1,0:T(8,128)(2,1)S(1)}, u32[]{:S(2)}, u32[]{:S(2)}) collective-permute-start(bf16[416,384]{1,0:T(8,128)(2,1)S(1)} %get-tuple-element.31.refs_0_), channel_id=1, source_target_pairs={{0,192},{64,0},{128,64},{192,128},{1,193},{65,1},{129,65},{193,129... | collective-permute-start | bytes 958472 | tf_op jit(solution)/shard_map/ppermute | solution.py:324
  54.6 0.4 collective-permute-start.7
  55.0 3.1 %collective-permute-done.6.refs_5_ = bf16[400,384]{1,0:T(8,128)(2,1)S(1)} collective-permute-done((bf16[400,384]{1,0:T(8,128)(2,1)S(1)}, bf16[400,384]{1,0:T(8,128)(2,1)S(1)}, u32[]{:S(2)}, u32[]{:S(2)}) %collective-permute-start.6) | collective-permute-done | bytes 307232 | tf_op jit(solution)/shard_map/ppermute | solution.py:324
  58.0 1.2 %collective-permute-start.8 = (bf16[400,384]{1,0:T(8,128)(2,1)S(1)}, bf16[400,384]{1,0:T(8,128)(2,1)S(1)}, u32[]{:S(2)}, u32[]{:S(2)}) collective-permute-start(bf16[400,384]{1,0:T(8,128)(2,1)S(1)} %get-tuple-element.32.refs_4_), channel_id=1, source_target_pairs={{0,192},{64,0},{128,64},{192,128},{1,193},{65,1},{129,65},{193,129... | collective-permute-start | bytes 921608 | tf_op jit(solution)/shard_map/ppermute | solution.py:324
  59.2 2.9 %shard_map.107 = bf16[512,128]{1,0:T(8,128)(2,1)} custom-call(bf16[416,384]{1,0:T(8,128)(2,1)S(1)} %get-tuple-element.27.grad_ref, f32[400,384]{1,0:T(8,128)S(1)} %get-tuple-element.28.mid_ref, bf16[1,3456,384]{2,1,0:T(8,128)(2,1)S(1)} %get-tuple-element.37.weight, bf16[512,400]{1,0:T(8,128)(2,1)S(1)} %get-tuple-element.29.chosen), custom_call_target="tpu_custom_call" | custom-call | flops 1200000000 | bytes 3000000 | tf_op jit(solution)/shard_map/pallas_call | solution.py:302
  62.1 8.4 %all-to-all-start.1 = ((bf16[64,8,128]{2,1,0:T(8,128)(2,1)}), bf16[64,8,128]{2,1,0:T(8,128)(2,1)S(1)}, u32[]{:S(2)}, u32[]{:S(2)}) async-start(bf16[64,8,128]{2,1,0:T(8,128)(2,1)} %bitcast.3), calls=%async_computation.1 | async-start | bytes 262144 | tf_op jit(solution)/shard_map/all_to_all | solution.py:413
  70.5 0.0 copy-start
  70.5 0.0 copy-start.1
  70.5 9.8 %collective-permute-done.7.refs_6_ = bf16[400,384]{1,0:T(8,128)(2,1)S(1)} collective-permute-done((bf16[400,384]{1,0:T(8,128)(2,1)S(1)}, bf16[400,384]{1,0:T(8,128)(2,1)S(1)}, u32[]{:S(2)}, u32[]{:S(2)}) %collective-permute-start.7) | collective-permute-done | bytes 307232 | tf_op jit(solution)/shard_map/ppermute | solution.py:324
  80.4 1.1 collective-permute-done.8.refs_7_
  81.4 0.0 collective-permute-done.3.refs_1_
  81.4 0.0 collective-permute-done.4.refs_2_
  81.4 0.0 collective-permute-done.5.refs_3_
  81.4 5.5 %shard_map.109 = bf16[16,54,384]{2,1,0:T(8,128)(2,1)} custom-call(bf16[416,384]{1,0:T(8,128)(2,1)S(1)} %get-tuple-element.31.refs_0_, bf16[416,384]{1,0:T(8,128)(2,1)S(1)} %collective-permute-done.3.refs_1_, bf16[416,384]{1,0:T(8,128)(2,1)S(1)} %collective-permute-done.4.refs_2_, bf16[416,384]{1,0:T(8,128)(2,1)S(1)} %collective-permute-done.5.refs_3_, ...), custom_call_target="tpu_custom_call" | custom-call | flops 1500000000 | bytes 3750000 | tf_op jit(solution)/shard_map/pallas_call | solution.py:302
  87.0 0.0 all-to-all-done.1
  87.0 5.1 %all-to-all-start.2 = ((bf16[16,54,384]{2,1,0:T(8,128)(2,1)}), bf16[16,54,384]{2,1,0:T(8,128)(2,1)S(1)}, u32[]{:S(2)}, u32[]{:S(2)}) async-start(bf16[16,54,384]{2,1,0:T(8,128)(2,1)} %shard_map.109), calls=%async_computation.2 | async-start | bytes 1376256 | tf_op jit(solution)/shard_map/all_to_all | solution.py:429
  92.0 0.7 constant_dynamic-slice_fusion
  92.7 0.0 copy-done
  92.7 0.0 copy-done.1
  92.7 1.1 shard_map.108
  93.9 18.9 %all-to-all-done.2 = bf16[16,54,384]{2,1,0:T(8,128)(2,1)S(1)} async-done(((bf16[16,54,384]{2,1,0:T(8,128)(2,1)}), bf16[16,54,384]{2,1,0:T(8,128)(2,1)S(1)}, u32[]{:S(2)}, u32[]{:S(2)}) %all-to-all-start.2) | async-done | bytes 663584 | tf_op jit(solution)/shard_map/all_to_all | solution.py:429
  112.7 0.1 convert_reduce_fusion
  112.8 0.8 copy.13
  (1 shorter events, 0.0 us)
Async XLA Ops:
  3.0 24.9 %all-to-all-start = ((bf16[64,8,256]{2,1,0:T(8,128)(2,1)}), bf16[64,8,256]{2,1,0:T(8,128)(2,1)S(1)}, u32[]{:S(2)}, u32[]{:S(2)}) async-start(bf16[64,8,256]{2,1,0:T(8,128)(2,1)} %bitcast.11), calls=%async_computation | async-start | bytes 524288 | tf_op jit(solution)/shard_map/all_to_all | solution.py:345
  17.9 1.6 %collective-permute-start = (bf16[200,384]{1,0:T(8,128)(2,1)S(1)}, bf16[200,384]{1,0:T(8,128)(2,1)S(1)}, u32[]{:S(2)}, u32[]{:S(2)}) collective-permute-start(bf16[200,384]{1,0:T(8,128)(2,1)S(1)} %reshape.20.own_aim), channel_id=1, source_target_pairs={{0,4},{4,0},{1,5},{5,1},{2,6},{6,2},{3,7},{7,3},{8,12},{12,8},{9,1... | collective-permute-start | bytes 460808 | tf_op jit(solution)/shard_map/ppermute | solution.py:324
  29.2 7.5 %collective-permute-start.1 = (bf16[48,384]{1,0:T(8,128)(2,1)S(1)}, bf16[48,384]{1,0:T(8,128)(2,1)S(1)}, u32[]{:S(2)}, u32[]{:S(2)}) collective-permute-start(bf16[48,384]{1,0:T(8,128)(2,1)S(1)} %get-tuple-element.19), channel_id=1, source_target_pairs={{0,8},{8,16},{16,24},{24,32},{32,40},{40,48},{48,56},{56,64},{64,7... | collective-permute-start | bytes 110600 | tf_op jit(solution)/shard_map/ppermute | solution.py:324
  32.3 4.7 %collective-permute-start.2 = (bf16[48,384]{1,0:T(8,128)(2,1)S(1)}, bf16[48,384]{1,0:T(8,128)(2,1)S(1)}, u32[]{:S(2)}, u32[]{:S(2)}) collective-permute-start(bf16[48,384]{1,0:T(8,128)(2,1)S(1)} %get-tuple-element.21), channel_id=1, source_target_pairs={{8,0},{16,8},{24,16},{32,24},{40,32},{48,40},{56,48},{64,56},{72,6... | collective-permute-start | bytes 110600 | tf_op jit(solution)/shard_map/ppermute | solution.py:324
  37.0 2.9 %copy-start.2 = (bf16[384,256]{1,0:T(8,128)(2,1)S(1)}, bf16[384,256]{1,0:T(8,128)(2,1)}, u32[]{:S(2)}) copy-start(bf16[384,256]{1,0:T(8,128)(2,1)} %head.1) | copy-start | bytes 589828
  46.0 12.1 %collective-permute-start.6 = (bf16[400,384]{1,0:T(8,128)(2,1)S(1)}, bf16[400,384]{1,0:T(8,128)(2,1)S(1)}, u32[]{:S(2)}, u32[]{:S(2)}) collective-permute-start(bf16[400,384]{1,0:T(8,128)(2,1)S(1)} %get-tuple-element.32.refs_4_), channel_id=1, source_target_pairs={{0,64},{64,128},{128,192},{192,0},{1,65},{65,129},{129,193},{193,1... | collective-permute-start | bytes 921608 | tf_op jit(solution)/shard_map/ppermute | solution.py:324
  49.9 31.5 %collective-permute-start.3 = (bf16[416,384]{1,0:T(8,128)(2,1)S(1)}, bf16[416,384]{1,0:T(8,128)(2,1)S(1)}, u32[]{:S(2)}, u32[]{:S(2)}) collective-permute-start(bf16[416,384]{1,0:T(8,128)(2,1)S(1)} %get-tuple-element.31.refs_0_), channel_id=1, source_target_pairs={{0,64},{64,128},{128,192},{192,0},{1,65},{65,129},{129,193},{193,1... | collective-permute-start | bytes 958472 | tf_op jit(solution)/shard_map/ppermute | solution.py:324
  51.2 30.2 %collective-permute-start.4 = (bf16[416,384]{1,0:T(8,128)(2,1)S(1)}, bf16[416,384]{1,0:T(8,128)(2,1)S(1)}, u32[]{:S(2)}, u32[]{:S(2)}) collective-permute-start(bf16[416,384]{1,0:T(8,128)(2,1)S(1)} %get-tuple-element.31.refs_0_), channel_id=1, source_target_pairs={{0,128},{64,192},{128,0},{192,64},{1,129},{65,193},{129,1},{193,65... | collective-permute-start | bytes 958472 | tf_op jit(solution)/shard_map/ppermute | solution.py:324
  52.6 28.8 %collective-permute-start.5 = (bf16[416,384]{1,0:T(8,128)(2,1)S(1)}, bf16[416,384]{1,0:T(8,128)(2,1)S(1)}, u32[]{:S(2)}, u32[]{:S(2)}) collective-permute-start(bf16[416,384]{1,0:T(8,128)(2,1)S(1)} %get-tuple-element.31.refs_0_), channel_id=1, source_target_pairs={{0,192},{64,0},{128,64},{192,128},{1,193},{65,1},{129,65},{193,129... | collective-permute-start | bytes 958472 | tf_op jit(solution)/shard_map/ppermute | solution.py:324
  54.6 25.8 %collective-permute-start.7 = (bf16[400,384]{1,0:T(8,128)(2,1)S(1)}, bf16[400,384]{1,0:T(8,128)(2,1)S(1)}, u32[]{:S(2)}, u32[]{:S(2)}) collective-permute-start(bf16[400,384]{1,0:T(8,128)(2,1)S(1)} %get-tuple-element.32.refs_4_), channel_id=1, source_target_pairs={{0,128},{64,192},{128,0},{192,64},{1,129},{65,193},{129,1},{193,65... | collective-permute-start | bytes 921608 | tf_op jit(solution)/shard_map/ppermute | solution.py:324
  58.0 23.4 %collective-permute-start.8 = (bf16[400,384]{1,0:T(8,128)(2,1)S(1)}, bf16[400,384]{1,0:T(8,128)(2,1)S(1)}, u32[]{:S(2)}, u32[]{:S(2)}) collective-permute-start(bf16[400,384]{1,0:T(8,128)(2,1)S(1)} %get-tuple-element.32.refs_4_), channel_id=1, source_target_pairs={{0,192},{64,0},{128,64},{192,128},{1,193},{65,1},{129,65},{193,129... | collective-permute-start | bytes 921608 | tf_op jit(solution)/shard_map/ppermute | solution.py:324
  62.1 24.9 %all-to-all-start.1 = ((bf16[64,8,128]{2,1,0:T(8,128)(2,1)}), bf16[64,8,128]{2,1,0:T(8,128)(2,1)S(1)}, u32[]{:S(2)}, u32[]{:S(2)}) async-start(bf16[64,8,128]{2,1,0:T(8,128)(2,1)} %bitcast.3), calls=%async_computation.1 | async-start | bytes 262144 | tf_op jit(solution)/shard_map/all_to_all | solution.py:413
  70.5 22.2 %copy-start = (bf16[768,384]{1,0:T(8,128)(2,1)S(1)}, bf16[768,384]{1,0:T(8,128)(2,1)}, u32[]{:S(2)}) copy-start(bf16[768,384]{1,0:T(8,128)(2,1)} %in_weight.3) | copy-start | bytes 1769476
  70.5 22.2 %copy-start.1 = (f32[40,128]{1,0:T(8,128)S(1)}, f32[40,128]{1,0:T(8,128)}, u32[]{:S(2)}) copy-start(f32[40,128]{1,0:T(8,128)} %get-tuple-element.30.where_ref) | copy-start | bytes 61444
  87.0 25.8 %all-to-all-start.2 = ((bf16[16,54,384]{2,1,0:T(8,128)(2,1)}), bf16[16,54,384]{2,1,0:T(8,128)(2,1)S(1)}, u32[]{:S(2)}, u32[]{:S(2)}) async-start(bf16[16,54,384]{2,1,0:T(8,128)(2,1)} %shard_map.109), calls=%async_computation.2 | async-start | bytes 1376256 | tf_op jit(solution)/shard_map/all_to_all | solution.py:429

commit v4 on v3

--- a/solution.py
+++ b/solution.py
@@ -104,6 +104,27 @@
     return summed[:, CHANNELS : 2 * CHANNELS] + total.reshape(cells, CHANNELS)
 
 
+def quarters(value):
+    tiles = [value[:, 128 * part : 128 * (part + 1)] for part in range(3)]
+    lane = lax.broadcasted_iota(jnp.int32, tiles[0].shape, 1)
+    one = jnp.where(lane < 32, pltpu.roll(tiles[0], 32, axis=1), pltpu.roll(tiles[1], 32, axis=1))
+    two = jnp.where(lane < 64, pltpu.roll(tiles[1], 64, axis=1), pltpu.roll(tiles[2], 64, axis=1))
+    return tiles[0], one, two, pltpu.roll(tiles[2], 96, axis=1)
+
+
+def joined(parts):
+    lane = lax.broadcasted_iota(jnp.int32, parts[0].shape, 1)
+    one = pltpu.roll(parts[1], 96, axis=1)
+    two = pltpu.roll(parts[2], 64, axis=1)
+    three = pltpu.roll(parts[3], 32, axis=1)
+    tiles = (
+        jnp.where(lane < 96, parts[0], one),
+        jnp.where(lane < 64, one, two),
+        jnp.where(lane < 32, two, three),
+    )
+    return jnp.concatenate(tiles, axis=1)
+
+
 def normed(conv_out):
     center = conv_out - jnp.mean(conv_out, axis=-1, keepdims=True)
     scale = lax.rsqrt(jnp.mean(center * center, axis=-1, keepdims=True) + 1e-05)
@@ -189,8 +210,8 @@
     spread = jnp.broadcast_to(cell, (slots, 128)).reshape(slots // 8, 8, 128)
     first = jnp.sum(jnp.where(within == 4 + 2 * core, spread, 0.0), axis=1, keepdims=True)
     second = jnp.sum(jnp.where(within == 5 + 2 * core, spread, 0.0), axis=1, keepdims=True)
-    spread = jnp.where((within & 1) == 0, first, second)
-    spread = jnp.where(within < 6, spread, -1.0).reshape(slots, 128)
+    spread = jnp.where(within == 6, first, jnp.where(within == 7, second, -1.0))
+    spread = spread.reshape(slots, 128)
     chosen_out[...] = jnp.where(lane == spread[:, 0:1].astype(jnp.int32), 1.0, 0.0).astype(BF16)
 
 
@@ -214,7 +235,7 @@
 
 def second_kernel(
     active_ref, unit_ref, scale_ref, weight, head, above, aim_ref, below,
-    pred, share_out, mid_out, grad_out, even, odd,
+    pred, share_own, share_one, share_two, share_three, mid_out, grad_out, even, odd,
 ):
     active = active_ref[...].astype(F32)
     store_columns(active, even, odd)
@@ -235,64 +256,84 @@
     grad_one = jnp.where(rows_valid(416, 1), grad_one, 0.0)
     grad_out[...] = grad_one.astype(BF16)
     mid_out[...] = grad_mid[8:408]
-    share_out[...] = jnp.where(
-        lax.axis_index("freq") == 1, grad_two.astype(F32)[16:416], grad_one[8:408]
-    ).astype(BF16)
+    share = jnp.where(lax.axis_index("freq") == 1, grad_two.astype(F32)[16:416], grad_one[8:408])
+    pieces = quarters(share)
+    lane = lax.broadcasted_iota(jnp.int32, (CELLS, 128), 1)
+    for step, share_out in enumerate((share_own, share_one, share_two, share_three)):
+        quarter = (lax.axis_index("tm_0") + step) & 3
+        piece = jnp.where(quarter == 0, pieces[0], pieces[1])
+        piece = jnp.where(quarter >= 2, jnp.where(quarter == 2, pieces[2], pieces[3]), piece)
+        share_out[...] = jnp.where(lane < 96, piece, 0.0).astype(BF16)
 
 
 def tail_kernel(grad_ref, mid_ref, weight, chosen, out):
     grad_cells = mid_ref[...] + conv_back(grad_ref[...], weight, CELLS)
-    picked = jnp.dot(chosen[...], grad_cells.astype(BF16), preferred_element_type=F32)
-    part = lax.broadcasted_iota(jnp.int32, out.shape, 0) & 6
-    picked = jnp.where(
-        part == 0, picked[:, 0:128], jnp.where(part == 2, picked[:, 128:256], picked[:, 256:384])
-    )
-    out[...] = picked.astype(BF16)
-
-
-def finish_kernel(returned, where_ref, in_weight, out):
+    out[...] = jnp.dot(chosen[...], grad_cells.astype(BF16), preferred_element_type=F32)
+
+
+def turn_kernel(*refs):
+    for part in range(4):
+        refs[4][part] = refs[part][...].astype(F32).T.astype(BF16)
+
+
+def weight_kernel(turned, *refs):
+    outers, picked = refs[0:4], refs[4]
+    out, moved, total = refs[5:]
+    summed = None
+    for part in range(4):
+        low, middle, high = column_shifted(outers[part][...].astype(F32))
+        for row_off in range(3):
+            for col_off, piece in enumerate((high, middle, low)):
+                rows = [piece]
+                if row_off:
+                    rows.insert(0, jnp.zeros((8 * row_off, 128), F32))
+                if row_off < 2:
+                    rows.append(jnp.zeros((16 - 8 * row_off, 128), F32))
+                tap = 3 * row_off + col_off
+                moved[part, :, tap * 128 : (tap + 1) * 128] = jnp.concatenate(
+                    rows, axis=0
+                ).astype(BF16)
+        term = jnp.dot(turned[part], moved[part], preferred_element_type=F32)
+        summed = term if summed is None else summed + term
+    for tap in range(9):
+        total[tap * CHANNELS : (tap + 1) * CHANNELS] = summed[:, tap * 128 : (tap + 1) * 128]
+    total[9 * CHANNELS :] = jnp.zeros((8, 128), F32)
+    row = lax.broadcasted_iota(jnp.int32, (16, CHANNELS), 0)
+    for shard in range(64):
+        start = 54 * shard
+        packed = joined([total[start + 14 * part : start + 14 * part + 16] for part in range(4)])
+        back = picked[8 * shard : 8 * shard + 8]
+        packed = jnp.where(row >= 14, jnp.concatenate([back, back], axis=0), packed)
+        out[shard] = packed.astype(BF16)
+
+
+def finish_kernel(arrived, where_ref, in_weight, token_out, conv_out):
     count = where_ref.shape[0]
-    slots = returned.shape[0]
-    index = lax.broadcasted_iota(jnp.int32, (count, slots), 1)
-    slot = lax.shift_right_logical(index, 3) * 2 + (index & 1)
-    hit = where_ref[:, 0:1].astype(jnp.int32) == slot
-    parts = []
-    for part in range(3):
-        taken = jnp.where(hit & ((index & 6) == 2 * part), 1.0, 0.0).astype(BF16)
-        parts.append(jnp.dot(taken, returned[...], preferred_element_type=F32))
-    grad_proj = jnp.concatenate(parts, axis=1).astype(BF16)
-    out[...] = lax.dot_general(
+    rows = arrived.shape[0] * 16
+    index = lax.broadcasted_iota(jnp.int32, (count, rows), 1)
+    within = index & 15
+    slot = lax.shift_right_logical(index, 4) * 2 + within - 14
+    hit = (where_ref[:, 0:1].astype(jnp.int32) == slot) & (within >= 14)
+    grad_proj = jnp.dot(
+        jnp.where(hit, 1.0, 0.0).astype(BF16),
+        arrived[...].reshape(rows, CHANNELS),
+        preferred_element_type=F32,
+    ).astype(BF16)
+    token_out[...] = lax.dot_general(
         grad_proj, in_weight[...], (((1,), (1,)), ((), ())), preferred_element_type=F32
     )
-
-
-def weight_kernel(*refs):
-    inners, outers = refs[0:4], [ref[...].astype(F32) for ref in refs[4:8]]
-    out, turned, moved, total = refs[8:]
-    place = lax.axis_index("tm_0")
-    for part in range(4):
-        turned[part] = inners[part][...].astype(F32).T.astype(BF16)
-    column = lax.broadcasted_iota(jnp.int32, (ROWS, COLS, CHANNELS), 1)
-    for step in range(3):
-        tap = place * 2 + step
-        row_off = jnp.where(tap >= 6, 2, jnp.where(tap >= 3, 1, 0))
-        shift = tap - 3 * row_off - 1
-        start = pl.multiple_of(row_off * 8, 8)
-        inside = (column >= shift) & (column < COLS + shift)
-        summed = None
-        for part in range(4):
-            piece = pltpu.roll(outers[part].reshape(ROWS, COLS, CHANNELS), shift & 7, axis=1)
-            piece = jnp.where(inside, piece, 0.0).reshape(CELLS, CHANNELS)
-            moved[part, 0:16] = jnp.zeros((16, CHANNELS), F32)
-            moved[part, CELLS : CELLS + 16] = jnp.zeros((16, CHANNELS), F32)
-            moved[part, pl.ds(start, CELLS), :] = piece
-            term = jnp.dot(turned[part], moved[part].astype(BF16), preferred_element_type=F32)
-            summed = term if summed is None else summed + term
-        total[step * CHANNELS : (step + 1) * CHANNELS] = summed
-    base = pl.multiple_of(place * 96, 8)
-    kept = total[pl.ds(base, 864), :]
-    for block in range(16):
-        out[block] = kept[54 * block : 54 * (block + 1)].astype(BF16)
+    for layer in range(2):
+        parts = []
+        for peer in range(4):
+            summed = None
+            for near in range(8):
+                term = arrived[16 * peer + 2 * near + layer].astype(F32)
+                summed = term if summed is None else summed + term
+            parts.append(quarters(summed))
+        for group in range(4):
+            height = min(14, 54 - 14 * group)
+            wide = joined([parts[peer][group] for peer in range(4)])
+            conv_out[layer, 14 * group : 14 * group + height] = wide[0:height]
 
 
 VMEM = pl.BlockSpec(memory_space=pltpu.VMEM)
@@ -386,17 +427,17 @@
         weights[0],
     )
     inners = [inner] + [send(inner, "tm_0", step, True) for step in (1, 2, 3)]
-    pred, outer, mid, grad = call(
+    pred, *outers, mid, grad = call(
         second_kernel,
         (
             shape((CELLS, PIX)),
-            shape((CELLS, CHANNELS)),
+            *[shape((CELLS, 128))] * 4,
             shape((CELLS, CHANNELS), F32),
             shape((416, CHANNELS)),
         ),
         columns,
         3_500_000_000,
-18,
+        18,
         active,
         unit,
         scale,
@@ -406,38 +447,40 @@
         aim,
         below,
     )
-    outers = [outer] + [send(outer, "tm_0", step, True) for step in (1, 2, 3)]
-    outgoing = call(
-        tail_kernel, shape((shards * 8, 128)), [], 1_200_000_000, 12, grad, mid, weights[0], chosen
-    )
-    returned = lax.all_to_all(
-        outgoing, TM_FREQ, split_axis=0, concat_axis=0, tiled=True
-    )
+    outers[1:] = [send(outers[step], "tm_0", step, True) for step in (1, 2, 3)]
+    picked = call(
+        tail_kernel,
+        shape((shards * 8, CHANNELS), F32),
+        [],
+        1_200_000_000,
+        12,
+        grad,
+        mid,
+        weights[0],
+        chosen,
+    )
+    turned = call(turn_kernel, shape((4, CHANNELS, 416)), [], 400_000_000, 8, *inners)
     terms = call(
         weight_kernel,
-        shape((16, 54, CHANNELS)),
-        [
-            pltpu.VMEM((4, CHANNELS, 416), BF16),
-            pltpu.VMEM((4, 416, CHANNELS), F32),
-            pltpu.VMEM((DEPTH, CHANNELS), F32),
-        ],
+        shape((shards, 16, CHANNELS)),
+        [pltpu.VMEM((4, 416, 9 * 128), BF16), pltpu.VMEM((9 * CHANNELS + 8, 128), F32)],
         1_500_000_000,
         16,
-        *inners,
+        turned,
         *outers,
-    )
-    terms = lax.all_to_all(terms, ("tm_1", "freq"), split_axis=0, concat_axis=0, tiled=True)
-    token_grad = call(
+        picked,
+    )
+    terms = lax.all_to_all(terms, TM_FREQ, split_axis=0, concat_axis=0, tiled=True)
+    token_grad, conv_grad = call(
         finish_kernel,
-        shape((visible, in_weight.shape[0]), F32),
+        (shape((visible, in_weight.shape[0]), F32), shape((2, 54, CHANNELS), F32)),
         [],
         80_000_000,
-        4,
-        returned,
+        6,
+        terms,
         where_to,
         in_weight,
     )
-    conv_grad = terms.reshape(-1, 2, 54, CHANNELS).astype(F32).sum(axis=0)
     pred = lax.dynamic_slice_in_dim(pred.reshape(ROWS, COLS, PIX), core * half, half, axis=1)
     return (pred, token_grad, conv_grad)
 

time: 114 us -> 101 us (0.89)
  starting transfers between devices: 41.6 us -> 35.6 us
  waiting for transfers between devices: 41.9 us -> 36.5 us
  Pallas kernels: 22.1 us -> 20.1 us
    ppermute x9, waiting for transfers between devices: 14.6 us -> 5.82 us  [send(): return lax.ppermute(value, axis, pairs)]
    all_to_all x2 -> x1, starting transfers between devices: 13.5 us -> 7.33 us  [per_device(): lax.all_to_all(terms, TM_FREQ, split_axis=0, concat_axis=0, tiled=True)]
    all_to_all x2 -> x1, waiting for transfers between devices: 18.9 us -> 22.2 us  [per_device(): lax.all_to_all(terms, TM_FREQ, split_axis=0, concat_axis=0, tiled=True)]
    pallas_call x7 -> x8, Pallas kernels: 22.1 us -> 20.1 us  [call(): pl.pallas_call(kernel, out_shape=shapes, in_specs=[VMEM] * len(operands),...]
  transfers between devices with their start and end apart: 12 -> 11, of which waited for: 7 -> 7; matrix products, arithmetic and copies ran while one was open for 6% -> 6% of each run, Pallas kernels for 8% -> 9%
where the time goes in v4:
time: 101 us; the launch traced here: 100 us
  waiting for transfers between devices  36.5 us (36%)
  starting transfers between devices  35.6 us (35%)
  Pallas kernels  20.1 us (20%)
  local copies, waits for them, and re-layouts  5.52 us (5%)
  other arithmetic  1.66 us (2%)
    all_to_all x1, waiting for transfers between devices, per_device(): lax.all_to_all(terms, TM_FREQ, split_axis=0, concat_axis=0, tiled=True)  22.2 us
    pallas_call x8, Pallas kernels, call(): pl.pallas_call(kernel, out_shape=shapes, in_specs=[VMEM] * len(operands),...  20.1 us
    ppermute x9, starting transfers between devices, send(): return lax.ppermute(value, axis, pairs)  15.3 us
    all_to_all x1, starting transfers between devices, per_device(): lax.all_to_all(packed, TM_FREQ, split_axis=0, concat_axis=0, tiled=True)  13 us
    all_to_all x1, waiting for transfers between devices, per_device(): lax.all_to_all(packed, TM_FREQ, split_axis=0, concat_axis=0, tiled=True)  8.46 us
    all_to_all x1, starting transfers between devices, per_device(): lax.all_to_all(terms, TM_FREQ, split_axis=0, concat_axis=0, tiled=True)  7.33 us
    ppermute x9, waiting for transfers between devices, send(): return lax.ppermute(value, axis, pairs)  5.82 us
    slice x1, local copies, waits for them, and re-layouts, per_device(): weights = [conv_weight[layer:layer + 1] for layer in range(2)]  3.09 us
  transfers between devices with their start and end apart: 11, of which 7 were waited for; matrix products, arithmetic and copies ran while one was open for 6% of the time, Pallas kernels for 9%

profile of v4, /device:TPU:1, one launch (start us, length us, event | category | flops | bytes accessed | tf_op | source)
XLA Modules:
  0.0 100.1 jit_solution(15669812748921581461)
XLA Ops:
  0.6 2.3 %shard_map.103 = (bf16[512,256]{1,0:T(8,128)(2,1)}, f32[40,128]{1,0:T(8,128)}) custom-call(bf16[40,768]{1,0:T(8,128)(2,1)} %tokens.1, s32[2,40]{1,0:T(2,128)} %placement.1, bf16[768,384]{1,0:T(8,128)(2,1)} %in_weight.3), custom_call_target="tpu_custom_call" | custom-call | flops 80000000 | bytes 200000 | tf_op jit(solution)/shard_map/pallas_call | solution.py:343
  3.0 13.0 %all-to-all-start = ((bf16[64,8,256]{2,1,0:T(8,128)(2,1)}), bf16[64,8,256]{2,1,0:T(8,128)(2,1)S(1)}, u32[]{:S(2)}, u32[]{:S(2)}) async-start(bf16[64,8,256]{2,1,0:T(8,128)(2,1)} %bitcast.5), calls=%async_computation | async-start | bytes 524288 | tf_op jit(solution)/shard_map/all_to_all | solution.py:386
  15.9 0.7 compare_convert_fusion
  16.6 0.1 copy.11
  16.7 0.1 broadcast_in_dim.4
  16.9 1.0 pad_maximum_fusion
  17.9 0.5 collective-permute-start
  18.4 0.7 broadcast_in_dim.10.token
  19.1 0.3 collective-permute-done.other_aim
  19.4 8.5 %all-to-all-done = bf16[64,8,256]{2,1,0:T(8,128)(2,1)S(1)} async-done(((bf16[64,8,256]{2,1,0:T(8,128)(2,1)}), bf16[64,8,256]{2,1,0:T(8,128)(2,1)S(1)}, u32[]{:S(2)}, u32[]{:S(2)}) %all-to-all-start) | async-done | bytes 262176 | tf_op jit(solution)/shard_map/all_to_all | solution.py:386
  27.9 1.3 %shard_map.104 = (bf16[400,384]{1,0:T(8,128)(2,1)S(1)}, bf16[400,384]{1,0:T(8,128)(2,1)S(1)}, bf16[48,384]{1,0:T(8,128)(2,1)S(1)}, bf16[48,384]{1,0:T(8,128)(2,1)S(1)}, bf16[512,400]{1,0:T(8,128)(2,1)S(1)}) custom-call(bf16[512,256]{1,0:T(8,128)(2,1)S(1)} %bitcast.3, bf16[200,384]{1,0:T(8,128)(2,1)S(1)} %reshape.15.own_aim, ...), custom_call_target="tpu_custom_call" | custom-call | flops 300000000 | bytes 750000 | tf_op jit(solution)/shard_map/pallas_call | solution.py:343
  29.2 3.1 %collective-permute-start.1 = (bf16[48,384]{1,0:T(8,128)(2,1)S(1)}, bf16[48,384]{1,0:T(8,128)(2,1)S(1)}, u32[]{:S(2)}, u32[]{:S(2)}) collective-permute-start(bf16[48,384]{1,0:T(8,128)(2,1)S(1)} %get-tuple-element.24), channel_id=1, source_target_pairs={{0,8},{8,16},{16,24},{24,32},{32,40},{40,48},{48,56},{56,64},{64,7... | collective-permute-start | bytes 110600 | tf_op jit(solution)/shard_map/ppermute | solution.py:365
  32.3 1.3 %collective-permute-start.2 = (bf16[48,384]{1,0:T(8,128)(2,1)S(1)}, bf16[48,384]{1,0:T(8,128)(2,1)S(1)}, u32[]{:S(2)}, u32[]{:S(2)}) collective-permute-start(bf16[48,384]{1,0:T(8,128)(2,1)S(1)} %get-tuple-element.26), channel_id=1, source_target_pairs={{8,0},{16,8},{24,16},{32,24},{40,32},{48,40},{56,48},{64,56},{72,6... | collective-permute-start | bytes 110600 | tf_op jit(solution)/shard_map/ppermute | solution.py:365
  33.6 3.1 %fusion = (bf16[1,3456,384]{2,1,0:T(8,128)(2,1)S(1)}, bf16[1,3456,384]{2,1,0:T(8,128)(2,1)S(1)}) fusion(bf16[2,3456,384]{2,1,0:T(8,128)(2,1)} %param.14), kind=kLoop, calls=%fused_computation.3 | loop fusion | bytes 10616832 | tf_op jit(solution)/shard_map/slice | solution.py:391
  36.7 0.0 collective-permute-done.1.above
  36.7 0.3 collective-permute-done.2.below
  37.0 0.0 copy-start.2
  37.0 2.9 %shard_map.105 = (bf16[448,384]{1,0:T(8,128)(2,1)S(1)}, f32[416,384]{1,0:T(8,128)S(1)}, f32[416,128]{1,0:T(8,128)S(1)}, bf16[416,384]{1,0:T(8,128)(2,1)S(1)}) custom-call(bf16[48,384]{1,0:T(8,128)(2,1)S(1)} %collective-permute-done.1.above, bf16[400,384]{1,0:T(8,128)(2,1)S(1)} %get-tuple-element.25.own, bf16[48,384]{1,0:T(8,128)(2,1)S(1)} %collective-permute-done.2.below, ...), custom_call_target="tpu_custom_call" | custom-call | flops 1500000000 | bytes 3750000 | tf_op jit(solution)/shard_map/pallas_call | solution.py:343
  39.9 3.8 %collective-permute-start.3 = (bf16[416,384]{1,0:T(8,128)(2,1)S(1)}, bf16[416,384]{1,0:T(8,128)(2,1)S(1)}, u32[]{:S(2)}, u32[]{:S(2)}) collective-permute-start(bf16[416,384]{1,0:T(8,128)(2,1)S(1)} %get-tuple-element.32.refs_0_), channel_id=1, source_target_pairs={{0,64},{64,128},{128,192},{192,0},{1,65},{65,129},{129,193},{193,1... | collective-permute-start | bytes 958472 | tf_op jit(solution)/shard_map/ppermute | solution.py:365
  43.7 2.6 %collective-permute-start.4 = (bf16[416,384]{1,0:T(8,128)(2,1)S(1)}, bf16[416,384]{1,0:T(8,128)(2,1)S(1)}, u32[]{:S(2)}, u32[]{:S(2)}) collective-permute-start(bf16[416,384]{1,0:T(8,128)(2,1)S(1)} %get-tuple-element.32.refs_0_), channel_id=1, source_target_pairs={{0,128},{64,192},{128,0},{192,64},{1,129},{65,193},{129,1},{193,65... | collective-permute-start | bytes 958472 | tf_op jit(solution)/shard_map/ppermute | solution.py:365
  46.3 1.1 %collective-permute-start.5 = (bf16[416,384]{1,0:T(8,128)(2,1)S(1)}, bf16[416,384]{1,0:T(8,128)(2,1)S(1)}, u32[]{:S(2)}, u32[]{:S(2)}) collective-permute-start(bf16[416,384]{1,0:T(8,128)(2,1)S(1)} %get-tuple-element.32.refs_0_), channel_id=1, source_target_pairs={{0,192},{64,0},{128,64},{192,128},{1,193},{65,1},{129,65},{193,129... | collective-permute-start | bytes 958472 | tf_op jit(solution)/shard_map/ppermute | solution.py:365
  47.4 0.0 copy-done.2
  47.4 6.2 %shard_map.106 = (bf16[400,256]{1,0:T(8,128)(2,1)S(1)}, bf16[400,128]{1,0:T(8,128)(2,1)S(1)}, bf16[400,128]{1,0:T(8,128)(2,1)S(1)}, bf16[400,128]{1,0:T(8,128)(2...) custom-call(bf16[448,384]{1,0:T(8,128)(2,1)S(1)} %get-tuple-element.27.active_ref, ...), custom_call_target="tpu_custom_call" | custom-call | flops 3500000000 | bytes 8750000 | tf_op jit(solution)/shard_map/pallas_call | solution.py:343
  53.6 0.5 collective-permute-start.6
  54.0 0.8 collective-permute-start.7
  54.9 0.0 collective-permute-done.3.refs_1_
  54.9 1.7 %collective-permute-start.8 = (bf16[400,128]{1,0:T(8,128)(2,1)S(1)}, bf16[400,128]{1,0:T(8,128)(2,1)S(1)}, u32[]{:S(2)}, u32[]{:S(2)}) collective-permute-start(bf16[400,128]{1,0:T(8,128)(2,1)S(1)} %get-tuple-element.36), channel_id=1, source_target_pairs={{0,192},{64,0},{128,64},{192,128},{1,193},{65,1},{129,65},{193,129... | collective-permute-start | bytes 307208 | tf_op jit(solution)/shard_map/ppermute | solution.py:365
  56.5 2.2 %shard_map.108.refs_4_ = f32[512,384]{1,0:T(8,128)S(1)} custom-call(bf16[416,384]{1,0:T(8,128)(2,1)S(1)} %get-tuple-element.37.grad_ref, f32[400,384]{1,0:T(8,128)S(1)} %get-tuple-element.38.mid_ref, bf16[1,3456,384]{2,1,0:T(8,128)(2,1)S(1)} %get-tuple-element.47.weight, bf16[512,400]{1,0:T(8,128)(2,1)S(1)} %get-tuple-element.39.chosen), custom_call_target="tpu_custom_call" | custom-call | flops 1200000000 | bytes 3000000 | tf_op jit(solution)/shard_map/pallas_call | solution.py:343
  58.8 1.1 %collective-permute-done.4.refs_2_ = bf16[416,384]{1,0:T(8,128)(2,1)S(1)} collective-permute-done((bf16[416,384]{1,0:T(8,128)(2,1)S(1)}, bf16[416,384]{1,0:T(8,128)(2,1)S(1)}, u32[]{:S(2)}, u32[]{:S(2)}) %collective-permute-start.4) | collective-permute-done | bytes 319520 | tf_op jit(solution)/shard_map/ppermute | solution.py:365
  59.9 0.5 collective-permute-done.5.refs_3_
  60.4 0.5 shard_map.107.turned
  60.9 3.6 %collective-permute-done.6.refs_1_ = bf16[400,128]{1,0:T(8,128)(2,1)S(1)} collective-permute-done((bf16[400,128]{1,0:T(8,128)(2,1)S(1)}, bf16[400,128]{1,0:T(8,128)(2,1)S(1)}, u32[]{:S(2)}, u32[]{:S(2)}) %collective-permute-start.6) | collective-permute-done | bytes 102432 | tf_op jit(solution)/shard_map/ppermute | solution.py:365
  64.4 0.0 collective-permute-done.7.refs_2_
  64.4 0.0 collective-permute-done.8.refs_3_
  64.4 0.0 copy-start
  64.4 0.0 copy-start.1
  64.4 3.4 %shard_map.109 = bf16[64,16,384]{2,1,0:T(8,128)(2,1)} custom-call(bf16[4,384,416]{2,1,0:T(8,128)(2,1)S(1)} %shard_map.107.turned, bf16[400,128]{1,0:T(8,128)(2,1)S(1)} %get-tuple-element.33.refs_0_, bf16[400,128]{1,0:T(8,128)(2,1)S(1)} %collective-permute-done.6.refs_1_, bf16[400,128]{1,0:T(8,128)(2,1)S(1)} %collective-permute-done.7.refs_2_, ...), custom_call_target="tpu_custom_call" | custom-call | flops 1500000000 | bytes 3750000 | tf_op jit(solution)/shard_map/pallas_call | solution.py:343
  67.9 7.3 %all-to-all-start.1 = ((bf16[64,16,384]{2,1,0:T(8,128)(2,1)}), bf16[64,16,384]{2,1,0:T(8,128)(2,1)S(1)}, u32[]{:S(2)}, u32[]{:S(2)}) async-start(bf16[64,16,384]{2,1,0:T(8,128)(2,1)} %shard_map.109), calls=%async_computation.1 | async-start | bytes 1572864 | tf_op jit(solution)/shard_map/all_to_all | solution.py:473
  75.2 0.7 constant_dynamic-slice_fusion
  75.9 22.2 %all-to-all-done.1.arrived = bf16[64,16,384]{2,1,0:T(8,128)(2,1)S(1)} async-done(((bf16[64,16,384]{2,1,0:T(8,128)(2,1)}), bf16[64,16,384]{2,1,0:T(8,128)(2,1)S(1)}, u32[]{:S(2)}, u32[]{:S(2)}) %all-to-all-start.1) | async-done | bytes 786464 | tf_op jit(solution)/shard_map/all_to_all | solution.py:473
  98.1 0.0 copy-done
  98.1 0.0 copy-done.1
  98.1 1.3 %shard_map.110 = (f32[40,768]{1,0:T(8,128)}, f32[2,54,384]{2,1,0:T(8,128)S(1)}) custom-call(bf16[64,16,384]{2,1,0:T(8,128)(2,1)S(1)} %all-to-all-done.1.arrived, f32[40,128]{1,0:T(8,128)S(1)} %copy-done.1, bf16[768,384]{1,0:T(8,128)(2,1)S(1)} %copy-done), custom_call_target="tpu_custom_call" | custom-call | flops 80000000 | bytes 200000 | tf_op jit(solution)/shard_map/pallas_call | solution.py:343
  99.4 0.8 copy.12
  (1 shorter events, 0.0 us)
Async XLA Ops:
  3.0 24.9 %all-to-all-start = ((bf16[64,8,256]{2,1,0:T(8,128)(2,1)}), bf16[64,8,256]{2,1,0:T(8,128)(2,1)S(1)}, u32[]{:S(2)}, u32[]{:S(2)}) async-start(bf16[64,8,256]{2,1,0:T(8,128)(2,1)} %bitcast.5), calls=%async_computation | async-start | bytes 524288 | tf_op jit(solution)/shard_map/all_to_all | solution.py:386
  17.9 1.6 %collective-permute-start = (bf16[200,384]{1,0:T(8,128)(2,1)S(1)}, bf16[200,384]{1,0:T(8,128)(2,1)S(1)}, u32[]{:S(2)}, u32[]{:S(2)}) collective-permute-start(bf16[200,384]{1,0:T(8,128)(2,1)S(1)} %reshape.15.own_aim), channel_id=1, source_target_pairs={{0,4},{4,0},{1,5},{5,1},{2,6},{6,2},{3,7},{7,3},{8,12},{12,8},{9,1... | collective-permute-start | bytes 460808 | tf_op jit(solution)/shard_map/ppermute | solution.py:365
  29.2 7.5 %collective-permute-start.1 = (bf16[48,384]{1,0:T(8,128)(2,1)S(1)}, bf16[48,384]{1,0:T(8,128)(2,1)S(1)}, u32[]{:S(2)}, u32[]{:S(2)}) collective-permute-start(bf16[48,384]{1,0:T(8,128)(2,1)S(1)} %get-tuple-element.24), channel_id=1, source_target_pairs={{0,8},{8,16},{16,24},{24,32},{32,40},{40,48},{48,56},{56,64},{64,7... | collective-permute-start | bytes 110600 | tf_op jit(solution)/shard_map/ppermute | solution.py:365
  32.3 4.7 %collective-permute-start.2 = (bf16[48,384]{1,0:T(8,128)(2,1)S(1)}, bf16[48,384]{1,0:T(8,128)(2,1)S(1)}, u32[]{:S(2)}, u32[]{:S(2)}) collective-permute-start(bf16[48,384]{1,0:T(8,128)(2,1)S(1)} %get-tuple-element.26), channel_id=1, source_target_pairs={{8,0},{16,8},{24,16},{32,24},{40,32},{48,40},{56,48},{64,56},{72,6... | collective-permute-start | bytes 110600 | tf_op jit(solution)/shard_map/ppermute | solution.py:365
  37.0 10.4 %copy-start.2 = (bf16[384,256]{1,0:T(8,128)(2,1)S(1)}, bf16[384,256]{1,0:T(8,128)(2,1)}, u32[]{:S(2)}) copy-start(bf16[384,256]{1,0:T(8,128)(2,1)} %head.1) | copy-start | bytes 589828
  39.9 15.0 %collective-permute-start.3 = (bf16[416,384]{1,0:T(8,128)(2,1)S(1)}, bf16[416,384]{1,0:T(8,128)(2,1)S(1)}, u32[]{:S(2)}, u32[]{:S(2)}) collective-permute-start(bf16[416,384]{1,0:T(8,128)(2,1)S(1)} %get-tuple-element.32.refs_0_), channel_id=1, source_target_pairs={{0,64},{64,128},{128,192},{192,0},{1,65},{65,129},{129,193},{193,1... | collective-permute-start | bytes 958472 | tf_op jit(solution)/shard_map/ppermute | solution.py:365
  43.7 16.2 %collective-permute-start.4 = (bf16[416,384]{1,0:T(8,128)(2,1)S(1)}, bf16[416,384]{1,0:T(8,128)(2,1)S(1)}, u32[]{:S(2)}, u32[]{:S(2)}) collective-permute-start(bf16[416,384]{1,0:T(8,128)(2,1)S(1)} %get-tuple-element.32.refs_0_), channel_id=1, source_target_pairs={{0,128},{64,192},{128,0},{192,64},{1,129},{65,193},{129,1},{193,65... | collective-permute-start | bytes 958472 | tf_op jit(solution)/shard_map/ppermute | solution.py:365
  46.3 14.1 %collective-permute-start.5 = (bf16[416,384]{1,0:T(8,128)(2,1)S(1)}, bf16[416,384]{1,0:T(8,128)(2,1)S(1)}, u32[]{:S(2)}, u32[]{:S(2)}) collective-permute-start(bf16[416,384]{1,0:T(8,128)(2,1)S(1)} %get-tuple-element.32.refs_0_), channel_id=1, source_target_pairs={{0,192},{64,0},{128,64},{192,128},{1,193},{65,1},{129,65},{193,129... | collective-permute-start | bytes 958472 | tf_op jit(solution)/shard_map/ppermute | solution.py:365
  53.6 10.8 %collective-permute-start.6 = (bf16[400,128]{1,0:T(8,128)(2,1)S(1)}, bf16[400,128]{1,0:T(8,128)(2,1)S(1)}, u32[]{:S(2)}, u32[]{:S(2)}) collective-permute-start(bf16[400,128]{1,0:T(8,128)(2,1)S(1)} %get-tuple-element.34), channel_id=1, source_target_pairs={{0,64},{64,128},{128,192},{192,0},{1,65},{65,129},{129,193},{193,1... | collective-permute-start | bytes 307208 | tf_op jit(solution)/shard_map/ppermute | solution.py:365
  54.0 10.4 %collective-permute-start.7 = (bf16[400,128]{1,0:T(8,128)(2,1)S(1)}, bf16[400,128]{1,0:T(8,128)(2,1)S(1)}, u32[]{:S(2)}, u32[]{:S(2)}) collective-permute-start(bf16[400,128]{1,0:T(8,128)(2,1)S(1)} %get-tuple-element.35), channel_id=1, source_target_pairs={{0,128},{64,192},{128,0},{192,64},{1,129},{65,193},{129,1},{193,65... | collective-permute-start | bytes 307208 | tf_op jit(solution)/shard_map/ppermute | solution.py:365
  54.9 9.6 %collective-permute-start.8 = (bf16[400,128]{1,0:T(8,128)(2,1)S(1)}, bf16[400,128]{1,0:T(8,128)(2,1)S(1)}, u32[]{:S(2)}, u32[]{:S(2)}) collective-permute-start(bf16[400,128]{1,0:T(8,128)(2,1)S(1)} %get-tuple-element.36), channel_id=1, source_target_pairs={{0,192},{64,0},{128,64},{192,128},{1,193},{65,1},{129,65},{193,129... | collective-permute-start | bytes 307208 | tf_op jit(solution)/shard_map/ppermute | solution.py:365
  64.4 33.7 %copy-start = (bf16[768,384]{1,0:T(8,128)(2,1)S(1)}, bf16[768,384]{1,0:T(8,128)(2,1)}, u32[]{:S(2)}) copy-start(bf16[768,384]{1,0:T(8,128)(2,1)} %in_weight.3) | copy-start | bytes 1769476
  64.4 33.7 %copy-start.1 = (f32[40,128]{1,0:T(8,128)S(1)}, f32[40,128]{1,0:T(8,128)}, u32[]{:S(2)}) copy-start(f32[40,128]{1,0:T(8,128)} %get-tuple-element.40.where_ref) | copy-start | bytes 61444
  67.9 30.3 %all-to-all-start.1 = ((bf16[64,16,384]{2,1,0:T(8,128)(2,1)}), bf16[64,16,384]{2,1,0:T(8,128)(2,1)S(1)}, u32[]{:S(2)}, u32[]{:S(2)}) async-start(bf16[64,16,384]{2,1,0:T(8,128)(2,1)} %shard_map.109), calls=%async_computation.1 | async-start | bytes 1572864 | tf_op jit(solution)/shard_map/all_to_all | solution.py:473

commit v5 on v4

--- a/solution.py
+++ b/solution.py
@@ -145,7 +145,9 @@
     return (row >= 0) & (row < lax.axis_size(TM) * ROWS)
 
 
-def pack_kernel(tokens, placement, in_weight, packed, where_out):
+def pack_kernel(tokens, placement, weight_ref, packed, where_out, in_weight, arrival):
+    load = pltpu.make_async_copy(weight_ref, in_weight, arrival)
+    load.start()
     count = tokens.shape[0]
     rows = placement[0:1, :].astype(F32)
     cols = placement[1:2, :].astype(F32)
@@ -163,6 +165,7 @@
     index = lax.broadcasted_iota(jnp.int32, (packed.shape[0], 1), 0)
     wanted = lax.shift_right_logical(index, 4) * 4 + (index & 3)
     match = jnp.where(wanted.astype(F32) == where_to, 1.0, 0.0).astype(BF16)
+    load.wait()
     proj = jnp.dot(tokens[...], in_weight[...], preferred_element_type=F32).astype(BF16)
     lane = lax.broadcasted_iota(jnp.int32, (count, 128), 1)
     notes = jnp.where(lane == 1, column(cols), jnp.where(lane == 2, 1.0, 0.0))
@@ -173,7 +176,20 @@
     packed[...] = jnp.where((index & 4) == 0, low, high).astype(BF16)
 
 
-def place_kernel(arrived, own_aim, other_aim, token, x_out, aim_out, down_out, up_out, chosen_out):
+def order_kernel(own_aim, other_aim, aim_out):
+    core = lax.axis_index("freq")
+    number = lax.broadcasted_iota(jnp.int32, (CELLS, 1), 0)
+    far = (lax.shift_right_logical(number, 2) & 1) != core
+    source = lax.shift_right_logical(number, 3) * 4 + (number & 3) + jnp.where(far, CELLS // 2, 0)
+    order = lax.broadcasted_iota(jnp.int32, (CELLS, CELLS), 1) == source
+    aim_out[...] = jnp.dot(
+        jnp.where(order, 1.0, 0.0).astype(BF16),
+        jnp.concatenate([own_aim[...].astype(F32), other_aim[...].astype(F32)], axis=0).astype(BF16),
+        preferred_element_type=F32,
+    ).astype(BF16)
+
+
+def place_kernel(arrived, aim, token, x_out, down_out, up_out, chosen_out):
     core = lax.axis_index("freq")
     slots = arrived.shape[0]
     notes = arrived[:, 128:256].astype(F32).reshape(slots // 8, 8, 128)
@@ -193,20 +209,13 @@
         )
 
     placed = jnp.concatenate([pick((index & 4) == 0), pick((index & 4) == 4)[:, 0:128]], axis=1)
-    number = lax.broadcasted_iota(jnp.int32, (CELLS, 1), 0)
-    far = (lax.shift_right_logical(number, 2) & 1) != core
-    source = lax.shift_right_logical(number, 3) * 4 + (number & 3) + jnp.where(far, CELLS // 2, 0)
-    order = lax.broadcasted_iota(jnp.int32, (CELLS, CELLS), 1) == source
-    aim = jnp.dot(
-        jnp.where(order, 1.0, 0.0).astype(BF16),
-        jnp.concatenate([own_aim[...].astype(F32), other_aim[...].astype(F32)], axis=0).astype(BF16),
-        preferred_element_type=F32,
-    )
-    x = jnp.where(aim[:, PIX : PIX + 1] == 1.0, token[...].astype(F32), placed)
-    x_out[...] = x.astype(BF16)
-    aim_out[...] = aim.astype(BF16)
-    down_out[...] = jnp.concatenate([x[CELLS - 32 :], aim[CELLS - 16 :]], axis=0).astype(BF16)
-    up_out[...] = jnp.concatenate([x[0:32], aim[0:16]], axis=0).astype(BF16)
+    masked = aim[:, PIX : PIX + 1] == 1.0
+    x = jnp.where(masked, token[...].astype(F32), placed).astype(BF16)
+    x_out[...] = x
+    down_out[0:32] = x[CELLS - 32 :]
+    down_out[32:48] = aim[CELLS - 16 :]
+    up_out[0:32] = x[0:32]
+    up_out[32:48] = aim[0:16]
     spread = jnp.broadcast_to(cell, (slots, 128)).reshape(slots // 8, 8, 128)
     first = jnp.sum(jnp.where(within == 4 + 2 * core, spread, 0.0), axis=1, keepdims=True)
     second = jnp.sum(jnp.where(within == 5 + 2 * core, spread, 0.0), axis=1, keepdims=True)
@@ -333,17 +342,18 @@
         for group in range(4):
             height = min(14, 54 - 14 * group)
             wide = joined([parts[peer][group] for peer in range(4)])
-            conv_out[layer, 14 * group : 14 * group + height] = wide[0:height]
+            conv_out[14 * group : 14 * group + height, layer] = wide[0:height]
 
 
 VMEM = pl.BlockSpec(memory_space=pltpu.VMEM)
-
-
-def call(kernel, shapes, scratch, cost, limit, *operands):
+ANY = pl.BlockSpec(memory_space=pl.ANY)
+
+
+def call(kernel, shapes, scratch, cost, limit, *operands, far=-1):
     return pl.pallas_call(
         kernel,
         out_shape=shapes,
-        in_specs=[VMEM] * len(operands),
+        in_specs=[ANY if i == far else VMEM for i in range(len(operands))],
         out_specs=jax.tree.map(lambda _: VMEM, shapes),
         scratch_shapes=scratch,
         compiler_params=pltpu.CompilerParams(vmem_limit_bytes=limit << 20),
@@ -376,25 +386,26 @@
     packed, where_to = call(
         pack_kernel,
         (shape((shards * 8, 256)), shape((visible, 128), F32)),
-        [],
+        [pltpu.VMEM(in_weight.shape, BF16), pltpu.SemaphoreType.DMA],
         80_000_000,
         62,
         tokens,
         placement,
         in_weight,
+        far=2,
     )
     arrived = lax.all_to_all(packed, TM_FREQ, split_axis=0, concat_axis=0, tiled=True)
     flags = jnp.broadcast_to((patch_mask == 1)[:, :, None], (*patch_mask.shape, 128))
     aim = jnp.concatenate([targets, flags.astype(BF16)], axis=2).reshape(-1, PIX + 128)
 
     other = send(aim, "freq", 1, True)
+    aim = call(order_kernel, shape((CELLS, PIX + 128)), [], 200_000_000, 8, aim, other)
     weights = [conv_weight[layer : layer + 1] for layer in range(2)]
 
-    own, aim, down, up, chosen = call(
+    own, down, up, chosen = call(
         place_kernel,
         (
             shape((CELLS, CHANNELS)),
-            shape((CELLS, PIX + 128)),
             shape((48, CHANNELS)),
             shape((48, CHANNELS)),
             shape((shards * 8, CELLS)),
@@ -404,7 +415,6 @@
         8,
         arrived,
         aim,
-        other,
         mask_token[None, :],
     )
     above = send(down, TM, 1, False)
@@ -473,7 +483,7 @@
     terms = lax.all_to_all(terms, TM_FREQ, split_axis=0, concat_axis=0, tiled=True)
     token_grad, conv_grad = call(
         finish_kernel,
-        (shape((visible, in_weight.shape[0]), F32), shape((2, 54, CHANNELS), F32)),
+        (shape((visible, in_weight.shape[0]), F32), shape((54, 2, CHANNELS), F32)),
         [],
         80_000_000,
         6,
@@ -481,6 +491,7 @@
         where_to,
         in_weight,
     )
+    conv_grad = conv_grad.transpose(1, 0, 2)
     pred = lax.dynamic_slice_in_dim(pred.reshape(ROWS, COLS, PIX), core * half, half, axis=1)
     return (pred, token_grad, conv_grad)
 

time: 101 us -> 100 us (0.990)
    pallas_call x8 -> x9, Pallas kernels: 20.1 us -> 21.1 us  [call(): pl.pallas_call(kernel, out_shape=shapes, in_specs=[ANY if i == far else V...]
where the time goes in v5:
time: 100 us
  waiting for transfers between devices  36.1 us (36%)
  starting transfers between devices  35.6 us (36%)
  Pallas kernels  21.1 us (21%)
  local copies, waits for them, and re-layouts  4.76 us (5%)
  other arithmetic  1.66 us (2%)
    all_to_all x1, waiting for transfers between devices, per_device(): lax.all_to_all(terms, TM_FREQ, split_axis=0, concat_axis=0, tiled=True)  22.2 us
    pallas_call x9, Pallas kernels, call(): pl.pallas_call(kernel, out_shape=shapes, in_specs=[ANY if i == far else V...  21.1 us
    ppermute x9, starting transfers between devices, send(): return lax.ppermute(value, axis, pairs)  15.3 us
    all_to_all x1, starting transfers between devices, per_device(): lax.all_to_all(packed, TM_FREQ, split_axis=0, concat_axis=0, tiled=True)  13 us
    all_to_all x1, waiting for transfers between devices, per_device(): lax.all_to_all(packed, TM_FREQ, split_axis=0, concat_axis=0, tiled=True)  8.07 us
    all_to_all x1, starting transfers between devices, per_device(): lax.all_to_all(terms, TM_FREQ, split_axis=0, concat_axis=0, tiled=True)  7.33 us
    ppermute x9, waiting for transfers between devices, send(): return lax.ppermute(value, axis, pairs)  5.81 us
    slice x1, local copies, waits for them, and re-layouts, per_device(): weights = [conv_weight[layer:layer + 1] for layer in range(2)]  3.09 us
  transfers between devices with their start and end apart: 11, of which 7 were waited for; matrix products, arithmetic and copies ran while one was open for 6% of the time, Pallas kernels for 9%

profile of v5, /device:TPU:1, one launch (start us, length us, event | category | flops | bytes accessed | tf_op | source)
XLA Modules:
  0.0 100.0 jit_solution(14393542136435732054)
XLA Ops:
  0.6 3.1 %shard_map.103 = (bf16[512,256]{1,0:T(8,128)(2,1)}, f32[40,128]{1,0:T(8,128)}) custom-call(bf16[40,768]{1,0:T(8,128)(2,1)} %tokens.1, s32[2,40]{1,0:T(2,128)} %placement.1, bf16[768,384]{1,0:T(8,128)(2,1)} %in_weight.1), custom_call_target="tpu_custom_call" | custom-call | flops 80000000 | bytes 200000 | tf_op jit(solution)/shard_map/pallas_call | solution.py:353
  3.8 13.0 %all-to-all-start = ((bf16[64,8,256]{2,1,0:T(8,128)(2,1)}), bf16[64,8,256]{2,1,0:T(8,128)(2,1)S(1)}, u32[]{:S(2)}, u32[]{:S(2)}) async-start(bf16[64,8,256]{2,1,0:T(8,128)(2,1)} %bitcast.6), calls=%async_computation | async-start | bytes 524288 | tf_op jit(solution)/shard_map/all_to_all | solution.py:397
  16.7 0.7 compare_convert_fusion
  17.4 0.1 copy.11
  17.6 0.1 broadcast_in_dim.4
  17.7 1.0 pad_maximum_fusion
  18.7 0.5 collective-permute-start
  19.2 0.7 broadcast_in_dim.10.token
  19.9 0.3 collective-permute-done.other_aim
  20.3 0.4 shard_map.104.aim.aim_ref
  20.6 8.1 %all-to-all-done = bf16[64,8,256]{2,1,0:T(8,128)(2,1)S(1)} async-done(((bf16[64,8,256]{2,1,0:T(8,128)(2,1)}), bf16[64,8,256]{2,1,0:T(8,128)(2,1)S(1)}, u32[]{:S(2)}, u32[]{:S(2)}) %all-to-all-start) | async-done | bytes 262176 | tf_op jit(solution)/shard_map/all_to_all | solution.py:397
  28.7 1.1 %shard_map.105 = (bf16[400,384]{1,0:T(8,128)(2,1)S(1)}, bf16[48,384]{1,0:T(8,128)(2,1)S(1)}, bf16[48,384]{1,0:T(8,128)(2,1)S(1)}, bf16[512,400]{1,0:T(8,128)(2,1)S(1)}) custom-call(bf16[512,256]{1,0:T(8,128)(2,1)S(1)} %bitcast.4, bf16[400,384]{1,0:T(8,128)(2,1)S(1)} %shard_map.104.aim.aim_ref, bf16[1,384]{1,0:T(2,128)(2,1)S(1)} %broadcast_in_dim.10.token), custom_call_target="tpu_custom_call" | custom-call | flops 300000000 | bytes 750000 | tf_op jit(solution)/shard_map/pallas_call | solution.py:353
  29.8 3.1 %collective-permute-start.1 = (bf16[48,384]{1,0:T(8,128)(2,1)S(1)}, bf16[48,384]{1,0:T(8,128)(2,1)S(1)}, u32[]{:S(2)}, u32[]{:S(2)}) collective-permute-start(bf16[48,384]{1,0:T(8,128)(2,1)S(1)} %get-tuple-element.23), channel_id=1, source_target_pairs={{0,8},{8,16},{16,24},{24,32},{32,40},{40,48},{48,56},{56,64},{64,7... | collective-permute-start | bytes 110600 | tf_op jit(solution)/shard_map/ppermute | solution.py:375
  32.9 1.3 %collective-permute-start.2 = (bf16[48,384]{1,0:T(8,128)(2,1)S(1)}, bf16[48,384]{1,0:T(8,128)(2,1)S(1)}, u32[]{:S(2)}, u32[]{:S(2)}) collective-permute-start(bf16[48,384]{1,0:T(8,128)(2,1)S(1)} %get-tuple-element.25), channel_id=1, source_target_pairs={{8,0},{16,8},{24,16},{32,24},{40,32},{48,40},{56,48},{64,56},{72,6... | collective-permute-start | bytes 110600 | tf_op jit(solution)/shard_map/ppermute | solution.py:375
  34.2 3.1 %fusion = (bf16[1,3456,384]{2,1,0:T(8,128)(2,1)S(1)}, bf16[1,3456,384]{2,1,0:T(8,128)(2,1)S(1)}) fusion(bf16[2,3456,384]{2,1,0:T(8,128)(2,1)} %param.14), kind=kLoop, calls=%fused_computation.3 | loop fusion | bytes 10616832 | tf_op jit(solution)/shard_map/slice | solution.py:403
  37.2 0.0 collective-permute-done.1.above
  37.3 0.3 collective-permute-done.2.below
  37.6 0.0 copy-start.2
  37.6 2.9 %shard_map.106 = (bf16[448,384]{1,0:T(8,128)(2,1)S(1)}, f32[416,384]{1,0:T(8,128)S(1)}, f32[416,128]{1,0:T(8,128)S(1)}, bf16[416,384]{1,0:T(8,128)(2,1)S(1)}) custom-call(bf16[48,384]{1,0:T(8,128)(2,1)S(1)} %collective-permute-done.1.above, bf16[400,384]{1,0:T(8,128)(2,1)S(1)} %get-tuple-element.24.own, bf16[48,384]{1,0:T(8,128)(2,1)S(1)} %collective-permute-done.2.below, ...), custom_call_target="tpu_custom_call" | custom-call | flops 1500000000 | bytes 3750000 | tf_op jit(solution)/shard_map/pallas_call | solution.py:353
  40.5 3.8 %collective-permute-start.3 = (bf16[416,384]{1,0:T(8,128)(2,1)S(1)}, bf16[416,384]{1,0:T(8,128)(2,1)S(1)}, u32[]{:S(2)}, u32[]{:S(2)}) collective-permute-start(bf16[416,384]{1,0:T(8,128)(2,1)S(1)} %get-tuple-element.30.refs_0_), channel_id=1, source_target_pairs={{0,64},{64,128},{128,192},{192,0},{1,65},{65,129},{129,193},{193,1... | collective-permute-start | bytes 958472 | tf_op jit(solution)/shard_map/ppermute | solution.py:375
  44.3 2.6 %collective-permute-start.4 = (bf16[416,384]{1,0:T(8,128)(2,1)S(1)}, bf16[416,384]{1,0:T(8,128)(2,1)S(1)}, u32[]{:S(2)}, u32[]{:S(2)}) collective-permute-start(bf16[416,384]{1,0:T(8,128)(2,1)S(1)} %get-tuple-element.30.refs_0_), channel_id=1, source_target_pairs={{0,128},{64,192},{128,0},{192,64},{1,129},{65,193},{129,1},{193,65... | collective-permute-start | bytes 958472 | tf_op jit(solution)/shard_map/ppermute | solution.py:375
  46.9 1.1 %collective-permute-start.5 = (bf16[416,384]{1,0:T(8,128)(2,1)S(1)}, bf16[416,384]{1,0:T(8,128)(2,1)S(1)}, u32[]{:S(2)}, u32[]{:S(2)}) collective-permute-start(bf16[416,384]{1,0:T(8,128)(2,1)S(1)} %get-tuple-element.30.refs_0_), channel_id=1, source_target_pairs={{0,192},{64,0},{128,64},{192,128},{1,193},{65,1},{129,65},{193,129... | collective-permute-start | bytes 958472 | tf_op jit(solution)/shard_map/ppermute | solution.py:375
  47.9 0.0 copy-done.2
  47.9 6.2 %shard_map.107 = (bf16[400,256]{1,0:T(8,128)(2,1)S(1)}, bf16[400,128]{1,0:T(8,128)(2,1)S(1)}, bf16[400,128]{1,0:T(8,128)(2,1)S(1)}, bf16[400,128]{1,0:T(8,128)(2...) custom-call(bf16[448,384]{1,0:T(8,128)(2,1)S(1)} %get-tuple-element.26.active_ref, ...), custom_call_target="tpu_custom_call" | custom-call | flops 3500000000 | bytes 8750000 | tf_op jit(solution)/shard_map/pallas_call | solution.py:353
  54.1 0.5 collective-permute-start.6
  54.6 0.8 collective-permute-start.7
  55.4 0.0 collective-permute-done.3.refs_1_
  55.4 1.7 %collective-permute-start.8 = (bf16[400,128]{1,0:T(8,128)(2,1)S(1)}, bf16[400,128]{1,0:T(8,128)(2,1)S(1)}, u32[]{:S(2)}, u32[]{:S(2)}) collective-permute-start(bf16[400,128]{1,0:T(8,128)(2,1)S(1)} %get-tuple-element.34), channel_id=1, source_target_pairs={{0,192},{64,0},{128,64},{192,128},{1,193},{65,1},{129,65},{193,129... | collective-permute-start | bytes 307208 | tf_op jit(solution)/shard_map/ppermute | solution.py:375
  57.1 2.2 %shard_map.109.refs_4_ = f32[512,384]{1,0:T(8,128)S(1)} custom-call(bf16[416,384]{1,0:T(8,128)(2,1)S(1)} %get-tuple-element.35.grad_ref, f32[400,384]{1,0:T(8,128)S(1)} %get-tuple-element.36.mid_ref, bf16[1,3456,384]{2,1,0:T(8,128)(2,1)S(1)} %get-tuple-element.42.weight, bf16[512,400]{1,0:T(8,128)(2,1)S(1)} %get-tuple-element.37.chosen), custom_call_target="tpu_custom_call" | custom-call | flops 1200000000 | bytes 3000000 | tf_op jit(solution)/shard_map/pallas_call | solution.py:353
  59.3 1.1 %collective-permute-done.4.refs_2_ = bf16[416,384]{1,0:T(8,128)(2,1)S(1)} collective-permute-done((bf16[416,384]{1,0:T(8,128)(2,1)S(1)}, bf16[416,384]{1,0:T(8,128)(2,1)S(1)}, u32[]{:S(2)}, u32[]{:S(2)}) %collective-permute-start.4) | collective-permute-done | bytes 319520 | tf_op jit(solution)/shard_map/ppermute | solution.py:375
  60.4 0.5 collective-permute-done.5.refs_3_
  60.9 0.5 shard_map.108.turned
  61.4 3.6 %collective-permute-done.6.refs_1_ = bf16[400,128]{1,0:T(8,128)(2,1)S(1)} collective-permute-done((bf16[400,128]{1,0:T(8,128)(2,1)S(1)}, bf16[400,128]{1,0:T(8,128)(2,1)S(1)}, u32[]{:S(2)}, u32[]{:S(2)}) %collective-permute-start.6) | collective-permute-done | bytes 102432 | tf_op jit(solution)/shard_map/ppermute | solution.py:375
  65.0 0.0 collective-permute-done.7.refs_2_
  65.0 0.0 collective-permute-done.8.refs_3_
  65.0 0.0 copy-start
  65.0 0.0 copy-start.1
  65.0 3.4 %shard_map.110 = bf16[64,16,384]{2,1,0:T(8,128)(2,1)} custom-call(bf16[4,384,416]{2,1,0:T(8,128)(2,1)S(1)} %shard_map.108.turned, bf16[400,128]{1,0:T(8,128)(2,1)S(1)} %get-tuple-element.31.refs_0_, bf16[400,128]{1,0:T(8,128)(2,1)S(1)} %collective-permute-done.6.refs_1_, bf16[400,128]{1,0:T(8,128)(2,1)S(1)} %collective-permute-done.7.refs_2_, ...), custom_call_target="tpu_custom_call" | custom-call | flops 1500000000 | bytes 3750000 | tf_op jit(solution)/shard_map/pallas_call | solution.py:353
  68.4 7.3 %all-to-all-start.1 = ((bf16[64,16,384]{2,1,0:T(8,128)(2,1)}), bf16[64,16,384]{2,1,0:T(8,128)(2,1)S(1)}, u32[]{:S(2)}, u32[]{:S(2)}) async-start(bf16[64,16,384]{2,1,0:T(8,128)(2,1)} %shard_map.110), calls=%async_computation.1 | async-start | bytes 1572864 | tf_op jit(solution)/shard_map/all_to_all | solution.py:483
  75.8 0.7 constant_dynamic-slice_fusion
  76.5 22.2 %all-to-all-done.1.arrived = bf16[64,16,384]{2,1,0:T(8,128)(2,1)S(1)} async-done(((bf16[64,16,384]{2,1,0:T(8,128)(2,1)}), bf16[64,16,384]{2,1,0:T(8,128)(2,1)S(1)}, u32[]{:S(2)}, u32[]{:S(2)}) %all-to-all-start.1) | async-done | bytes 786464 | tf_op jit(solution)/shard_map/all_to_all | solution.py:483
  98.7 0.0 copy-done
  98.7 0.0 copy-done.1
  98.7 1.3 %shard_map.111 = (f32[40,768]{1,0:T(8,128)}, f32[54,2,384]{2,1,0:T(2,128)}) custom-call(bf16[64,16,384]{2,1,0:T(8,128)(2,1)S(1)} %all-to-all-done.1.arrived, f32[40,128]{1,0:T(8,128)S(1)} %copy-done.1, bf16[768,384]{1,0:T(8,128)(2,1)S(1)} %copy-done), custom_call_target="tpu_custom_call" | custom-call | flops 80000000 | bytes 200000 | tf_op jit(solution)/shard_map/pallas_call | solution.py:353
  (1 shorter events, 0.0 us)
Async XLA Ops:
  3.8 25.0 %all-to-all-start = ((bf16[64,8,256]{2,1,0:T(8,128)(2,1)}), bf16[64,8,256]{2,1,0:T(8,128)(2,1)S(1)}, u32[]{:S(2)}, u32[]{:S(2)}) async-start(bf16[64,8,256]{2,1,0:T(8,128)(2,1)} %bitcast.6), calls=%async_computation | async-start | bytes 524288 | tf_op jit(solution)/shard_map/all_to_all | solution.py:397
  18.7 1.6 %collective-permute-start = (bf16[200,384]{1,0:T(8,128)(2,1)S(1)}, bf16[200,384]{1,0:T(8,128)(2,1)S(1)}, u32[]{:S(2)}, u32[]{:S(2)}) collective-permute-start(bf16[200,384]{1,0:T(8,128)(2,1)S(1)} %reshape.15.own_aim), channel_id=1, source_target_pairs={{0,4},{4,0},{1,5},{5,1},{2,6},{6,2},{3,7},{7,3},{8,12},{12,8},{9,1... | collective-permute-start | bytes 460808 | tf_op jit(solution)/shard_map/ppermute | solution.py:375
  29.8 7.5 %collective-permute-start.1 = (bf16[48,384]{1,0:T(8,128)(2,1)S(1)}, bf16[48,384]{1,0:T(8,128)(2,1)S(1)}, u32[]{:S(2)}, u32[]{:S(2)}) collective-permute-start(bf16[48,384]{1,0:T(8,128)(2,1)S(1)} %get-tuple-element.23), channel_id=1, source_target_pairs={{0,8},{8,16},{16,24},{24,32},{32,40},{40,48},{48,56},{56,64},{64,7... | collective-permute-start | bytes 110600 | tf_op jit(solution)/shard_map/ppermute | solution.py:375
  32.9 4.7 %collective-permute-start.2 = (bf16[48,384]{1,0:T(8,128)(2,1)S(1)}, bf16[48,384]{1,0:T(8,128)(2,1)S(1)}, u32[]{:S(2)}, u32[]{:S(2)}) collective-permute-start(bf16[48,384]{1,0:T(8,128)(2,1)S(1)} %get-tuple-element.25), channel_id=1, source_target_pairs={{8,0},{16,8},{24,16},{32,24},{40,32},{48,40},{56,48},{64,56},{72,6... | collective-permute-start | bytes 110600 | tf_op jit(solution)/shard_map/ppermute | solution.py:375
  37.6 10.4 %copy-start.2 = (bf16[384,256]{1,0:T(8,128)(2,1)S(1)}, bf16[384,256]{1,0:T(8,128)(2,1)}, u32[]{:S(2)}) copy-start(bf16[384,256]{1,0:T(8,128)(2,1)} %head.1) | copy-start | bytes 589828
  40.5 14.9 %collective-permute-start.3 = (bf16[416,384]{1,0:T(8,128)(2,1)S(1)}, bf16[416,384]{1,0:T(8,128)(2,1)S(1)}, u32[]{:S(2)}, u32[]{:S(2)}) collective-permute-start(bf16[416,384]{1,0:T(8,128)(2,1)S(1)} %get-tuple-element.30.refs_0_), channel_id=1, source_target_pairs={{0,64},{64,128},{128,192},{192,0},{1,65},{65,129},{129,193},{193,1... | collective-permute-start | bytes 958472 | tf_op jit(solution)/shard_map/ppermute | solution.py:375
  44.3 16.2 %collective-permute-start.4 = (bf16[416,384]{1,0:T(8,128)(2,1)S(1)}, bf16[416,384]{1,0:T(8,128)(2,1)S(1)}, u32[]{:S(2)}, u32[]{:S(2)}) collective-permute-start(bf16[416,384]{1,0:T(8,128)(2,1)S(1)} %get-tuple-element.30.refs_0_), channel_id=1, source_target_pairs={{0,128},{64,192},{128,0},{192,64},{1,129},{65,193},{129,1},{193,65... | collective-permute-start | bytes 958472 | tf_op jit(solution)/shard_map/ppermute | solution.py:375
  46.9 14.1 %collective-permute-start.5 = (bf16[416,384]{1,0:T(8,128)(2,1)S(1)}, bf16[416,384]{1,0:T(8,128)(2,1)S(1)}, u32[]{:S(2)}, u32[]{:S(2)}) collective-permute-start(bf16[416,384]{1,0:T(8,128)(2,1)S(1)} %get-tuple-element.30.refs_0_), channel_id=1, source_target_pairs={{0,192},{64,0},{128,64},{192,128},{1,193},{65,1},{129,65},{193,129... | collective-permute-start | bytes 958472 | tf_op jit(solution)/shard_map/ppermute | solution.py:375
  54.1 10.8 %collective-permute-start.6 = (bf16[400,128]{1,0:T(8,128)(2,1)S(1)}, bf16[400,128]{1,0:T(8,128)(2,1)S(1)}, u32[]{:S(2)}, u32[]{:S(2)}) collective-permute-start(bf16[400,128]{1,0:T(8,128)(2,1)S(1)} %get-tuple-element.32), channel_id=1, source_target_pairs={{0,64},{64,128},{128,192},{192,0},{1,65},{65,129},{129,193},{193,1... | collective-permute-start | bytes 307208 | tf_op jit(solution)/shard_map/ppermute | solution.py:375
  54.6 10.4 %collective-permute-start.7 = (bf16[400,128]{1,0:T(8,128)(2,1)S(1)}, bf16[400,128]{1,0:T(8,128)(2,1)S(1)}, u32[]{:S(2)}, u32[]{:S(2)}) collective-permute-start(bf16[400,128]{1,0:T(8,128)(2,1)S(1)} %get-tuple-element.33), channel_id=1, source_target_pairs={{0,128},{64,192},{128,0},{192,64},{1,129},{65,193},{129,1},{193,65... | collective-permute-start | bytes 307208 | tf_op jit(solution)/shard_map/ppermute | solution.py:375
  55.4 9.6 %collective-permute-start.8 = (bf16[400,128]{1,0:T(8,128)(2,1)S(1)}, bf16[400,128]{1,0:T(8,128)(2,1)S(1)}, u32[]{:S(2)}, u32[]{:S(2)}) collective-permute-start(bf16[400,128]{1,0:T(8,128)(2,1)S(1)} %get-tuple-element.34), channel_id=1, source_target_pairs={{0,192},{64,0},{128,64},{192,128},{1,193},{65,1},{129,65},{193,129... | collective-permute-start | bytes 307208 | tf_op jit(solution)/shard_map/ppermute | solution.py:375
  65.0 33.7 %copy-start = (bf16[768,384]{1,0:T(8,128)(2,1)S(1)}, bf16[768,384]{1,0:T(8,128)(2,1)}, u32[]{:S(2)}) copy-start(bf16[768,384]{1,0:T(8,128)(2,1)} %in_weight.1) | copy-start | bytes 1769476
  65.0 33.7 %copy-start.1 = (f32[40,128]{1,0:T(8,128)S(1)}, f32[40,128]{1,0:T(8,128)}, u32[]{:S(2)}) copy-start(f32[40,128]{1,0:T(8,128)} %get-tuple-element.38.where_ref) | copy-start | bytes 61444
  68.4 30.3 %all-to-all-start.1 = ((bf16[64,16,384]{2,1,0:T(8,128)(2,1)}), bf16[64,16,384]{2,1,0:T(8,128)(2,1)S(1)}, u32[]{:S(2)}, u32[]{:S(2)}) async-start(bf16[64,16,384]{2,1,0:T(8,128)(2,1)} %shard_map.110), calls=%async_computation.1 | async-start | bytes 1572864 | tf_op jit(solution)/shard_map/all_to_all | solution.py:483

commit v6 on v5

--- a/solution.py
+++ b/solution.py
@@ -74,9 +74,9 @@
         odd[0 : cells - 8, lanes] = shifted[8:].astype(BF16)
 
 
-def conv_taps(even, odd, taps, cells):
+def conv_taps(windows, taps):
     summed = None
-    for part, window in enumerate((even[0:cells], odd[0:cells], even[16 : 16 + cells])):
+    for part, window in enumerate(windows):
         term = jnp.dot(
             window, taps[0, part * DEPTH : (part + 1) * DEPTH], preferred_element_type=F32
         )
@@ -139,15 +139,16 @@
     return scale * (grad - mean - unit * along)
 
 
-def rows_valid(cells, before):
-    row = lax.shift_right_logical(lax.broadcasted_iota(jnp.int32, (cells, 1), 0), 3)
-    row = row + lax.axis_index(TM) * ROWS - before
+def rows_valid(row):
+    row = row + lax.axis_index(TM) * ROWS
     return (row >= 0) & (row < lax.axis_size(TM) * ROWS)
 
 
-def pack_kernel(tokens, placement, weight_ref, packed, where_out, in_weight, arrival):
-    load = pltpu.make_async_copy(weight_ref, in_weight, arrival)
-    load.start()
+def row_number(cells):
+    return lax.shift_right_logical(lax.broadcasted_iota(jnp.int32, (cells, 1), 0), 3)
+
+
+def pack_kernel(tokens, placement, in_weight, packed, where_out):
     count = tokens.shape[0]
     rows = placement[0:1, :].astype(F32)
     cols = placement[1:2, :].astype(F32)
@@ -165,7 +166,6 @@
     index = lax.broadcasted_iota(jnp.int32, (packed.shape[0], 1), 0)
     wanted = lax.shift_right_logical(index, 4) * 4 + (index & 3)
     match = jnp.where(wanted.astype(F32) == where_to, 1.0, 0.0).astype(BF16)
-    load.wait()
     proj = jnp.dot(tokens[...], in_weight[...], preferred_element_type=F32).astype(BF16)
     lane = lax.broadcasted_iota(jnp.int32, (count, 128), 1)
     notes = jnp.where(lane == 1, column(cols), jnp.where(lane == 2, 1.0, 0.0))
@@ -224,22 +224,47 @@
     chosen_out[...] = jnp.where(lane == spread[:, 0:1].astype(jnp.int32), 1.0, 0.0).astype(BF16)
 
 
+def inside_kernel(own, weight, active_out, unit_out, scale_out, even, odd):
+    source = own[...].astype(F32)
+    store_columns(source, even, odd)
+    unit, scale = normed(conv_taps((even[0:384], odd[0:384], even[16:400]), weight))
+    unit_out[...] = unit
+    scale_out[...] = jnp.broadcast_to(scale, scale_out.shape)
+    active_out[...] = (source[8:392] + unit * half_erf(unit)).astype(BF16)
+
+
 def first_kernel(
-    above, own, below, weight, active_out, unit_out, scale_out, share_out, even, odd
+    above, own, below, weight, active_in, unit_in, scale_in,
+    active_out, unit_out, scale_out, share_out, even, odd,
 ):
-    source = jnp.concatenate(
-        [above[0:32].astype(F32), own[...].astype(F32), below[0:32].astype(F32)], axis=0
-    )
-    store_columns(source, even, odd)
-    unit, scale = normed(conv_taps(even, odd, weight, 448))
-    unit_out[...] = unit[16:432]
-    scale_out[...] = jnp.broadcast_to(scale[16:432], (416, 128))
-    active = source[8:456] + unit * half_erf(unit)
-    active = jnp.where(rows_valid(448, 3), active, 0.0)
-    active_out[...] = active.astype(BF16)
-    share_out[...] = jnp.where(
-        lax.axis_index("freq") == 1, active[16:432], source[24:440]
-    ).astype(BF16)
+    upper, lower = above[0:32].astype(F32), below[0:32].astype(F32)
+    border = jnp.concatenate(
+        [upper, own[0:16].astype(F32), own[384:400].astype(F32), lower], axis=0
+    )
+    store_columns(border, even, odd)
+    windows = (
+        jnp.concatenate([even[0:32], even[48:80]], axis=0),
+        jnp.concatenate([odd[0:32], odd[48:80]], axis=0),
+        jnp.concatenate([even[16:48], even[64:96]], axis=0),
+    )
+    unit, scale = normed(conv_taps(windows, weight))
+    edge = jnp.concatenate([border[8:40], border[56:88]], axis=0) + unit * half_erf(unit)
+    number = row_number(64)
+    number = jnp.where(number < 4, number - 3, number + 45)
+    edge = jnp.where(rows_valid(number), edge, 0.0)
+    active_out[0:32] = edge[0:32].astype(BF16)
+    active_out[32:416] = active_in[...]
+    active_out[416:448] = edge[32:64].astype(BF16)
+    unit_out[0:16] = unit[16:32]
+    unit_out[16:400] = unit_in[...]
+    unit_out[400:416] = unit[32:48]
+    scale = jnp.broadcast_to(scale, (64, 128))
+    scale_out[0:16] = scale[16:32]
+    scale_out[16:400] = scale_in[...]
+    scale_out[400:416] = scale[32:48]
+    source = jnp.concatenate([upper[24:32], own[...].astype(F32), lower[0:8]], axis=0)
+    active = jnp.concatenate([edge[16:32], active_in[...].astype(F32), edge[32:48]], axis=0)
+    share_out[...] = jnp.where(lax.axis_index("freq") == 1, active, source).astype(BF16)
 
 
 def second_kernel(
@@ -248,7 +273,7 @@
 ):
     active = active_ref[...].astype(F32)
     store_columns(active, even, odd)
-    unit, scale = normed(conv_taps(even, odd, weight, 432))
+    unit, scale = normed(conv_taps((even[0:432], odd[0:432], even[16:448]), weight))
     top = (active[8:440] + unit * half_erf(unit)).astype(BF16)
     guess = jnp.dot(top, head[...], preferred_element_type=F32)
     pred[...] = guess[16:416].astype(BF16)
@@ -262,7 +287,7 @@
     grad_two = pull_back(unit, scale, grad_top).astype(BF16)
     grad_mid = grad_top[8:424] + conv_back(grad_two, weight, 416)
     grad_one = pull_back(unit_ref[...], scale_ref[:, 0:1], grad_mid)
-    grad_one = jnp.where(rows_valid(416, 1), grad_one, 0.0)
+    grad_one = jnp.where(rows_valid(row_number(416) - 1), grad_one, 0.0)
     grad_out[...] = grad_one.astype(BF16)
     mid_out[...] = grad_mid[8:408]
     share = jnp.where(lax.axis_index("freq") == 1, grad_two.astype(F32)[16:416], grad_one[8:408])
@@ -346,14 +371,13 @@
 
 
 VMEM = pl.BlockSpec(memory_space=pltpu.VMEM)
-ANY = pl.BlockSpec(memory_space=pl.ANY)
-
-
-def call(kernel, shapes, scratch, cost, limit, *operands, far=-1):
+
+
+def call(kernel, shapes, scratch, cost, limit, *operands):
     return pl.pallas_call(
         kernel,
         out_shape=shapes,
-        in_specs=[ANY if i == far else VMEM for i in range(len(operands))],
+        in_specs=[VMEM] * len(operands),
         out_specs=jax.tree.map(lambda _: VMEM, shapes),
         scratch_shapes=scratch,
         compiler_params=pltpu.CompilerParams(vmem_limit_bytes=limit << 20),
@@ -386,13 +410,12 @@
     packed, where_to = call(
         pack_kernel,
         (shape((shards * 8, 256)), shape((visible, 128), F32)),
-        [pltpu.VMEM(in_weight.shape, BF16), pltpu.SemaphoreType.DMA],
+        [],
         80_000_000,
         62,
         tokens,
         placement,
         in_weight,
-        far=2,
     )
     arrived = lax.all_to_all(packed, TM_FREQ, split_axis=0, concat_axis=0, tiled=True)
     flags = jnp.broadcast_to((patch_mask == 1)[:, :, None], (*patch_mask.shape, 128))
@@ -417,9 +440,18 @@
         aim,
         mask_token[None, :],
     )
+    columns = [pltpu.VMEM((464, DEPTH), BF16), pltpu.VMEM((464, DEPTH), BF16)]
     above = send(down, TM, 1, False)
     below = send(up, TM, -1, False)
-    columns = [pltpu.VMEM((464, DEPTH), BF16), pltpu.VMEM((464, DEPTH), BF16)]
+    inside = call(
+        inside_kernel,
+        (shape((384, CHANNELS)), shape((384, CHANNELS), F32), shape((384, 128), F32)),
+        columns,
+        1_200_000_000,
+        12,
+        own,
+        weights[0],
+    )
     active, unit, scale, inner = call(
         first_kernel,
         (
@@ -435,6 +467,7 @@
         own,
         below,
         weights[0],
+        *inside,
     )
     inners = [inner] + [send(inner, "tm_0", step, True) for step in (1, 2, 3)]
     pred, *outers, mid, grad = call(

time: 100 us -> 99.7 us (level)
    all_to_all x1, starting transfers between devices: 13 us -> 9.89 us  [per_device(): lax.all_to_all(packed, TM_FREQ, split_axis=0, concat_axis=0, tiled=True)]
    ppermute x9, starting transfers between devices: 15.3 us -> 17.4 us  [send(): return lax.ppermute(value, axis, pairs)]
    slice x1, local copies, waits for them, and re-layouts: 3.09 us -> 4.59 us  [per_device(): weights = [conv_weight[layer:layer + 1] for layer in range(2)]]
    all_to_all x1, waiting for transfers between devices: 8.07 us -> 6.96 us  [per_device(): lax.all_to_all(packed, TM_FREQ, split_axis=0, concat_axis=0, tiled=True)]
    pallas_call x9 -> x10, Pallas kernels: 21.1 us -> 20.8 us  [call(): pl.pallas_call(kernel, out_shape=shapes, in_specs=[VMEM] * len(operands),...]
  transfers between devices with their start and end apart: 11 -> 11, of which waited for: 7 -> 6; matrix products, arithmetic and copies ran while one was open for 6% -> 5% of each run, Pallas kernels for 9% -> 14%
where the time goes in v6:
time: 99.7 us; the launch traced here: 99.4 us
  starting transfers between devices  35.3 us (35%)
  waiting for transfers between devices  35.3 us (35%)
  Pallas kernels  20.8 us (21%)
  local copies, waits for them, and re-layouts  5.6 us (6%)
  other arithmetic  1.66 us (2%)
    all_to_all x1, waiting for transfers between devices, per_device(): lax.all_to_all(terms, TM_FREQ, split_axis=0, concat_axis=0, tiled=True)  22.2 us
    pallas_call x10, Pallas kernels, call(): pl.pallas_call(kernel, out_shape=shapes, in_specs=[VMEM] * len(operands),...  20.8 us
    ppermute x9, starting transfers between devices, send(): return lax.ppermute(value, axis, pairs)  17.4 us
    all_to_all x1, starting transfers between devices, per_device(): lax.all_to_all(packed, TM_FREQ, split_axis=0, concat_axis=0, tiled=True)  9.89 us
    all_to_all x1, starting transfers between devices, per_device(): lax.all_to_all(terms, TM_FREQ, split_axis=0, concat_axis=0, tiled=True)  8 us
    all_to_all x1, waiting for transfers between devices, per_device(): lax.all_to_all(packed, TM_FREQ, split_axis=0, concat_axis=0, tiled=True)  6.96 us
    ppermute x9, waiting for transfers between devices, send(): return lax.ppermute(value, axis, pairs)  6.12 us
    slice x1, local copies, waits for them, and re-layouts, per_device(): weights = [conv_weight[layer:layer + 1] for layer in range(2)]  4.59 us
  transfers between devices with their start and end apart: 11, of which 6 were waited for; matrix products, arithmetic and copies ran while one was open for 5% of the time, Pallas kernels for 14%

profile of v6, /device:TPU:1, one launch (start us, length us, event | category | flops | bytes accessed | tf_op | source)
XLA Modules:
  0.0 99.4 jit_solution(15306414484713596558)
XLA Ops:
  0.6 0.7 compare_convert_fusion
  1.3 0.1 copy.11
  1.4 0.1 broadcast_in_dim.4
  1.6 1.0 pad_maximum_fusion
  2.6 3.3 %collective-permute-start = (bf16[200,384]{1,0:T(8,128)(2,1)S(1)}, bf16[200,384]{1,0:T(8,128)(2,1)S(1)}, u32[]{:S(2)}, u32[]{:S(2)}) collective-permute-start(bf16[200,384]{1,0:T(8,128)(2,1)S(1)} %reshape.15.own_aim), channel_id=1, source_target_pairs={{0,4},{4,0},{1,5},{5,1},{2,6},{6,2},{3,7},{7,3},{8,12},{12,8},{9,1... | collective-permute-start | bytes 460808 | tf_op jit(solution)/shard_map/ppermute | solution.py:399
  5.9 2.3 %shard_map.103 = (bf16[512,256]{1,0:T(8,128)(2,1)}, f32[40,128]{1,0:T(8,128)}) custom-call(bf16[40,768]{1,0:T(8,128)(2,1)} %tokens.1, s32[2,40]{1,0:T(2,128)} %placement.1, bf16[768,384]{1,0:T(8,128)(2,1)} %in_weight.3), custom_call_target="tpu_custom_call" | custom-call | flops 80000000 | bytes 200000 | tf_op jit(solution)/shard_map/pallas_call | solution.py:377
  8.2 9.9 %all-to-all-start = ((bf16[64,8,256]{2,1,0:T(8,128)(2,1)}), bf16[64,8,256]{2,1,0:T(8,128)(2,1)S(1)}, u32[]{:S(2)}, u32[]{:S(2)}) async-start(bf16[64,8,256]{2,1,0:T(8,128)(2,1)} %bitcast.6), calls=%async_computation | async-start | bytes 524288 | tf_op jit(solution)/shard_map/all_to_all | solution.py:420
  18.1 0.0 copy-start.4
  18.1 4.6 %fusion = (bf16[1,3456,384]{2,1,0:T(8,128)(2,1)}, bf16[1,3456,384]{2,1,0:T(8,128)(2,1)S(1)}) fusion(bf16[2,3456,384]{2,1,0:T(8,128)(2,1)} %param.14), kind=kLoop, calls=%fused_computation.3 | loop fusion | bytes 10616832 | tf_op jit(solution)/shard_map/slice | solution.py:426
  22.7 0.0 copy-done.4
  22.7 0.0 collective-permute-done.other_aim
  22.7 0.4 shard_map.104.aim.aim_ref
  23.1 7.0 %all-to-all-done = bf16[64,8,256]{2,1,0:T(8,128)(2,1)S(1)} async-done(((bf16[64,8,256]{2,1,0:T(8,128)(2,1)}), bf16[64,8,256]{2,1,0:T(8,128)(2,1)S(1)}, u32[]{:S(2)}, u32[]{:S(2)}) %all-to-all-start) | async-done | bytes 262176 | tf_op jit(solution)/shard_map/all_to_all | solution.py:420
  30.1 1.1 %shard_map.105 = (bf16[400,384]{1,0:T(8,128)(2,1)S(1)}, bf16[48,384]{1,0:T(8,128)(2,1)S(1)}, bf16[48,384]{1,0:T(8,128)(2,1)S(1)}, bf16[512,400]{1,0:T(8,128)(2,1)S(1)}) custom-call(bf16[512,256]{1,0:T(8,128)(2,1)S(1)} %bitcast.4, bf16[400,384]{1,0:T(8,128)(2,1)S(1)} %shard_map.104.aim.aim_ref, bf16[1,384]{1,0:T(2,128)(2,1)S(1)} %broadcast_in_dim.10.token), custom_call_target="tpu_custom_call" | custom-call | flops 300000000 | bytes 750000 | tf_op jit(solution)/shard_map/pallas_call | solution.py:377
  31.1 3.1 %collective-permute-start.1 = (bf16[48,384]{1,0:T(8,128)(2,1)S(1)}, bf16[48,384]{1,0:T(8,128)(2,1)S(1)}, u32[]{:S(2)}, u32[]{:S(2)}) collective-permute-start(bf16[48,384]{1,0:T(8,128)(2,1)S(1)} %get-tuple-element.26), channel_id=1, source_target_pairs={{0,8},{8,16},{16,24},{24,32},{32,40},{40,48},{48,56},{56,64},{64,7... | collective-permute-start | bytes 110600 | tf_op jit(solution)/shard_map/ppermute | solution.py:399
  34.2 1.3 %collective-permute-start.2 = (bf16[48,384]{1,0:T(8,128)(2,1)S(1)}, bf16[48,384]{1,0:T(8,128)(2,1)S(1)}, u32[]{:S(2)}, u32[]{:S(2)}) collective-permute-start(bf16[48,384]{1,0:T(8,128)(2,1)S(1)} %get-tuple-element.28), channel_id=1, source_target_pairs={{8,0},{16,8},{24,16},{32,24},{40,32},{48,40},{56,48},{64,56},{72,6... | collective-permute-start | bytes 110600 | tf_op jit(solution)/shard_map/ppermute | solution.py:399
  35.5 2.4 %shard_map.106 = (bf16[384,384]{1,0:T(8,128)(2,1)S(1)}, f32[384,384]{1,0:T(8,128)S(1)}, f32[384,128]{1,0:T(8,128)S(1)}) custom-call(bf16[400,384]{1,0:T(8,128)(2,1)S(1)} %get-tuple-element.27.own, bf16[1,3456,384]{2,1,0:T(8,128)(2,1)S(1)} %get-tuple-element.48.weight), custom_call_target="tpu_custom_call" | custom-call | flops 1200000000 | bytes 3000000 | tf_op jit(solution)/shard_map/pallas_call | solution.py:377
  37.9 0.0 collective-permute-done.1.above
  37.9 1.0 collective-permute-done.2.below
  38.9 0.0 copy-start
  38.9 0.0 copy-start.3
  38.9 0.9 shard_map.107
  39.8 3.1 %collective-permute-start.3 = (bf16[416,384]{1,0:T(8,128)(2,1)S(1)}, bf16[416,384]{1,0:T(8,128)(2,1)S(1)}, u32[]{:S(2)}, u32[]{:S(2)}) collective-permute-start(bf16[416,384]{1,0:T(8,128)(2,1)S(1)} %get-tuple-element.36.refs_0_), channel_id=1, source_target_pairs={{0,64},{64,128},{128,192},{192,0},{1,65},{65,129},{129,193},{193,1... | collective-permute-start | bytes 958472 | tf_op jit(solution)/shard_map/ppermute | solution.py:399
  42.9 2.6 %collective-permute-start.4 = (bf16[416,384]{1,0:T(8,128)(2,1)S(1)}, bf16[416,384]{1,0:T(8,128)(2,1)S(1)}, u32[]{:S(2)}, u32[]{:S(2)}) collective-permute-start(bf16[416,384]{1,0:T(8,128)(2,1)S(1)} %get-tuple-element.36.refs_0_), channel_id=1, source_target_pairs={{0,128},{64,192},{128,0},{192,64},{1,129},{65,193},{129,1},{193,65... | collective-permute-start | bytes 958472 | tf_op jit(solution)/shard_map/ppermute | solution.py:399
  45.6 1.1 %collective-permute-start.5 = (bf16[416,384]{1,0:T(8,128)(2,1)S(1)}, bf16[416,384]{1,0:T(8,128)(2,1)S(1)}, u32[]{:S(2)}, u32[]{:S(2)}) collective-permute-start(bf16[416,384]{1,0:T(8,128)(2,1)S(1)} %get-tuple-element.36.refs_0_), channel_id=1, source_target_pairs={{0,192},{64,0},{128,64},{192,128},{1,193},{65,1},{129,65},{193,129... | collective-permute-start | bytes 958472 | tf_op jit(solution)/shard_map/ppermute | solution.py:399
  46.6 0.0 copy-done
  46.6 0.0 copy-done.3
  46.6 6.2 %shard_map.108 = (bf16[400,256]{1,0:T(8,128)(2,1)S(1)}, bf16[400,128]{1,0:T(8,128)(2,1)S(1)}, bf16[400,128]{1,0:T(8,128)(2,1)S(1)}, bf16[400,128]{1,0:T(8,128)(2...) custom-call(bf16[448,384]{1,0:T(8,128)(2,1)S(1)} %get-tuple-element.32.active_ref, ...), custom_call_target="tpu_custom_call" | custom-call | flops 3500000000 | bytes 8750000 | tf_op jit(solution)/shard_map/pallas_call | solution.py:377
  52.9 0.5 collective-permute-start.6
  53.3 0.8 collective-permute-start.7
  54.2 0.0 collective-permute-done.3.refs_1_
  54.2 1.7 %collective-permute-start.8 = (bf16[400,128]{1,0:T(8,128)(2,1)S(1)}, bf16[400,128]{1,0:T(8,128)(2,1)S(1)}, u32[]{:S(2)}, u32[]{:S(2)}) collective-permute-start(bf16[400,128]{1,0:T(8,128)(2,1)S(1)} %get-tuple-element.40), channel_id=1, source_target_pairs={{0,192},{64,0},{128,64},{192,128},{1,193},{65,1},{129,65},{193,129... | collective-permute-start | bytes 307208 | tf_op jit(solution)/shard_map/ppermute | solution.py:399
  55.8 2.2 %shard_map.110.refs_4_ = f32[512,384]{1,0:T(8,128)S(1)} custom-call(bf16[416,384]{1,0:T(8,128)(2,1)S(1)} %get-tuple-element.41.grad_ref, f32[400,384]{1,0:T(8,128)S(1)} %get-tuple-element.42.mid_ref, bf16[1,3456,384]{2,1,0:T(8,128)(2,1)S(1)} %get-tuple-element.48.weight, bf16[512,400]{1,0:T(8,128)(2,1)S(1)} %get-tuple-element.43.chosen), custom_call_target="tpu_custom_call" | custom-call | flops 1200000000 | bytes 3000000 | tf_op jit(solution)/shard_map/pallas_call | solution.py:377
  58.1 1.1 %collective-permute-done.4.refs_2_ = bf16[416,384]{1,0:T(8,128)(2,1)S(1)} collective-permute-done((bf16[416,384]{1,0:T(8,128)(2,1)S(1)}, bf16[416,384]{1,0:T(8,128)(2,1)S(1)}, u32[]{:S(2)}, u32[]{:S(2)}) %collective-permute-start.4) | collective-permute-done | bytes 319520 | tf_op jit(solution)/shard_map/ppermute | solution.py:399
  59.1 0.5 collective-permute-done.5.refs_3_
  59.6 0.5 shard_map.109.turned
  60.1 3.6 %collective-permute-done.6.refs_1_ = bf16[400,128]{1,0:T(8,128)(2,1)S(1)} collective-permute-done((bf16[400,128]{1,0:T(8,128)(2,1)S(1)}, bf16[400,128]{1,0:T(8,128)(2,1)S(1)}, u32[]{:S(2)}, u32[]{:S(2)}) %collective-permute-start.6) | collective-permute-done | bytes 102432 | tf_op jit(solution)/shard_map/ppermute | solution.py:399
  63.7 0.0 collective-permute-done.7.refs_2_
  63.7 0.0 collective-permute-done.8.refs_3_
  63.7 0.0 copy-start.1
  63.7 0.0 copy-start.2
  63.7 3.5 %shard_map.111 = bf16[64,16,384]{2,1,0:T(8,128)(2,1)} custom-call(bf16[4,384,416]{2,1,0:T(8,128)(2,1)S(1)} %shard_map.109.turned, bf16[400,128]{1,0:T(8,128)(2,1)S(1)} %get-tuple-element.37.refs_0_, bf16[400,128]{1,0:T(8,128)(2,1)S(1)} %collective-permute-done.6.refs_1_, bf16[400,128]{1,0:T(8,128)(2,1)S(1)} %collective-permute-done.7.refs_2_, ...), custom_call_target="tpu_custom_call" | custom-call | flops 1500000000 | bytes 3750000 | tf_op jit(solution)/shard_map/pallas_call | solution.py:377
  67.2 8.0 %all-to-all-start.1 = ((bf16[64,16,384]{2,1,0:T(8,128)(2,1)}), bf16[64,16,384]{2,1,0:T(8,128)(2,1)S(1)}, u32[]{:S(2)}, u32[]{:S(2)}) async-start(bf16[64,16,384]{2,1,0:T(8,128)(2,1)} %shard_map.111), calls=%async_computation.1 | async-start | bytes 1572864 | tf_op jit(solution)/shard_map/all_to_all | solution.py:516
  75.2 0.7 constant_dynamic-slice_fusion
  75.9 22.2 %all-to-all-done.1.arrived = bf16[64,16,384]{2,1,0:T(8,128)(2,1)S(1)} async-done(((bf16[64,16,384]{2,1,0:T(8,128)(2,1)}), bf16[64,16,384]{2,1,0:T(8,128)(2,1)S(1)}, u32[]{:S(2)}, u32[]{:S(2)}) %all-to-all-start.1) | async-done | bytes 786464 | tf_op jit(solution)/shard_map/all_to_all | solution.py:516
  98.1 0.0 copy-done.1
  98.1 0.0 copy-done.2
  98.1 1.2 %shard_map.112 = (f32[40,768]{1,0:T(8,128)}, f32[54,2,384]{2,1,0:T(2,128)}) custom-call(bf16[64,16,384]{2,1,0:T(8,128)(2,1)S(1)} %all-to-all-done.1.arrived, f32[40,128]{1,0:T(8,128)S(1)} %copy-done.2, bf16[768,384]{1,0:T(8,128)(2,1)S(1)} %copy-done.1), custom_call_target="tpu_custom_call" | custom-call | flops 80000000 | bytes 200000 | tf_op jit(solution)/shard_map/pallas_call | solution.py:377
  (2 shorter events, 0.0 us)
Async XLA Ops:
  2.6 20.1 %collective-permute-start = (bf16[200,384]{1,0:T(8,128)(2,1)S(1)}, bf16[200,384]{1,0:T(8,128)(2,1)S(1)}, u32[]{:S(2)}, u32[]{:S(2)}) collective-permute-start(bf16[200,384]{1,0:T(8,128)(2,1)S(1)} %reshape.15.own_aim), channel_id=1, source_target_pairs={{0,4},{4,0},{1,5},{5,1},{2,6},{6,2},{3,7},{7,3},{8,12},{12,8},{9,1... | collective-permute-start | bytes 460808 | tf_op jit(solution)/shard_map/ppermute | solution.py:399
  8.2 21.9 %all-to-all-start = ((bf16[64,8,256]{2,1,0:T(8,128)(2,1)}), bf16[64,8,256]{2,1,0:T(8,128)(2,1)S(1)}, u32[]{:S(2)}, u32[]{:S(2)}) async-start(bf16[64,8,256]{2,1,0:T(8,128)(2,1)} %bitcast.6), calls=%async_computation | async-start | bytes 524288 | tf_op jit(solution)/shard_map/all_to_all | solution.py:420
  18.1 4.6 %copy-start.4 = (bf16[384]{0:T(512)(128)(2,1)S(1)}, bf16[384]{0:T(512)(128)(2,1)}, u32[]{:S(2)}) copy-start(bf16[384]{0:T(512)(128)(2,1)} %param.13) | copy-start | bytes 2308
  31.1 6.8 %collective-permute-start.1 = (bf16[48,384]{1,0:T(8,128)(2,1)S(1)}, bf16[48,384]{1,0:T(8,128)(2,1)S(1)}, u32[]{:S(2)}, u32[]{:S(2)}) collective-permute-start(bf16[48,384]{1,0:T(8,128)(2,1)S(1)} %get-tuple-element.26), channel_id=1, source_target_pairs={{0,8},{8,16},{16,24},{24,32},{32,40},{40,48},{48,56},{56,64},{64,7... | collective-permute-start | bytes 110600 | tf_op jit(solution)/shard_map/ppermute | solution.py:399
  34.2 4.7 %collective-permute-start.2 = (bf16[48,384]{1,0:T(8,128)(2,1)S(1)}, bf16[48,384]{1,0:T(8,128)(2,1)S(1)}, u32[]{:S(2)}, u32[]{:S(2)}) collective-permute-start(bf16[48,384]{1,0:T(8,128)(2,1)S(1)} %get-tuple-element.28), channel_id=1, source_target_pairs={{8,0},{16,8},{24,16},{32,24},{40,32},{48,40},{56,48},{64,56},{72,6... | collective-permute-start | bytes 110600 | tf_op jit(solution)/shard_map/ppermute | solution.py:399
  38.9 7.7 %copy-start = (bf16[1,3456,384]{2,1,0:T(8,128)(2,1)S(1)}, bf16[1,3456,384]{2,1,0:T(8,128)(2,1)}, u32[]{:S(2)}) copy-start(bf16[1,3456,384]{2,1,0:T(8,128)(2,1)} %get-tuple-element.47.weight) | copy-start | bytes 7962628
  38.9 7.7 %copy-start.3 = (bf16[384,256]{1,0:T(8,128)(2,1)S(1)}, bf16[384,256]{1,0:T(8,128)(2,1)}, u32[]{:S(2)}) copy-start(bf16[384,256]{1,0:T(8,128)(2,1)} %head.1) | copy-start | bytes 589828
  39.8 14.3 %collective-permute-start.3 = (bf16[416,384]{1,0:T(8,128)(2,1)S(1)}, bf16[416,384]{1,0:T(8,128)(2,1)S(1)}, u32[]{:S(2)}, u32[]{:S(2)}) collective-permute-start(bf16[416,384]{1,0:T(8,128)(2,1)S(1)} %get-tuple-element.36.refs_0_), channel_id=1, source_target_pairs={{0,64},{64,128},{128,192},{192,0},{1,65},{65,129},{129,193},{193,1... | collective-permute-start | bytes 958472 | tf_op jit(solution)/shard_map/ppermute | solution.py:399
  42.9 16.2 %collective-permute-start.4 = (bf16[416,384]{1,0:T(8,128)(2,1)S(1)}, bf16[416,384]{1,0:T(8,128)(2,1)S(1)}, u32[]{:S(2)}, u32[]{:S(2)}) collective-permute-start(bf16[416,384]{1,0:T(8,128)(2,1)S(1)} %get-tuple-element.36.refs_0_), channel_id=1, source_target_pairs={{0,128},{64,192},{128,0},{192,64},{1,129},{65,193},{129,1},{193,65... | collective-permute-start | bytes 958472 | tf_op jit(solution)/shard_map/ppermute | solution.py:399
  45.6 14.1 %collective-permute-start.5 = (bf16[416,384]{1,0:T(8,128)(2,1)S(1)}, bf16[416,384]{1,0:T(8,128)(2,1)S(1)}, u32[]{:S(2)}, u32[]{:S(2)}) collective-permute-start(bf16[416,384]{1,0:T(8,128)(2,1)S(1)} %get-tuple-element.36.refs_0_), channel_id=1, source_target_pairs={{0,192},{64,0},{128,64},{192,128},{1,193},{65,1},{129,65},{193,129... | collective-permute-start | bytes 958472 | tf_op jit(solution)/shard_map/ppermute | solution.py:399
  52.9 10.8 %collective-permute-start.6 = (bf16[400,128]{1,0:T(8,128)(2,1)S(1)}, bf16[400,128]{1,0:T(8,128)(2,1)S(1)}, u32[]{:S(2)}, u32[]{:S(2)}) collective-permute-start(bf16[400,128]{1,0:T(8,128)(2,1)S(1)} %get-tuple-element.38), channel_id=1, source_target_pairs={{0,64},{64,128},{128,192},{192,0},{1,65},{65,129},{129,193},{193,1... | collective-permute-start | bytes 307208 | tf_op jit(solution)/shard_map/ppermute | solution.py:399
  53.3 10.3 %collective-permute-start.7 = (bf16[400,128]{1,0:T(8,128)(2,1)S(1)}, bf16[400,128]{1,0:T(8,128)(2,1)S(1)}, u32[]{:S(2)}, u32[]{:S(2)}) collective-permute-start(bf16[400,128]{1,0:T(8,128)(2,1)S(1)} %get-tuple-element.39), channel_id=1, source_target_pairs={{0,128},{64,192},{128,0},{192,64},{1,129},{65,193},{129,1},{193,65... | collective-permute-start | bytes 307208 | tf_op jit(solution)/shard_map/ppermute | solution.py:399
  54.2 9.5 %collective-permute-start.8 = (bf16[400,128]{1,0:T(8,128)(2,1)S(1)}, bf16[400,128]{1,0:T(8,128)(2,1)S(1)}, u32[]{:S(2)}, u32[]{:S(2)}) collective-permute-start(bf16[400,128]{1,0:T(8,128)(2,1)S(1)} %get-tuple-element.40), channel_id=1, source_target_pairs={{0,192},{64,0},{128,64},{192,128},{1,193},{65,1},{129,65},{193,129... | collective-permute-start | bytes 307208 | tf_op jit(solution)/shard_map/ppermute | solution.py:399
  63.7 34.4 %copy-start.1 = (bf16[768,384]{1,0:T(8,128)(2,1)S(1)}, bf16[768,384]{1,0:T(8,128)(2,1)}, u32[]{:S(2)}) copy-start(bf16[768,384]{1,0:T(8,128)(2,1)} %in_weight.3) | copy-start | bytes 1769476
  63.7 34.4 %copy-start.2 = (f32[40,128]{1,0:T(8,128)S(1)}, f32[40,128]{1,0:T(8,128)}, u32[]{:S(2)}) copy-start(f32[40,128]{1,0:T(8,128)} %get-tuple-element.44.where_ref) | copy-start | bytes 61444
  67.2 30.9 %all-to-all-start.1 = ((bf16[64,16,384]{2,1,0:T(8,128)(2,1)}), bf16[64,16,384]{2,1,0:T(8,128)(2,1)S(1)}, u32[]{:S(2)}, u32[]{:S(2)}) async-start(bf16[64,16,384]{2,1,0:T(8,128)(2,1)} %shard_map.111), calls=%async_computation.1 | async-start | bytes 1572864 | tf_op jit(solution)/shard_map/all_to_all | solution.py:516

commit v7 on v6

--- a/solution.py
+++ b/solution.py
@@ -224,13 +224,15 @@
     chosen_out[...] = jnp.where(lane == spread[:, 0:1].astype(jnp.int32), 1.0, 0.0).astype(BF16)
 
 
-def inside_kernel(own, weight, active_out, unit_out, scale_out, even, odd):
+def inside_kernel(own, weight, active_out, unit_out, scale_out, share_out, even, odd):
     source = own[...].astype(F32)
     store_columns(source, even, odd)
     unit, scale = normed(conv_taps((even[0:384], odd[0:384], even[16:400]), weight))
     unit_out[...] = unit
     scale_out[...] = jnp.broadcast_to(scale, scale_out.shape)
-    active_out[...] = (source[8:392] + unit * half_erf(unit)).astype(BF16)
+    active = source[8:392] + unit * half_erf(unit)
+    active_out[...] = active.astype(BF16)
+    share_out[...] = jnp.where(lax.axis_index("freq") == 1, active, source[8:392]).astype(BF16)
 
 
 def first_kernel(
@@ -262,13 +264,14 @@
     scale_out[0:16] = scale[16:32]
     scale_out[16:400] = scale_in[...]
     scale_out[400:416] = scale[32:48]
-    source = jnp.concatenate([upper[24:32], own[...].astype(F32), lower[0:8]], axis=0)
-    active = jnp.concatenate([edge[16:32], active_in[...].astype(F32), edge[32:48]], axis=0)
-    share_out[...] = jnp.where(lax.axis_index("freq") == 1, active, source).astype(BF16)
+    source = jnp.concatenate(
+        [upper[24:32], own[0:8].astype(F32), own[392:400].astype(F32), lower[0:8]], axis=0
+    )
+    share_out[...] = jnp.where(lax.axis_index("freq") == 1, edge[16:48], source).astype(BF16)
 
 
 def second_kernel(
-    active_ref, unit_ref, scale_ref, weight, head, above, aim_ref, below,
+    active_ref, unit_ref, scale_ref, border, weight, head, above, aim_ref, below,
     pred, share_own, share_one, share_two, share_three, mid_out, grad_out, even, odd,
 ):
     active = active_ref[...].astype(F32)
@@ -297,7 +300,11 @@
         quarter = (lax.axis_index("tm_0") + step) & 3
         piece = jnp.where(quarter == 0, pieces[0], pieces[1])
         piece = jnp.where(quarter >= 2, jnp.where(quarter == 2, pieces[2], pieces[3]), piece)
-        share_out[...] = jnp.where(lane < 96, piece, 0.0).astype(BF16)
+        share_out[0:CELLS] = jnp.where(lane < 96, piece, 0.0).astype(BF16)
+        for part in range(3):
+            share_out[CELLS + 32 * part : CELLS + 32 * (part + 1)] = border[
+                :, 128 * part : 128 * (part + 1)
+            ]
 
 
 def tail_kernel(grad_ref, mid_ref, weight, chosen, out):
@@ -315,7 +322,7 @@
     out, moved, total = refs[5:]
     summed = None
     for part in range(4):
-        low, middle, high = column_shifted(outers[part][...].astype(F32))
+        low, middle, high = column_shifted(outers[part][0:CELLS].astype(F32))
         for row_off in range(3):
             for col_off, piece in enumerate((high, middle, low)):
                 rows = [piece]
@@ -323,11 +330,17 @@
                     rows.insert(0, jnp.zeros((8 * row_off, 128), F32))
                 if row_off < 2:
                     rows.append(jnp.zeros((16 - 8 * row_off, 128), F32))
+                rows = jnp.concatenate(rows, axis=0).astype(BF16)
                 tap = 3 * row_off + col_off
-                moved[part, :, tap * 128 : (tap + 1) * 128] = jnp.concatenate(
-                    rows, axis=0
-                ).astype(BF16)
-        term = jnp.dot(turned[part], moved[part], preferred_element_type=F32)
+                lanes = slice(tap * 128, (tap + 1) * 128)
+                moved[part, 0:384, lanes] = rows[16:400]
+                moved[part, 384:400, lanes] = rows[0:16]
+                moved[part, 400:416, lanes] = rows[400:416]
+        border = jnp.concatenate(
+            [outers[part][CELLS + 32 * k : CELLS + 32 * (k + 1)] for k in range(3)], axis=1
+        )
+        inner = jnp.concatenate([turned[part], border.astype(F32).T.astype(BF16)], axis=1)
+        term = jnp.dot(inner, moved[part], preferred_element_type=F32)
         summed = term if summed is None else summed + term
     for tap in range(9):
         total[tap * CHANNELS : (tap + 1) * CHANNELS] = summed[:, tap * 128 : (tap + 1) * 128]
@@ -441,27 +454,34 @@
         mask_token[None, :],
     )
     columns = [pltpu.VMEM((464, DEPTH), BF16), pltpu.VMEM((464, DEPTH), BF16)]
+    columns = [pltpu.VMEM((464, DEPTH), BF16), pltpu.VMEM((464, DEPTH), BF16)]
     above = send(down, TM, 1, False)
     below = send(up, TM, -1, False)
-    inside = call(
+    *inside, inner = call(
         inside_kernel,
-        (shape((384, CHANNELS)), shape((384, CHANNELS), F32), shape((384, 128), F32)),
+        (
+            shape((384, CHANNELS)),
+            shape((384, CHANNELS), F32),
+            shape((384, 128), F32),
+            shape((384, CHANNELS)),
+        ),
         columns,
         1_200_000_000,
         12,
         own,
         weights[0],
     )
-    active, unit, scale, inner = call(
+    inners = [inner] + [send(inner, "tm_0", step, True) for step in (1, 2, 3)]
+    active, unit, scale, border = call(
         first_kernel,
         (
             shape((448, CHANNELS)),
             shape((416, CHANNELS), F32),
             shape((416, 128), F32),
-            shape((416, CHANNELS)),
+            shape((32, CHANNELS)),
         ),
         columns,
-        1_500_000_000,
+        500_000_000,
         12,
         above,
         own,
@@ -469,12 +489,11 @@
         weights[0],
         *inside,
     )
-    inners = [inner] + [send(inner, "tm_0", step, True) for step in (1, 2, 3)]
     pred, *outers, mid, grad = call(
         second_kernel,
         (
             shape((CELLS, PIX)),
-            *[shape((CELLS, 128))] * 4,
+            *[shape((CELLS + 96, 128))] * 4,
             shape((CELLS, CHANNELS), F32),
             shape((416, CHANNELS)),
         ),
@@ -484,6 +503,7 @@
         active,
         unit,
         scale,
+        border,
         weights[1],
         head_weight,
         above,
@@ -502,7 +522,7 @@
         weights[0],
         chosen,
     )
-    turned = call(turn_kernel, shape((4, CHANNELS, 416)), [], 400_000_000, 8, *inners)
+    turned = call(turn_kernel, shape((4, CHANNELS, 384)), [], 400_000_000, 8, *inners)
     terms = call(
         weight_kernel,
         shape((shards, 16, CHANNELS)),

time: 99.7 us -> 97.9 us (0.982)
  waiting for transfers between devices: 35.3 us -> 33 us
    ppermute x9, waiting for transfers between devices: 6.12 us -> 3.84 us  [send(): return lax.ppermute(value, axis, pairs)]
  transfers between devices with their start and end apart: 11 -> 11, of which waited for: 6 -> 4; matrix products, arithmetic and copies ran while one was open for 5% -> 5% of each run, Pallas kernels for 14% -> 15%
where the time goes in v7:
time: 97.9 us; the launch traced here: 97.6 us
  starting transfers between devices  35.9 us (37%)
  waiting for transfers between devices  33 us (34%)
  Pallas kernels  20.6 us (21%)
  local copies, waits for them, and re-layouts  5.6 us (6%)
  other arithmetic  1.66 us (2%)
    all_to_all x1, waiting for transfers between devices, per_device(): lax.all_to_all(terms, TM_FREQ, split_axis=0, concat_axis=0, tiled=True)  22.2 us
    pallas_call x10, Pallas kernels, call(): pl.pallas_call(kernel, out_shape=shapes, in_specs=[VMEM] * len(operands),...  20.6 us
    ppermute x9, starting transfers between devices, send(): return lax.ppermute(value, axis, pairs)  18.3 us
    all_to_all x1, starting transfers between devices, per_device(): lax.all_to_all(packed, TM_FREQ, split_axis=0, concat_axis=0, tiled=True)  9.89 us
    all_to_all x1, starting transfers between devices, per_device(): lax.all_to_all(terms, TM_FREQ, split_axis=0, concat_axis=0, tiled=True)  7.64 us
    all_to_all x1, waiting for transfers between devices, per_device(): lax.all_to_all(packed, TM_FREQ, split_axis=0, concat_axis=0, tiled=True)  6.96 us
    slice x1, local copies, waits for them, and re-layouts, per_device(): weights = [conv_weight[layer:layer + 1] for layer in range(2)]  4.59 us
    ppermute x9, waiting for transfers between devices, send(): return lax.ppermute(value, axis, pairs)  3.84 us
  transfers between devices with their start and end apart: 11, of which 4 were waited for; matrix products, arithmetic and copies ran while one was open for 5% of the time, Pallas kernels for 15%

profile of v7, /device:TPU:1, one launch (start us, length us, event | category | flops | bytes accessed | tf_op | source)
XLA Modules:
  0.0 97.6 jit_solution(12629624007023618665)
XLA Ops:
  0.6 0.7 compare_convert_fusion
  1.3 0.1 copy.11
  1.4 0.1 broadcast_in_dim.4
  1.6 1.0 pad_maximum_fusion
  2.6 3.3 %collective-permute-start = (bf16[200,384]{1,0:T(8,128)(2,1)S(1)}, bf16[200,384]{1,0:T(8,128)(2,1)S(1)}, u32[]{:S(2)}, u32[]{:S(2)}) collective-permute-start(bf16[200,384]{1,0:T(8,128)(2,1)S(1)} %reshape.15.own_aim), channel_id=1, source_target_pairs={{0,4},{4,0},{1,5},{5,1},{2,6},{6,2},{3,7},{7,3},{8,12},{12,8},{9,1... | collective-permute-start | bytes 460808 | tf_op jit(solution)/shard_map/ppermute | solution.py:412
  5.9 2.3 %shard_map.103 = (bf16[512,256]{1,0:T(8,128)(2,1)}, f32[40,128]{1,0:T(8,128)}) custom-call(bf16[40,768]{1,0:T(8,128)(2,1)} %tokens.1, s32[2,40]{1,0:T(2,128)} %placement.1, bf16[768,384]{1,0:T(8,128)(2,1)} %in_weight.3), custom_call_target="tpu_custom_call" | custom-call | flops 80000000 | bytes 200000 | tf_op jit(solution)/shard_map/pallas_call | solution.py:390
  8.2 9.9 %all-to-all-start = ((bf16[64,8,256]{2,1,0:T(8,128)(2,1)}), bf16[64,8,256]{2,1,0:T(8,128)(2,1)S(1)}, u32[]{:S(2)}, u32[]{:S(2)}) async-start(bf16[64,8,256]{2,1,0:T(8,128)(2,1)} %bitcast.6), calls=%async_computation | async-start | bytes 524288 | tf_op jit(solution)/shard_map/all_to_all | solution.py:433
  18.1 0.0 copy-start.4
  18.1 4.6 %fusion = (bf16[1,3456,384]{2,1,0:T(8,128)(2,1)}, bf16[1,3456,384]{2,1,0:T(8,128)(2,1)S(1)}) fusion(bf16[2,3456,384]{2,1,0:T(8,128)(2,1)} %param.14), kind=kLoop, calls=%fused_computation.3 | loop fusion | bytes 10616832 | tf_op jit(solution)/shard_map/slice | solution.py:439
  22.7 0.0 copy-done.4
  22.7 0.0 collective-permute-done.other_aim
  22.7 0.4 shard_map.104.aim.aim_ref
  23.1 7.0 %all-to-all-done = bf16[64,8,256]{2,1,0:T(8,128)(2,1)S(1)} async-done(((bf16[64,8,256]{2,1,0:T(8,128)(2,1)}), bf16[64,8,256]{2,1,0:T(8,128)(2,1)S(1)}, u32[]{:S(2)}, u32[]{:S(2)}) %all-to-all-start) | async-done | bytes 262176 | tf_op jit(solution)/shard_map/all_to_all | solution.py:433
  30.1 1.1 %shard_map.105 = (bf16[400,384]{1,0:T(8,128)(2,1)S(1)}, bf16[48,384]{1,0:T(8,128)(2,1)S(1)}, bf16[48,384]{1,0:T(8,128)(2,1)S(1)}, bf16[512,400]{1,0:T(8,128)(2,1)S(1)}) custom-call(bf16[512,256]{1,0:T(8,128)(2,1)S(1)} %bitcast.4, bf16[400,384]{1,0:T(8,128)(2,1)S(1)} %shard_map.104.aim.aim_ref, bf16[1,384]{1,0:T(2,128)(2,1)S(1)} %broadcast_in_dim.10.token), custom_call_target="tpu_custom_call" | custom-call | flops 300000000 | bytes 750000 | tf_op jit(solution)/shard_map/pallas_call | solution.py:390
  31.1 3.1 %collective-permute-start.1 = (bf16[48,384]{1,0:T(8,128)(2,1)S(1)}, bf16[48,384]{1,0:T(8,128)(2,1)S(1)}, u32[]{:S(2)}, u32[]{:S(2)}) collective-permute-start(bf16[48,384]{1,0:T(8,128)(2,1)S(1)} %get-tuple-element.27), channel_id=1, source_target_pairs={{0,8},{8,16},{16,24},{24,32},{32,40},{40,48},{48,56},{56,64},{64,7... | collective-permute-start | bytes 110600 | tf_op jit(solution)/shard_map/ppermute | solution.py:412
  34.2 1.3 %collective-permute-start.2 = (bf16[48,384]{1,0:T(8,128)(2,1)S(1)}, bf16[48,384]{1,0:T(8,128)(2,1)S(1)}, u32[]{:S(2)}, u32[]{:S(2)}) collective-permute-start(bf16[48,384]{1,0:T(8,128)(2,1)S(1)} %get-tuple-element.29), channel_id=1, source_target_pairs={{8,0},{16,8},{24,16},{32,24},{40,32},{48,40},{56,48},{64,56},{72,6... | collective-permute-start | bytes 110600 | tf_op jit(solution)/shard_map/ppermute | solution.py:412
  35.5 2.5 %shard_map.106 = (bf16[384,384]{1,0:T(8,128)(2,1)S(1)}, f32[384,384]{1,0:T(8,128)S(1)}, f32[384,128]{1,0:T(8,128)S(1)}, bf16[384,384]{1,0:T(8,128)(2,1)S(1)}) custom-call(bf16[400,384]{1,0:T(8,128)(2,1)S(1)} %get-tuple-element.28.own, bf16[1,3456,384]{2,1,0:T(8,128)(2,1)S(1)} %get-tuple-element.50.weight), custom_call_target="tpu_custom_call" | custom-call | flops 1200000000 | bytes 3000000 | tf_op jit(solution)/shard_map/pallas_call | solution.py:390
  38.0 0.0 copy-start
  38.0 0.0 copy-start.3
  38.0 4.1 %collective-permute-start.3 = (bf16[384,384]{1,0:T(8,128)(2,1)S(1)}, bf16[384,384]{1,0:T(8,128)(2,1)S(1)}, u32[]{:S(2)}, u32[]{:S(2)}) collective-permute-start(bf16[384,384]{1,0:T(8,128)(2,1)S(1)} %get-tuple-element.38.refs_0_), channel_id=1, source_target_pairs={{0,64},{64,128},{128,192},{192,0},{1,65},{65,129},{129,193},{193,1... | collective-permute-start | bytes 884744 | tf_op jit(solution)/shard_map/ppermute | solution.py:412
  42.0 2.6 %collective-permute-start.4 = (bf16[384,384]{1,0:T(8,128)(2,1)S(1)}, bf16[384,384]{1,0:T(8,128)(2,1)S(1)}, u32[]{:S(2)}, u32[]{:S(2)}) collective-permute-start(bf16[384,384]{1,0:T(8,128)(2,1)S(1)} %get-tuple-element.38.refs_0_), channel_id=1, source_target_pairs={{0,128},{64,192},{128,0},{192,64},{1,129},{65,193},{129,1},{193,65... | collective-permute-start | bytes 884744 | tf_op jit(solution)/shard_map/ppermute | solution.py:412
  44.6 1.1 %collective-permute-start.5 = (bf16[384,384]{1,0:T(8,128)(2,1)S(1)}, bf16[384,384]{1,0:T(8,128)(2,1)S(1)}, u32[]{:S(2)}, u32[]{:S(2)}) collective-permute-start(bf16[384,384]{1,0:T(8,128)(2,1)S(1)} %get-tuple-element.38.refs_0_), channel_id=1, source_target_pairs={{0,192},{64,0},{128,64},{192,128},{1,193},{65,1},{129,65},{193,129... | collective-permute-start | bytes 884744 | tf_op jit(solution)/shard_map/ppermute | solution.py:412
  45.7 0.0 collective-permute-done.1.above
  45.7 0.0 collective-permute-done.2.below
  45.7 0.8 shard_map.107
  46.5 0.0 copy-done
  46.5 0.0 copy-done.3
  46.6 6.3 %shard_map.108 = (bf16[400,256]{1,0:T(8,128)(2,1)S(1)}, bf16[496,128]{1,0:T(8,128)(2,1)S(1)}, bf16[496,128]{1,0:T(8,128)(2,1)S(1)}, bf16[496,128]{1,0:T(8,128)(2...) custom-call(bf16[448,384]{1,0:T(8,128)(2,1)S(1)} %get-tuple-element.33.active_ref, ...), custom_call_target="tpu_custom_call" | custom-call | flops 3500000000 | bytes 8750000 | tf_op jit(solution)/shard_map/pallas_call | solution.py:390
  52.8 0.5 collective-permute-start.6
  53.3 0.8 collective-permute-start.7
  54.1 0.0 collective-permute-done.3.refs_1_
  54.1 1.7 %collective-permute-start.8 = (bf16[496,128]{1,0:T(8,128)(2,1)S(1)}, bf16[496,128]{1,0:T(8,128)(2,1)S(1)}, u32[]{:S(2)}, u32[]{:S(2)}) collective-permute-start(bf16[496,128]{1,0:T(8,128)(2,1)S(1)} %get-tuple-element.42), channel_id=1, source_target_pairs={{0,192},{64,0},{128,64},{192,128},{1,193},{65,1},{129,65},{193,129... | collective-permute-start | bytes 380936 | tf_op jit(solution)/shard_map/ppermute | solution.py:412
  55.8 2.2 %shard_map.110.refs_4_ = f32[512,384]{1,0:T(8,128)S(1)} custom-call(bf16[416,384]{1,0:T(8,128)(2,1)S(1)} %get-tuple-element.43.grad_ref, f32[400,384]{1,0:T(8,128)S(1)} %get-tuple-element.44.mid_ref, bf16[1,3456,384]{2,1,0:T(8,128)(2,1)S(1)} %get-tuple-element.50.weight, bf16[512,400]{1,0:T(8,128)(2,1)S(1)} %get-tuple-element.45.chosen), custom_call_target="tpu_custom_call" | custom-call | flops 1200000000 | bytes 3000000 | tf_op jit(solution)/shard_map/pallas_call | solution.py:390
  58.0 0.0 collective-permute-done.4.refs_2_
  58.1 0.0 collective-permute-done.5.refs_3_
  58.1 0.4 shard_map.109.turned
  58.4 2.3 %collective-permute-done.6.refs_1_ = bf16[496,128]{1,0:T(8,128)(2,1)S(1)} collective-permute-done((bf16[496,128]{1,0:T(8,128)(2,1)S(1)}, bf16[496,128]{1,0:T(8,128)(2,1)S(1)}, u32[]{:S(2)}, u32[]{:S(2)}) %collective-permute-start.6) | collective-permute-done | bytes 127008 | tf_op jit(solution)/shard_map/ppermute | solution.py:412
  60.7 1.5 %collective-permute-done.7.refs_2_ = bf16[496,128]{1,0:T(8,128)(2,1)S(1)} collective-permute-done((bf16[496,128]{1,0:T(8,128)(2,1)S(1)}, bf16[496,128]{1,0:T(8,128)(2,1)S(1)}, u32[]{:S(2)}, u32[]{:S(2)}) %collective-permute-start.7) | collective-permute-done | bytes 127008 | tf_op jit(solution)/shard_map/ppermute | solution.py:412
  62.3 0.0 collective-permute-done.8.refs_3_
  62.3 0.0 copy-start.1
  62.3 0.0 copy-start.2
  62.3 3.5 %shard_map.111 = bf16[64,16,384]{2,1,0:T(8,128)(2,1)} custom-call(bf16[4,384,384]{2,1,0:T(8,128)(2,1)S(1)} %shard_map.109.turned, bf16[496,128]{1,0:T(8,128)(2,1)S(1)} %get-tuple-element.39.refs_0_, bf16[496,128]{1,0:T(8,128)(2,1)S(1)} %collective-permute-done.6.refs_1_, bf16[496,128]{1,0:T(8,128)(2,1)S(1)} %collective-permute-done.7.refs_2_, ...), custom_call_target="tpu_custom_call" | custom-call | flops 1500000000 | bytes 3750000 | tf_op jit(solution)/shard_map/pallas_call | solution.py:390
  65.8 7.6 %all-to-all-start.1 = ((bf16[64,16,384]{2,1,0:T(8,128)(2,1)}), bf16[64,16,384]{2,1,0:T(8,128)(2,1)S(1)}, u32[]{:S(2)}, u32[]{:S(2)}) async-start(bf16[64,16,384]{2,1,0:T(8,128)(2,1)} %shard_map.111), calls=%async_computation.1 | async-start | bytes 1572864 | tf_op jit(solution)/shard_map/all_to_all | solution.py:536
  73.4 0.7 constant_dynamic-slice_fusion
  74.1 22.2 %all-to-all-done.1.arrived = bf16[64,16,384]{2,1,0:T(8,128)(2,1)S(1)} async-done(((bf16[64,16,384]{2,1,0:T(8,128)(2,1)}), bf16[64,16,384]{2,1,0:T(8,128)(2,1)S(1)}, u32[]{:S(2)}, u32[]{:S(2)}) %all-to-all-start.1) | async-done | bytes 786464 | tf_op jit(solution)/shard_map/all_to_all | solution.py:536
  96.3 0.0 copy-done.1
  96.3 0.0 copy-done.2
  96.3 1.2 %shard_map.112 = (f32[40,768]{1,0:T(8,128)}, f32[54,2,384]{2,1,0:T(2,128)}) custom-call(bf16[64,16,384]{2,1,0:T(8,128)(2,1)S(1)} %all-to-all-done.1.arrived, f32[40,128]{1,0:T(8,128)S(1)} %copy-done.2, bf16[768,384]{1,0:T(8,128)(2,1)S(1)} %copy-done.1), custom_call_target="tpu_custom_call" | custom-call | flops 80000000 | bytes 200000 | tf_op jit(solution)/shard_map/pallas_call | solution.py:390
  (2 shorter events, 0.0 us)
Async XLA Ops:
  2.6 20.1 %collective-permute-start = (bf16[200,384]{1,0:T(8,128)(2,1)S(1)}, bf16[200,384]{1,0:T(8,128)(2,1)S(1)}, u32[]{:S(2)}, u32[]{:S(2)}) collective-permute-start(bf16[200,384]{1,0:T(8,128)(2,1)S(1)} %reshape.15.own_aim), channel_id=1, source_target_pairs={{0,4},{4,0},{1,5},{5,1},{2,6},{6,2},{3,7},{7,3},{8,12},{12,8},{9,1... | collective-permute-start | bytes 460808 | tf_op jit(solution)/shard_map/ppermute | solution.py:412
  8.2 21.9 %all-to-all-start = ((bf16[64,8,256]{2,1,0:T(8,128)(2,1)}), bf16[64,8,256]{2,1,0:T(8,128)(2,1)S(1)}, u32[]{:S(2)}, u32[]{:S(2)}) async-start(bf16[64,8,256]{2,1,0:T(8,128)(2,1)} %bitcast.6), calls=%async_computation | async-start | bytes 524288 | tf_op jit(solution)/shard_map/all_to_all | solution.py:433
  18.1 4.6 %copy-start.4 = (bf16[384]{0:T(512)(128)(2,1)S(1)}, bf16[384]{0:T(512)(128)(2,1)}, u32[]{:S(2)}) copy-start(bf16[384]{0:T(512)(128)(2,1)} %param.13) | copy-start | bytes 2308
  31.1 14.6 %collective-permute-start.1 = (bf16[48,384]{1,0:T(8,128)(2,1)S(1)}, bf16[48,384]{1,0:T(8,128)(2,1)S(1)}, u32[]{:S(2)}, u32[]{:S(2)}) collective-permute-start(bf16[48,384]{1,0:T(8,128)(2,1)S(1)} %get-tuple-element.27), channel_id=1, source_target_pairs={{0,8},{8,16},{16,24},{24,32},{32,40},{40,48},{48,56},{56,64},{64,7... | collective-permute-start | bytes 110600 | tf_op jit(solution)/shard_map/ppermute | solution.py:412
  34.2 11.5 %collective-permute-start.2 = (bf16[48,384]{1,0:T(8,128)(2,1)S(1)}, bf16[48,384]{1,0:T(8,128)(2,1)S(1)}, u32[]{:S(2)}, u32[]{:S(2)}) collective-permute-start(bf16[48,384]{1,0:T(8,128)(2,1)S(1)} %get-tuple-element.29), channel_id=1, source_target_pairs={{8,0},{16,8},{24,16},{32,24},{40,32},{48,40},{56,48},{64,56},{72,6... | collective-permute-start | bytes 110600 | tf_op jit(solution)/shard_map/ppermute | solution.py:412
  38.0 8.6 %copy-start = (bf16[1,3456,384]{2,1,0:T(8,128)(2,1)S(1)}, bf16[1,3456,384]{2,1,0:T(8,128)(2,1)}, u32[]{:S(2)}) copy-start(bf16[1,3456,384]{2,1,0:T(8,128)(2,1)} %get-tuple-element.49.weight) | copy-start | bytes 7962628
  38.0 8.6 %copy-start.3 = (bf16[384,256]{1,0:T(8,128)(2,1)S(1)}, bf16[384,256]{1,0:T(8,128)(2,1)}, u32[]{:S(2)}) copy-start(bf16[384,256]{1,0:T(8,128)(2,1)} %head.1) | copy-start | bytes 589828
  38.0 16.1 %collective-permute-start.3 = (bf16[384,384]{1,0:T(8,128)(2,1)S(1)}, bf16[384,384]{1,0:T(8,128)(2,1)S(1)}, u32[]{:S(2)}, u32[]{:S(2)}) collective-permute-start(bf16[384,384]{1,0:T(8,128)(2,1)S(1)} %get-tuple-element.38.refs_0_), channel_id=1, source_target_pairs={{0,64},{64,128},{128,192},{192,0},{1,65},{65,129},{129,193},{193,1... | collective-permute-start | bytes 884744 | tf_op jit(solution)/shard_map/ppermute | solution.py:412
  42.0 16.0 %collective-permute-start.4 = (bf16[384,384]{1,0:T(8,128)(2,1)S(1)}, bf16[384,384]{1,0:T(8,128)(2,1)S(1)}, u32[]{:S(2)}, u32[]{:S(2)}) collective-permute-start(bf16[384,384]{1,0:T(8,128)(2,1)S(1)} %get-tuple-element.38.refs_0_), channel_id=1, source_target_pairs={{0,128},{64,192},{128,0},{192,64},{1,129},{65,193},{129,1},{193,65... | collective-permute-start | bytes 884744 | tf_op jit(solution)/shard_map/ppermute | solution.py:412
  44.6 13.4 %collective-permute-start.5 = (bf16[384,384]{1,0:T(8,128)(2,1)S(1)}, bf16[384,384]{1,0:T(8,128)(2,1)S(1)}, u32[]{:S(2)}, u32[]{:S(2)}) collective-permute-start(bf16[384,384]{1,0:T(8,128)(2,1)S(1)} %get-tuple-element.38.refs_0_), channel_id=1, source_target_pairs={{0,192},{64,0},{128,64},{192,128},{1,193},{65,1},{129,65},{193,129... | collective-permute-start | bytes 884744 | tf_op jit(solution)/shard_map/ppermute | solution.py:412
  52.8 7.9 %collective-permute-start.6 = (bf16[496,128]{1,0:T(8,128)(2,1)S(1)}, bf16[496,128]{1,0:T(8,128)(2,1)S(1)}, u32[]{:S(2)}, u32[]{:S(2)}) collective-permute-start(bf16[496,128]{1,0:T(8,128)(2,1)S(1)} %get-tuple-element.40), channel_id=1, source_target_pairs={{0,64},{64,128},{128,192},{192,0},{1,65},{65,129},{129,193},{193,1... | collective-permute-start | bytes 380936 | tf_op jit(solution)/shard_map/ppermute | solution.py:412
  53.3 9.0 %collective-permute-start.7 = (bf16[496,128]{1,0:T(8,128)(2,1)S(1)}, bf16[496,128]{1,0:T(8,128)(2,1)S(1)}, u32[]{:S(2)}, u32[]{:S(2)}) collective-permute-start(bf16[496,128]{1,0:T(8,128)(2,1)S(1)} %get-tuple-element.41), channel_id=1, source_target_pairs={{0,128},{64,192},{128,0},{192,64},{1,129},{65,193},{129,1},{193,65... | collective-permute-start | bytes 380936 | tf_op jit(solution)/shard_map/ppermute | solution.py:412
  54.1 8.2 %collective-permute-start.8 = (bf16[496,128]{1,0:T(8,128)(2,1)S(1)}, bf16[496,128]{1,0:T(8,128)(2,1)S(1)}, u32[]{:S(2)}, u32[]{:S(2)}) collective-permute-start(bf16[496,128]{1,0:T(8,128)(2,1)S(1)} %get-tuple-element.42), channel_id=1, source_target_pairs={{0,192},{64,0},{128,64},{192,128},{1,193},{65,1},{129,65},{193,129... | collective-permute-start | bytes 380936 | tf_op jit(solution)/shard_map/ppermute | solution.py:412
  62.3 34.1 %copy-start.1 = (bf16[768,384]{1,0:T(8,128)(2,1)S(1)}, bf16[768,384]{1,0:T(8,128)(2,1)}, u32[]{:S(2)}) copy-start(bf16[768,384]{1,0:T(8,128)(2,1)} %in_weight.3) | copy-start | bytes 1769476
  62.3 34.1 %copy-start.2 = (f32[40,128]{1,0:T(8,128)S(1)}, f32[40,128]{1,0:T(8,128)}, u32[]{:S(2)}) copy-start(f32[40,128]{1,0:T(8,128)} %get-tuple-element.46.where_ref) | copy-start | bytes 61444
  65.8 30.6 %all-to-all-start.1 = ((bf16[64,16,384]{2,1,0:T(8,128)(2,1)}), bf16[64,16,384]{2,1,0:T(8,128)(2,1)S(1)}, u32[]{:S(2)}, u32[]{:S(2)}) async-start(bf16[64,16,384]{2,1,0:T(8,128)(2,1)} %shard_map.111), calls=%async_computation.1 | async-start | bytes 1572864 | tf_op jit(solution)/shard_map/all_to_all | solution.py:536

commit v8 on v7

--- a/solution.py
+++ b/solution.py
@@ -235,7 +235,7 @@
     share_out[...] = jnp.where(lax.axis_index("freq") == 1, active, source[8:392]).astype(BF16)
 
 
-def first_kernel(
+def border_rows(
     above, own, below, weight, active_in, unit_in, scale_in,
     active_out, unit_out, scale_out, share_out, even, odd,
 ):
@@ -271,9 +271,14 @@
 
 
 def second_kernel(
-    active_ref, unit_ref, scale_ref, border, weight, head, above, aim_ref, below,
-    pred, share_own, share_one, share_two, share_three, mid_out, grad_out, even, odd,
+    above, own, below, first_weight, active_in, unit_in, scale_in, weight, head, aim_ref,
+    pred, share_own, share_one, share_two, share_three, mid_out, grad_out,
+    even, odd, active_ref, unit_ref, scale_ref, border,
 ):
+    border_rows(
+        above, own, below, first_weight, active_in, unit_in, scale_in,
+        active_ref, unit_ref, scale_ref, border, even, odd,
+    )
     active = active_ref[...].astype(F32)
     store_columns(active, even, odd)
     unit, scale = normed(conv_taps((even[0:432], odd[0:432], even[16:448]), weight))
@@ -300,9 +305,12 @@
         quarter = (lax.axis_index("tm_0") + step) & 3
         piece = jnp.where(quarter == 0, pieces[0], pieces[1])
         piece = jnp.where(quarter >= 2, jnp.where(quarter == 2, pieces[2], pieces[3]), piece)
-        share_out[0:CELLS] = jnp.where(lane < 96, piece, 0.0).astype(BF16)
+        rest = piece[304:400]
+        side = [pltpu.roll(rest, 96 - 32 * part, axis=1) for part in range(3)]
+        side = jnp.concatenate([*side, jnp.zeros((16, 128), F32)], axis=0)
+        share_out[0:304] = jnp.where(lane[0:304] < 96, piece[0:304], side).astype(BF16)
         for part in range(3):
-            share_out[CELLS + 32 * part : CELLS + 32 * (part + 1)] = border[
+            share_out[304 + 32 * part : 304 + 32 * (part + 1)] = border[
                 :, 128 * part : 128 * (part + 1)
             ]
 
@@ -313,35 +321,47 @@
 
 
 def turn_kernel(*refs):
-    for part in range(4):
-        refs[4][part] = refs[part][...].astype(F32).T.astype(BF16)
-
-
-def weight_kernel(turned, *refs):
-    outers, picked = refs[0:4], refs[4]
-    out, moved, total = refs[5:]
-    summed = None
-    for part in range(4):
-        low, middle, high = column_shifted(outers[part][0:CELLS].astype(F32))
-        for row_off in range(3):
-            for col_off, piece in enumerate((high, middle, low)):
-                rows = [piece]
-                if row_off:
-                    rows.insert(0, jnp.zeros((8 * row_off, 128), F32))
-                if row_off < 2:
-                    rows.append(jnp.zeros((16 - 8 * row_off, 128), F32))
-                rows = jnp.concatenate(rows, axis=0).astype(BF16)
-                tap = 3 * row_off + col_off
-                lanes = slice(tap * 128, (tap + 1) * 128)
-                moved[part, 0:384, lanes] = rows[16:400]
-                moved[part, 384:400, lanes] = rows[0:16]
-                moved[part, 400:416, lanes] = rows[400:416]
-        border = jnp.concatenate(
-            [outers[part][CELLS + 32 * k : CELLS + 32 * (k + 1)] for k in range(3)], axis=1
-        )
-        inner = jnp.concatenate([turned[part], border.astype(F32).T.astype(BF16)], axis=1)
-        term = jnp.dot(inner, moved[part], preferred_element_type=F32)
-        summed = term if summed is None else summed + term
+    for part in range(3):
+        refs[3][part] = refs[part][...].astype(F32).T.astype(BF16)
+
+
+def chip_term(turned, outer, moved):
+    packed = outer[0:304].astype(F32)
+    lane = lax.broadcasted_iota(jnp.int32, (96, 128), 1)
+    rest = jnp.where(lane < 96, pltpu.roll(packed[192:288], 96, axis=1), 0.0)
+    rest = jnp.where(lane < 64, pltpu.roll(packed[96:192], 64, axis=1), rest)
+    rest = jnp.where(lane < 32, pltpu.roll(packed[0:96], 32, axis=1), rest)
+    lane = lax.broadcasted_iota(jnp.int32, (304, 128), 1)
+    gradient = jnp.concatenate([jnp.where(lane < 96, packed, 0.0), rest], axis=0)
+    low, middle, high = column_shifted(gradient)
+    for row_off in range(3):
+        for col_off, piece in enumerate((high, middle, low)):
+            rows = [piece]
+            if row_off:
+                rows.insert(0, jnp.zeros((8 * row_off, 128), F32))
+            if row_off < 2:
+                rows.append(jnp.zeros((16 - 8 * row_off, 128), F32))
+            rows = jnp.concatenate(rows, axis=0).astype(BF16)
+            tap = 3 * row_off + col_off
+            lanes = slice(tap * 128, (tap + 1) * 128)
+            moved[0:384, lanes] = rows[16:400]
+            moved[384:400, lanes] = rows[0:16]
+            moved[400:416, lanes] = rows[400:416]
+    border = jnp.concatenate([outer[304 + 32 * k : 336 + 32 * k] for k in range(3)], axis=1)
+    inner = jnp.concatenate([turned, border.astype(F32).T.astype(BF16)], axis=1)
+    return jnp.dot(inner, moved[...], preferred_element_type=F32)
+
+
+def own_kernel(inner, outer, out, moved):
+    out[...] = chip_term(inner[...].astype(F32).T.astype(BF16), outer, moved)
+
+
+def weight_kernel(summed_ref, turned, *refs):
+    outers, picked = refs[0:3], refs[3]
+    out, moved, total = refs[4:]
+    summed = summed_ref[...]
+    for part in range(3):
+        summed = summed + chip_term(turned[part], outers[part], moved.at[part])
     for tap in range(9):
         total[tap * CHANNELS : (tap + 1) * CHANNELS] = summed[:, tap * 128 : (tap + 1) * 128]
     total[9 * CHANNELS :] = jnp.zeros((8, 128), F32)
@@ -472,43 +492,31 @@
         weights[0],
     )
     inners = [inner] + [send(inner, "tm_0", step, True) for step in (1, 2, 3)]
-    active, unit, scale, border = call(
-        first_kernel,
+    pred, *outers, mid, grad = call(
+        second_kernel,
         (
-            shape((448, CHANNELS)),
-            shape((416, CHANNELS), F32),
-            shape((416, 128), F32),
-            shape((32, CHANNELS)),
+            shape((CELLS, PIX)),
+            *[shape((400, 128))] * 4,
+            shape((CELLS, CHANNELS), F32),
+            shape((416, CHANNELS)),
         ),
-        columns,
-        500_000_000,
-        12,
+        [
+            *columns,
+            pltpu.VMEM((448, CHANNELS), BF16),
+            pltpu.VMEM((416, CHANNELS), F32),
+            pltpu.VMEM((416, 128), F32),
+            pltpu.VMEM((32, CHANNELS), BF16),
+        ],
+        3_500_000_000,
+        22,
         above,
         own,
         below,
         weights[0],
         *inside,
-    )
-    pred, *outers, mid, grad = call(
-        second_kernel,
-        (
-            shape((CELLS, PIX)),
-            *[shape((CELLS + 96, 128))] * 4,
-            shape((CELLS, CHANNELS), F32),
-            shape((416, CHANNELS)),
-        ),
-        columns,
-        3_500_000_000,
-        18,
-        active,
-        unit,
-        scale,
-        border,
         weights[1],
         head_weight,
-        above,
         aim,
-        below,
     )
     outers[1:] = [send(outers[step], "tm_0", step, True) for step in (1, 2, 3)]
     picked = call(
@@ -522,15 +530,25 @@
         weights[0],
         chosen,
     )
-    turned = call(turn_kernel, shape((4, CHANNELS, 384)), [], 400_000_000, 8, *inners)
+    summed = call(
+        own_kernel,
+        shape((CHANNELS, 9 * 128), F32),
+        [pltpu.VMEM((416, 9 * 128), BF16)],
+        400_000_000,
+        12,
+        inner,
+        outers[0],
+    )
+    turned = call(turn_kernel, shape((3, CHANNELS, 384)), [], 300_000_000, 8, *inners[1:])
     terms = call(
         weight_kernel,
         shape((shards, 16, CHANNELS)),
-        [pltpu.VMEM((4, 416, 9 * 128), BF16), pltpu.VMEM((9 * CHANNELS + 8, 128), F32)],
+        [pltpu.VMEM((3, 416, 9 * 128), BF16), pltpu.VMEM((9 * CHANNELS + 8, 128), F32)],
         1_500_000_000,
         16,
+        summed,
         turned,
-        *outers,
+        *outers[1:],
         picked,
     )
     terms = lax.all_to_all(terms, TM_FREQ, split_axis=0, concat_axis=0, tiled=True)

time: 97.9 us -> 96.5 us (0.986)
  waiting for transfers between devices: 33 us -> 31.2 us
    ppermute x9, waiting for transfers between devices: 3.84 us -> 2.05 us  [send(): return lax.ppermute(value, axis, pairs)]
  transfers between devices with their start and end apart: 11 -> 11, of which waited for: 4 -> 4; matrix products, arithmetic and copies ran while one was open for 5% -> 6% of each run, Pallas kernels for 15% -> 16%
where the time goes in v8:
time: 96.5 us; the launch traced here: 96.1 us
  starting transfers between devices  35.9 us (37%)
  waiting for transfers between devices  31.2 us (32%)
  Pallas kernels  20.9 us (22%)
  local copies, waits for them, and re-layouts  5.61 us (6%)
  other arithmetic  1.66 us (2%)
    all_to_all x1, waiting for transfers between devices, per_device(): lax.all_to_all(terms, TM_FREQ, split_axis=0, concat_axis=0, tiled=True)  22.2 us
    pallas_call x10, Pallas kernels, call(): pl.pallas_call(kernel, out_shape=shapes, in_specs=[VMEM] * len(operands),...  20.9 us
    ppermute x9, starting transfers between devices, send(): return lax.ppermute(value, axis, pairs)  18.3 us
    all_to_all x1, starting transfers between devices, per_device(): lax.all_to_all(packed, TM_FREQ, split_axis=0, concat_axis=0, tiled=True)  9.89 us
    all_to_all x1, starting transfers between devices, per_device(): lax.all_to_all(terms, TM_FREQ, split_axis=0, concat_axis=0, tiled=True)  7.7 us
    all_to_all x1, waiting for transfers between devices, per_device(): lax.all_to_all(packed, TM_FREQ, split_axis=0, concat_axis=0, tiled=True)  6.95 us
    slice x1, local copies, waits for them, and re-layouts, per_device(): weights = [conv_weight[layer:layer + 1] for layer in range(2)]  4.6 us
    ppermute x9, waiting for transfers between devices, send(): return lax.ppermute(value, axis, pairs)  2.05 us
  transfers between devices with their start and end apart: 11, of which 4 were waited for; matrix products, arithmetic and copies ran while one was open for 6% of the time, Pallas kernels for 16%

profile of v8, /device:TPU:1, one launch (start us, length us, event | category | flops | bytes accessed | tf_op | source)
XLA Modules:
  0.0 96.1 jit_solution(7709630018274225127)
XLA Ops:
  0.6 0.7 compare_convert_fusion
  1.3 0.1 copy.11
  1.4 0.1 broadcast_in_dim.4
  1.6 1.0 %pad_maximum_fusion = bf16[50,4,384]{2,1,0:T(4,128)(2,1)S(1)} fusion(bf16[50,4,128]{2,1,0:T(4,128)(2,1)S(1)} %broadcast_in_dim.4, bf16[50,4,256]{2,1,0:T(4,128)(2,1)} %param.11), kind=kLoop, calls=%fused_computation | loop fusion | flops 307200 | bytes 307200 | tf_op jit(solution)/shard_map/concatenate | solution.py:455
  2.6 3.3 %collective-permute-start = (bf16[200,384]{1,0:T(8,128)(2,1)S(1)}, bf16[200,384]{1,0:T(8,128)(2,1)S(1)}, u32[]{:S(2)}, u32[]{:S(2)}) collective-permute-start(bf16[200,384]{1,0:T(8,128)(2,1)S(1)} %reshape.15.own_aim), channel_id=1, source_target_pairs={{0,4},{4,0},{1,5},{5,1},{2,6},{6,2},{3,7},{7,3},{8,12},{12,8},{9,1... | collective-permute-start | bytes 460808 | tf_op jit(solution)/shard_map/ppermute | solution.py:432
  5.9 2.3 %shard_map.103 = (bf16[512,256]{1,0:T(8,128)(2,1)}, f32[40,128]{1,0:T(8,128)}) custom-call(bf16[40,768]{1,0:T(8,128)(2,1)} %tokens.1, s32[2,40]{1,0:T(2,128)} %placement.1, bf16[768,384]{1,0:T(8,128)(2,1)} %in_weight.3), custom_call_target="tpu_custom_call" | custom-call | flops 80000000 | bytes 200000 | tf_op jit(solution)/shard_map/pallas_call | solution.py:410
  8.2 9.9 %all-to-all-start = ((bf16[64,8,256]{2,1,0:T(8,128)(2,1)}), bf16[64,8,256]{2,1,0:T(8,128)(2,1)S(1)}, u32[]{:S(2)}, u32[]{:S(2)}) async-start(bf16[64,8,256]{2,1,0:T(8,128)(2,1)} %bitcast.6), calls=%async_computation | async-start | bytes 524288 | tf_op jit(solution)/shard_map/all_to_all | solution.py:453
  18.1 0.0 copy-start.4
  18.1 4.6 %fusion = (bf16[1,3456,384]{2,1,0:T(8,128)(2,1)}, bf16[1,3456,384]{2,1,0:T(8,128)(2,1)S(1)}) fusion(bf16[2,3456,384]{2,1,0:T(8,128)(2,1)} %param.14), kind=kLoop, calls=%fused_computation.3 | loop fusion | bytes 10616832 | tf_op jit(solution)/shard_map/slice | solution.py:459
  22.7 0.0 copy-done.4
  22.7 0.0 collective-permute-done.other_aim
  22.7 0.4 shard_map.104.aim.aim_ref
  23.1 7.0 %all-to-all-done = bf16[64,8,256]{2,1,0:T(8,128)(2,1)S(1)} async-done(((bf16[64,8,256]{2,1,0:T(8,128)(2,1)}), bf16[64,8,256]{2,1,0:T(8,128)(2,1)S(1)}, u32[]{:S(2)}, u32[]{:S(2)}) %all-to-all-start) | async-done | bytes 262176 | tf_op jit(solution)/shard_map/all_to_all | solution.py:453
  30.1 0.0 copy-start
  30.1 0.0 copy-start.3
  30.1 1.1 %shard_map.105 = (bf16[400,384]{1,0:T(8,128)(2,1)S(1)}, bf16[48,384]{1,0:T(8,128)(2,1)S(1)}, bf16[48,384]{1,0:T(8,128)(2,1)S(1)}, bf16[512,400]{1,0:T(8,128)(2,1)S(1)}) custom-call(bf16[512,256]{1,0:T(8,128)(2,1)S(1)} %bitcast.4, bf16[400,384]{1,0:T(8,128)(2,1)S(1)} %shard_map.104.aim.aim_ref, bf16[1,384]{1,0:T(2,128)(2,1)S(1)} %broadcast_in_dim.10.token), custom_call_target="tpu_custom_call" | custom-call | flops 300000000 | bytes 750000 | tf_op jit(solution)/shard_map/pallas_call | solution.py:410
  31.2 3.1 %collective-permute-start.1 = (bf16[48,384]{1,0:T(8,128)(2,1)S(1)}, bf16[48,384]{1,0:T(8,128)(2,1)S(1)}, u32[]{:S(2)}, u32[]{:S(2)}) collective-permute-start(bf16[48,384]{1,0:T(8,128)(2,1)S(1)} %get-tuple-element.23), channel_id=1, source_target_pairs={{0,8},{8,16},{16,24},{24,32},{32,40},{40,48},{48,56},{56,64},{64,7... | collective-permute-start | bytes 110600 | tf_op jit(solution)/shard_map/ppermute | solution.py:432
  34.2 1.3 %collective-permute-start.2 = (bf16[48,384]{1,0:T(8,128)(2,1)S(1)}, bf16[48,384]{1,0:T(8,128)(2,1)S(1)}, u32[]{:S(2)}, u32[]{:S(2)}) collective-permute-start(bf16[48,384]{1,0:T(8,128)(2,1)S(1)} %get-tuple-element.25), channel_id=1, source_target_pairs={{8,0},{16,8},{24,16},{32,24},{40,32},{48,40},{56,48},{64,56},{72,6... | collective-permute-start | bytes 110600 | tf_op jit(solution)/shard_map/ppermute | solution.py:432
  35.5 2.4 %shard_map.106 = (bf16[384,384]{1,0:T(8,128)(2,1)S(1)}, f32[384,384]{1,0:T(8,128)S(1)}, f32[384,128]{1,0:T(8,128)S(1)}, bf16[384,384]{1,0:T(8,128)(2,1)S(1)}) custom-call(bf16[400,384]{1,0:T(8,128)(2,1)S(1)} %get-tuple-element.24.own, bf16[1,3456,384]{2,1,0:T(8,128)(2,1)S(1)} %get-tuple-element.42.weight.first_weight), custom_call_target="tpu_custom_call" | custom-call | flops 1200000000 | bytes 3000000 | tf_op jit(solution)/shard_map/pallas_call | solution.py:410
  38.0 4.1 %collective-permute-start.3 = (bf16[384,384]{1,0:T(8,128)(2,1)S(1)}, bf16[384,384]{1,0:T(8,128)(2,1)S(1)}, u32[]{:S(2)}, u32[]{:S(2)}) collective-permute-start(bf16[384,384]{1,0:T(8,128)(2,1)S(1)} %get-tuple-element.30.inner), channel_id=1, source_target_pairs={{0,64},{64,128},{128,192},{192,0},{1,65},{65,129},{129,193},{193,1... | collective-permute-start | bytes 884744 | tf_op jit(solution)/shard_map/ppermute | solution.py:432
  42.0 2.6 %collective-permute-start.4 = (bf16[384,384]{1,0:T(8,128)(2,1)S(1)}, bf16[384,384]{1,0:T(8,128)(2,1)S(1)}, u32[]{:S(2)}, u32[]{:S(2)}) collective-permute-start(bf16[384,384]{1,0:T(8,128)(2,1)S(1)} %get-tuple-element.30.inner), channel_id=1, source_target_pairs={{0,128},{64,192},{128,0},{192,64},{1,129},{65,193},{129,1},{193,65... | collective-permute-start | bytes 884744 | tf_op jit(solution)/shard_map/ppermute | solution.py:432
  44.6 1.1 %collective-permute-start.5 = (bf16[384,384]{1,0:T(8,128)(2,1)S(1)}, bf16[384,384]{1,0:T(8,128)(2,1)S(1)}, u32[]{:S(2)}, u32[]{:S(2)}) collective-permute-start(bf16[384,384]{1,0:T(8,128)(2,1)S(1)} %get-tuple-element.30.inner), channel_id=1, source_target_pairs={{0,192},{64,0},{128,64},{192,128},{1,193},{65,1},{129,65},{193,129... | collective-permute-start | bytes 884744 | tf_op jit(solution)/shard_map/ppermute | solution.py:432
  45.7 0.0 collective-permute-done.1.above
  45.7 0.0 collective-permute-done.2.below
  45.7 0.0 copy-done
  45.7 0.0 copy-done.3
  45.7 7.1 %shard_map.107 = (bf16[400,256]{1,0:T(8,128)(2,1)S(1)}, bf16[400,128]{1,0:T(8,128)(2,1)S(1)}, bf16[400,128]{1,0:T(8,128)(2,1)S(1)}, bf16[400,128]{1,0:T(8,128)(2...) custom-call(bf16[48,384]{1,0:T(8,128)(2,1)S(1)} %collective-permute-done.1.above, ...), custom_call_target="tpu_custom_call" | custom-call | flops 3500000000 | bytes 8750000 | tf_op jit(solution)/shard_map/pallas_call | solution.py:410
  52.8 0.5 collective-permute-start.6
  53.3 0.8 collective-permute-start.7
  54.1 0.0 collective-permute-done.3.refs_0_
  54.1 1.7 %collective-permute-start.8 = (bf16[400,128]{1,0:T(8,128)(2,1)S(1)}, bf16[400,128]{1,0:T(8,128)(2,1)S(1)}, u32[]{:S(2)}, u32[]{:S(2)}) collective-permute-start(bf16[400,128]{1,0:T(8,128)(2,1)S(1)} %get-tuple-element.34), channel_id=1, source_target_pairs={{0,192},{64,0},{128,64},{192,128},{1,193},{65,1},{129,65},{193,129... | collective-permute-start | bytes 307208 | tf_op jit(solution)/shard_map/ppermute | solution.py:432
  55.8 2.2 %shard_map.110.refs_3_ = f32[512,384]{1,0:T(8,128)S(1)} custom-call(bf16[416,384]{1,0:T(8,128)(2,1)S(1)} %get-tuple-element.35.grad_ref, f32[400,384]{1,0:T(8,128)S(1)} %get-tuple-element.36.mid_ref, bf16[1,3456,384]{2,1,0:T(8,128)(2,1)S(1)} %get-tuple-element.42.weight.first_weight, bf16[512,400]{1,0:T(8,128)(2,1)S(1)} %get-tuple-element.37.chosen), custom_call_target="tpu_custom_call" | custom-call | flops 1200000000 | bytes 3000000 | tf_op jit(solution)/shard_map/pallas_call | solution.py:410
  57.9 0.9 shard_map.108.summed_ref
  58.8 0.0 collective-permute-done.4.refs_1_
  58.8 0.0 collective-permute-done.5.refs_2_
  58.8 0.3 shard_map.109.turned
  59.1 0.0 copy-start.1
  59.2 0.0 copy-start.2
  59.2 1.0 %collective-permute-done.6.refs_0_ = bf16[400,128]{1,0:T(8,128)(2,1)S(1)} collective-permute-done((bf16[400,128]{1,0:T(8,128)(2,1)S(1)}, bf16[400,128]{1,0:T(8,128)(2,1)S(1)}, u32[]{:S(2)}, u32[]{:S(2)}) %collective-permute-start.6) | collective-permute-done | bytes 102432 | tf_op jit(solution)/shard_map/ppermute | solution.py:432
  60.2 1.0 %collective-permute-done.7.refs_1_ = bf16[400,128]{1,0:T(8,128)(2,1)S(1)} collective-permute-done((bf16[400,128]{1,0:T(8,128)(2,1)S(1)}, bf16[400,128]{1,0:T(8,128)(2,1)S(1)}, u32[]{:S(2)}, u32[]{:S(2)}) %collective-permute-start.7) | collective-permute-done | bytes 102432 | tf_op jit(solution)/shard_map/ppermute | solution.py:432
  61.2 0.0 collective-permute-done.8.refs_2_
  61.2 3.0 %shard_map.111 = bf16[64,16,384]{2,1,0:T(8,128)(2,1)} custom-call(f32[384,1152]{1,0:T(8,128)S(1)} %shard_map.108.summed_ref, bf16[3,384,384]{2,1,0:T(8,128)(2,1)S(1)} %shard_map.109.turned, bf16[400,128]{1,0:T(8,128)(2,1)S(1)} %collective-permute-done.6.refs_0_, bf16[400,128]{1,0:T(8,128)(2,1)S(1)} %collective-permute-done.7.refs_1_, ...), custom_call_target="tpu_custom_call" | custom-call | flops 1500000000 | bytes 3750000 | tf_op jit(solution)/shard_map/pallas_call | solution.py:410
  64.2 7.7 %all-to-all-start.1 = ((bf16[64,16,384]{2,1,0:T(8,128)(2,1)}), bf16[64,16,384]{2,1,0:T(8,128)(2,1)S(1)}, u32[]{:S(2)}, u32[]{:S(2)}) async-start(bf16[64,16,384]{2,1,0:T(8,128)(2,1)} %shard_map.111), calls=%async_computation.1 | async-start | bytes 1572864 | tf_op jit(solution)/shard_map/all_to_all | solution.py:554
  71.9 0.7 constant_dynamic-slice_fusion
  72.6 22.2 %all-to-all-done.1.arrived = bf16[64,16,384]{2,1,0:T(8,128)(2,1)S(1)} async-done(((bf16[64,16,384]{2,1,0:T(8,128)(2,1)}), bf16[64,16,384]{2,1,0:T(8,128)(2,1)S(1)}, u32[]{:S(2)}, u32[]{:S(2)}) %all-to-all-start.1) | async-done | bytes 786464 | tf_op jit(solution)/shard_map/all_to_all | solution.py:554
  94.9 0.0 copy-done.1
  94.9 0.0 copy-done.2
  94.9 1.2 %shard_map.112 = (f32[40,768]{1,0:T(8,128)}, f32[54,2,384]{2,1,0:T(2,128)}) custom-call(bf16[64,16,384]{2,1,0:T(8,128)(2,1)S(1)} %all-to-all-done.1.arrived, f32[40,128]{1,0:T(8,128)S(1)} %copy-done.2, bf16[768,384]{1,0:T(8,128)(2,1)S(1)} %copy-done.1), custom_call_target="tpu_custom_call" | custom-call | flops 80000000 | bytes 200000 | tf_op jit(solution)/shard_map/pallas_call | solution.py:410
  (2 shorter events, 0.0 us)
Async XLA Ops:
  2.6 20.1 %collective-permute-start = (bf16[200,384]{1,0:T(8,128)(2,1)S(1)}, bf16[200,384]{1,0:T(8,128)(2,1)S(1)}, u32[]{:S(2)}, u32[]{:S(2)}) collective-permute-start(bf16[200,384]{1,0:T(8,128)(2,1)S(1)} %reshape.15.own_aim), channel_id=1, source_target_pairs={{0,4},{4,0},{1,5},{5,1},{2,6},{6,2},{3,7},{7,3},{8,12},{12,8},{9,1... | collective-permute-start | bytes 460808 | tf_op jit(solution)/shard_map/ppermute | solution.py:432
  8.2 21.9 %all-to-all-start = ((bf16[64,8,256]{2,1,0:T(8,128)(2,1)}), bf16[64,8,256]{2,1,0:T(8,128)(2,1)S(1)}, u32[]{:S(2)}, u32[]{:S(2)}) async-start(bf16[64,8,256]{2,1,0:T(8,128)(2,1)} %bitcast.6), calls=%async_computation | async-start | bytes 524288 | tf_op jit(solution)/shard_map/all_to_all | solution.py:453
  18.1 4.6 %copy-start.4 = (bf16[384]{0:T(512)(128)(2,1)S(1)}, bf16[384]{0:T(512)(128)(2,1)}, u32[]{:S(2)}) copy-start(bf16[384]{0:T(512)(128)(2,1)} %param.13) | copy-start | bytes 2308
  30.1 15.6 %copy-start = (bf16[1,3456,384]{2,1,0:T(8,128)(2,1)S(1)}, bf16[1,3456,384]{2,1,0:T(8,128)(2,1)}, u32[]{:S(2)}) copy-start(bf16[1,3456,384]{2,1,0:T(8,128)(2,1)} %get-tuple-element.41.weight) | copy-start | bytes 7962628
  30.1 15.6 %copy-start.3 = (bf16[384,256]{1,0:T(8,128)(2,1)S(1)}, bf16[384,256]{1,0:T(8,128)(2,1)}, u32[]{:S(2)}) copy-start(bf16[384,256]{1,0:T(8,128)(2,1)} %head.1) | copy-start | bytes 589828
  31.2 14.6 %collective-permute-start.1 = (bf16[48,384]{1,0:T(8,128)(2,1)S(1)}, bf16[48,384]{1,0:T(8,128)(2,1)S(1)}, u32[]{:S(2)}, u32[]{:S(2)}) collective-permute-start(bf16[48,384]{1,0:T(8,128)(2,1)S(1)} %get-tuple-element.23), channel_id=1, source_target_pairs={{0,8},{8,16},{16,24},{24,32},{32,40},{40,48},{48,56},{56,64},{64,7... | collective-permute-start | bytes 110600 | tf_op jit(solution)/shard_map/ppermute | solution.py:432
  34.2 11.5 %collective-permute-start.2 = (bf16[48,384]{1,0:T(8,128)(2,1)S(1)}, bf16[48,384]{1,0:T(8,128)(2,1)S(1)}, u32[]{:S(2)}, u32[]{:S(2)}) collective-permute-start(bf16[48,384]{1,0:T(8,128)(2,1)S(1)} %get-tuple-element.25), channel_id=1, source_target_pairs={{8,0},{16,8},{24,16},{32,24},{40,32},{48,40},{56,48},{64,56},{72,6... | collective-permute-start | bytes 110600 | tf_op jit(solution)/shard_map/ppermute | solution.py:432
  38.0 16.1 %collective-permute-start.3 = (bf16[384,384]{1,0:T(8,128)(2,1)S(1)}, bf16[384,384]{1,0:T(8,128)(2,1)S(1)}, u32[]{:S(2)}, u32[]{:S(2)}) collective-permute-start(bf16[384,384]{1,0:T(8,128)(2,1)S(1)} %get-tuple-element.30.inner), channel_id=1, source_target_pairs={{0,64},{64,128},{128,192},{192,0},{1,65},{65,129},{129,193},{193,1... | collective-permute-start | bytes 884744 | tf_op jit(solution)/shard_map/ppermute | solution.py:432
  42.0 16.8 %collective-permute-start.4 = (bf16[384,384]{1,0:T(8,128)(2,1)S(1)}, bf16[384,384]{1,0:T(8,128)(2,1)S(1)}, u32[]{:S(2)}, u32[]{:S(2)}) collective-permute-start(bf16[384,384]{1,0:T(8,128)(2,1)S(1)} %get-tuple-element.30.inner), channel_id=1, source_target_pairs={{0,128},{64,192},{128,0},{192,64},{1,129},{65,193},{129,1},{193,65... | collective-permute-start | bytes 884744 | tf_op jit(solution)/shard_map/ppermute | solution.py:432
  44.6 14.2 %collective-permute-start.5 = (bf16[384,384]{1,0:T(8,128)(2,1)S(1)}, bf16[384,384]{1,0:T(8,128)(2,1)S(1)}, u32[]{:S(2)}, u32[]{:S(2)}) collective-permute-start(bf16[384,384]{1,0:T(8,128)(2,1)S(1)} %get-tuple-element.30.inner), channel_id=1, source_target_pairs={{0,192},{64,0},{128,64},{192,128},{1,193},{65,1},{129,65},{193,129... | collective-permute-start | bytes 884744 | tf_op jit(solution)/shard_map/ppermute | solution.py:432
  52.8 7.4 %collective-permute-start.6 = (bf16[400,128]{1,0:T(8,128)(2,1)S(1)}, bf16[400,128]{1,0:T(8,128)(2,1)S(1)}, u32[]{:S(2)}, u32[]{:S(2)}) collective-permute-start(bf16[400,128]{1,0:T(8,128)(2,1)S(1)} %get-tuple-element.32), channel_id=1, source_target_pairs={{0,64},{64,128},{128,192},{192,0},{1,65},{65,129},{129,193},{193,1... | collective-permute-start | bytes 307208 | tf_op jit(solution)/shard_map/ppermute | solution.py:432
  53.3 7.9 %collective-permute-start.7 = (bf16[400,128]{1,0:T(8,128)(2,1)S(1)}, bf16[400,128]{1,0:T(8,128)(2,1)S(1)}, u32[]{:S(2)}, u32[]{:S(2)}) collective-permute-start(bf16[400,128]{1,0:T(8,128)(2,1)S(1)} %get-tuple-element.33), channel_id=1, source_target_pairs={{0,128},{64,192},{128,0},{192,64},{1,129},{65,193},{129,1},{193,65... | collective-permute-start | bytes 307208 | tf_op jit(solution)/shard_map/ppermute | solution.py:432
  54.1 7.1 %collective-permute-start.8 = (bf16[400,128]{1,0:T(8,128)(2,1)S(1)}, bf16[400,128]{1,0:T(8,128)(2,1)S(1)}, u32[]{:S(2)}, u32[]{:S(2)}) collective-permute-start(bf16[400,128]{1,0:T(8,128)(2,1)S(1)} %get-tuple-element.34), channel_id=1, source_target_pairs={{0,192},{64,0},{128,64},{192,128},{1,193},{65,1},{129,65},{193,129... | collective-permute-start | bytes 307208 | tf_op jit(solution)/shard_map/ppermute | solution.py:432
  59.1 35.7 %copy-start.1 = (bf16[768,384]{1,0:T(8,128)(2,1)S(1)}, bf16[768,384]{1,0:T(8,128)(2,1)}, u32[]{:S(2)}) copy-start(bf16[768,384]{1,0:T(8,128)(2,1)} %in_weight.3) | copy-start | bytes 1769476
  59.2 35.7 %copy-start.2 = (f32[40,128]{1,0:T(8,128)S(1)}, f32[40,128]{1,0:T(8,128)}, u32[]{:S(2)}) copy-start(f32[40,128]{1,0:T(8,128)} %get-tuple-element.38.where_ref) | copy-start | bytes 61444
  64.2 30.6 %all-to-all-start.1 = ((bf16[64,16,384]{2,1,0:T(8,128)(2,1)}), bf16[64,16,384]{2,1,0:T(8,128)(2,1)S(1)}, u32[]{:S(2)}, u32[]{:S(2)}) async-start(bf16[64,16,384]{2,1,0:T(8,128)(2,1)} %shard_map.111), calls=%async_computation.1 | async-start | bytes 1572864 | tf_op jit(solution)/shard_map/all_to_all | solution.py:554

commit v9 on v8

--- a/solution.py
+++ b/solution.py
@@ -87,13 +87,13 @@
 def conv_back(grad, taps, cells):
     summed = None
     for row_off in range(3):
+        start = 8 * (2 - row_off)
         term = lax.dot_general(
-            grad,
+            grad[start : start + cells].astype(BF16),
             taps[0, row_off * DEPTH : (row_off + 1) * DEPTH],
             (((1,), (1,)), ((), ())),
             preferred_element_type=F32,
         )
-        term = term[8 * (2 - row_off) : 8 * (2 - row_off) + cells]
         summed = term if summed is None else summed + term
     grid = (cells // 8, 8, CHANNELS)
     column = lax.broadcasted_iota(jnp.int32, grid, 1)
@@ -131,8 +131,11 @@
     return center * scale, scale
 
 
-def pull_back(unit, scale, gradient):
-    slope = half_erf(unit) + unit * (PDF_SCALE * jnp.exp(-0.5 * unit * unit))
+def slope_of(unit, half):
+    return half + unit * (PDF_SCALE * jnp.exp(-0.5 * unit * unit))
+
+
+def pull_back(unit, scale, slope, gradient):
     grad = gradient * slope
     mean = jnp.mean(grad, axis=-1, keepdims=True)
     along = jnp.mean(grad * unit, axis=-1, keepdims=True)
@@ -224,20 +227,24 @@
     chosen_out[...] = jnp.where(lane == spread[:, 0:1].astype(jnp.int32), 1.0, 0.0).astype(BF16)
 
 
-def inside_kernel(own, weight, active_out, unit_out, scale_out, share_out, even, odd):
+def inside_kernel(
+    own, weight, active_out, unit_out, scale_out, slope_out, share_out, even, odd
+):
     source = own[...].astype(F32)
     store_columns(source, even, odd)
     unit, scale = normed(conv_taps((even[0:384], odd[0:384], even[16:400]), weight))
     unit_out[...] = unit
     scale_out[...] = jnp.broadcast_to(scale, scale_out.shape)
-    active = source[8:392] + unit * half_erf(unit)
+    half = half_erf(unit)
+    slope_out[...] = slope_of(unit, half)
+    active = source[8:392] + unit * half
     active_out[...] = active.astype(BF16)
     share_out[...] = jnp.where(lax.axis_index("freq") == 1, active, source[8:392]).astype(BF16)
 
 
 def border_rows(
-    above, own, below, weight, active_in, unit_in, scale_in,
-    active_out, unit_out, scale_out, share_out, even, odd,
+    above, own, below, weight, active_in, unit_in, scale_in, slope_in,
+    active_out, unit_out, scale_out, slope_out, share_out, even, odd,
 ):
     upper, lower = above[0:32].astype(F32), below[0:32].astype(F32)
     border = jnp.concatenate(
@@ -250,7 +257,12 @@
         jnp.concatenate([even[16:48], even[64:96]], axis=0),
     )
     unit, scale = normed(conv_taps(windows, weight))
-    edge = jnp.concatenate([border[8:40], border[56:88]], axis=0) + unit * half_erf(unit)
+    half = half_erf(unit)
+    slope = slope_of(unit, half)
+    slope_out[0:16] = slope[16:32]
+    slope_out[16:400] = slope_in[...]
+    slope_out[400:416] = slope[32:48]
+    edge = jnp.concatenate([border[8:40], border[56:88]], axis=0) + unit * half
     number = row_number(64)
     number = jnp.where(number < 4, number - 3, number + 45)
     edge = jnp.where(rows_valid(number), edge, 0.0)
@@ -271,18 +283,21 @@
 
 
 def second_kernel(
-    above, own, below, first_weight, active_in, unit_in, scale_in, weight, head, aim_ref,
+    above, own, below, first_weight, active_in, unit_in, scale_in, slope_in,
+    weight, head, aim_ref,
     pred, share_own, share_one, share_two, share_three, mid_out, grad_out,
-    even, odd, active_ref, unit_ref, scale_ref, border,
+    even, odd, active_ref, unit_ref, scale_ref, slope_ref, border,
 ):
     border_rows(
-        above, own, below, first_weight, active_in, unit_in, scale_in,
-        active_ref, unit_ref, scale_ref, border, even, odd,
+        above, own, below, first_weight, active_in, unit_in, scale_in, slope_in,
+        active_ref, unit_ref, scale_ref, slope_ref, border, even, odd,
     )
     active = active_ref[...].astype(F32)
     store_columns(active, even, odd)
     unit, scale = normed(conv_taps((even[0:432], odd[0:432], even[16:448]), weight))
-    top = (active[8:440] + unit * half_erf(unit)).astype(BF16)
+    half = half_erf(unit)
+    slope = slope_of(unit, half)
+    top = (active[8:440] + unit * half).astype(BF16)
     guess = jnp.dot(top, head[...], preferred_element_type=F32)
     pred[...] = guess[16:416].astype(BF16)
     aim = jnp.concatenate([above[32:48], aim_ref[...], below[32:48]], axis=0)
@@ -292,13 +307,13 @@
     grad_top = lax.dot_general(
         misfit, head[...], (((1,), (1,)), ((), ())), preferred_element_type=F32
     )
-    grad_two = pull_back(unit, scale, grad_top).astype(BF16)
+    grad_two = pull_back(unit, scale, slope, grad_top)
     grad_mid = grad_top[8:424] + conv_back(grad_two, weight, 416)
-    grad_one = pull_back(unit_ref[...], scale_ref[:, 0:1], grad_mid)
+    grad_one = pull_back(unit_ref[...], scale_ref[:, 0:1], slope_ref[...], grad_mid)
     grad_one = jnp.where(rows_valid(row_number(416) - 1), grad_one, 0.0)
     grad_out[...] = grad_one.astype(BF16)
     mid_out[...] = grad_mid[8:408]
-    share = jnp.where(lax.axis_index("freq") == 1, grad_two.astype(F32)[16:416], grad_one[8:408])
+    share = jnp.where(lax.axis_index("freq") == 1, grad_two[16:416], grad_one[8:408])
     pieces = quarters(share)
     lane = lax.broadcasted_iota(jnp.int32, (CELLS, 128), 1)
     for step, share_out in enumerate((share_own, share_one, share_two, share_three)):
@@ -316,7 +331,7 @@
 
 
 def tail_kernel(grad_ref, mid_ref, weight, chosen, out):
-    grad_cells = mid_ref[...] + conv_back(grad_ref[...], weight, CELLS)
+    grad_cells = mid_ref[...] + conv_back(grad_ref[...].astype(F32), weight, CELLS)
     out[...] = jnp.dot(chosen[...], grad_cells.astype(BF16), preferred_element_type=F32)
 
 
@@ -483,6 +498,7 @@
             shape((384, CHANNELS)),
             shape((384, CHANNELS), F32),
             shape((384, 128), F32),
+            shape((384, CHANNELS), F32),
             shape((384, CHANNELS)),
         ),
         columns,
@@ -505,6 +521,7 @@
             pltpu.VMEM((448, CHANNELS), BF16),
             pltpu.VMEM((416, CHANNELS), F32),
             pltpu.VMEM((416, 128), F32),
+            pltpu.VMEM((416, CHANNELS), F32),
             pltpu.VMEM((32, CHANNELS), BF16),
         ],
         3_500_000_000,

time: 96.5 us -> 96.6 us (level)
  no operation moved by 1% of the time
where the time goes in v9:
time: 96.6 us; the launch traced here: 96.2 us
  starting transfers between devices  35.9 us (37%)
  waiting for transfers between devices  31.6 us (33%)
  Pallas kernels  20.6 us (21%)
  local copies, waits for them, and re-layouts  5.61 us (6%)
  other arithmetic  1.66 us (2%)
    all_to_all x1, waiting for transfers between devices, per_device(): lax.all_to_all(terms, TM_FREQ, split_axis=0, concat_axis=0, tiled=True)  22.2 us
    pallas_call x10, Pallas kernels, call(): pl.pallas_call(kernel, out_shape=shapes, in_specs=[VMEM] * len(operands),...  20.6 us
    ppermute x9, starting transfers between devices, send(): return lax.ppermute(value, axis, pairs)  18.3 us
    all_to_all x1, starting transfers between devices, per_device(): lax.all_to_all(packed, TM_FREQ, split_axis=0, concat_axis=0, tiled=True)  9.89 us
    all_to_all x1, starting transfers between devices, per_device(): lax.all_to_all(terms, TM_FREQ, split_axis=0, concat_axis=0, tiled=True)  7.7 us
    all_to_all x1, waiting for transfers between devices, per_device(): lax.all_to_all(packed, TM_FREQ, split_axis=0, concat_axis=0, tiled=True)  6.95 us
    slice x1, local copies, waits for them, and re-layouts, per_device(): weights = [conv_weight[layer:layer + 1] for layer in range(2)]  4.6 us
    ppermute x9, waiting for transfers between devices, send(): return lax.ppermute(value, axis, pairs)  2.45 us
  transfers between devices with their start and end apart: 11, of which 4 were waited for; matrix products, arithmetic and copies ran while one was open for 6% of the time, Pallas kernels for 16%

profile of v9, /device:TPU:1, one launch (start us, length us, event | category | flops | bytes accessed | tf_op | source)
XLA Modules:
  0.0 96.2 jit_solution(6315517692970245535)
XLA Ops:
  0.6 0.7 compare_convert_fusion
  1.3 0.1 copy.11
  1.4 0.1 broadcast_in_dim.4
  1.6 1.0 %pad_maximum_fusion = bf16[50,4,384]{2,1,0:T(4,128)(2,1)S(1)} fusion(bf16[50,4,128]{2,1,0:T(4,128)(2,1)S(1)} %broadcast_in_dim.4, bf16[50,4,256]{2,1,0:T(4,128)(2,1)} %param.11), kind=kLoop, calls=%fused_computation | loop fusion | flops 307200 | bytes 307200 | tf_op jit(solution)/shard_map/concatenate | solution.py:470
  2.6 3.3 %collective-permute-start = (bf16[200,384]{1,0:T(8,128)(2,1)S(1)}, bf16[200,384]{1,0:T(8,128)(2,1)S(1)}, u32[]{:S(2)}, u32[]{:S(2)}) collective-permute-start(bf16[200,384]{1,0:T(8,128)(2,1)S(1)} %reshape.15.own_aim), channel_id=1, source_target_pairs={{0,4},{4,0},{1,5},{5,1},{2,6},{6,2},{3,7},{7,3},{8,12},{12,8},{9,1... | collective-permute-start | bytes 460808 | tf_op jit(solution)/shard_map/ppermute | solution.py:447
  5.9 2.3 %shard_map.103 = (bf16[512,256]{1,0:T(8,128)(2,1)}, f32[40,128]{1,0:T(8,128)}) custom-call(bf16[40,768]{1,0:T(8,128)(2,1)} %tokens.1, s32[2,40]{1,0:T(2,128)} %placement.1, bf16[768,384]{1,0:T(8,128)(2,1)} %in_weight.3), custom_call_target="tpu_custom_call" | custom-call | flops 80000000 | bytes 200000 | tf_op jit(solution)/shard_map/pallas_call | solution.py:425
  8.2 9.9 %all-to-all-start = ((bf16[64,8,256]{2,1,0:T(8,128)(2,1)}), bf16[64,8,256]{2,1,0:T(8,128)(2,1)S(1)}, u32[]{:S(2)}, u32[]{:S(2)}) async-start(bf16[64,8,256]{2,1,0:T(8,128)(2,1)} %bitcast.6), calls=%async_computation | async-start | bytes 524288 | tf_op jit(solution)/shard_map/all_to_all | solution.py:468
  18.1 0.0 copy-start.4
  18.1 4.6 %fusion = (bf16[1,3456,384]{2,1,0:T(8,128)(2,1)}, bf16[1,3456,384]{2,1,0:T(8,128)(2,1)S(1)}) fusion(bf16[2,3456,384]{2,1,0:T(8,128)(2,1)} %param.14), kind=kLoop, calls=%fused_computation.3 | loop fusion | bytes 10616832 | tf_op jit(solution)/shard_map/slice | solution.py:474
  22.7 0.0 copy-done.4
  22.7 0.0 collective-permute-done.other_aim
  22.7 0.4 shard_map.104.aim.aim_ref
  23.1 7.0 %all-to-all-done = bf16[64,8,256]{2,1,0:T(8,128)(2,1)S(1)} async-done(((bf16[64,8,256]{2,1,0:T(8,128)(2,1)}), bf16[64,8,256]{2,1,0:T(8,128)(2,1)S(1)}, u32[]{:S(2)}, u32[]{:S(2)}) %all-to-all-start) | async-done | bytes 262176 | tf_op jit(solution)/shard_map/all_to_all | solution.py:468
  30.1 0.0 copy-start
  30.1 0.0 copy-start.3
  30.1 1.1 %shard_map.105 = (bf16[400,384]{1,0:T(8,128)(2,1)S(1)}, bf16[48,384]{1,0:T(8,128)(2,1)S(1)}, bf16[48,384]{1,0:T(8,128)(2,1)S(1)}, bf16[512,400]{1,0:T(8,128)(2,1)S(1)}) custom-call(bf16[512,256]{1,0:T(8,128)(2,1)S(1)} %bitcast.4, bf16[400,384]{1,0:T(8,128)(2,1)S(1)} %shard_map.104.aim.aim_ref, bf16[1,384]{1,0:T(2,128)(2,1)S(1)} %broadcast_in_dim.10.token), custom_call_target="tpu_custom_call" | custom-call | flops 300000000 | bytes 750000 | tf_op jit(solution)/shard_map/pallas_call | solution.py:425
  31.2 3.1 %collective-permute-start.1 = (bf16[48,384]{1,0:T(8,128)(2,1)S(1)}, bf16[48,384]{1,0:T(8,128)(2,1)S(1)}, u32[]{:S(2)}, u32[]{:S(2)}) collective-permute-start(bf16[48,384]{1,0:T(8,128)(2,1)S(1)} %get-tuple-element.24), channel_id=1, source_target_pairs={{0,8},{8,16},{16,24},{24,32},{32,40},{40,48},{48,56},{56,64},{64,7... | collective-permute-start | bytes 110600 | tf_op jit(solution)/shard_map/ppermute | solution.py:447
  34.2 1.3 %collective-permute-start.2 = (bf16[48,384]{1,0:T(8,128)(2,1)S(1)}, bf16[48,384]{1,0:T(8,128)(2,1)S(1)}, u32[]{:S(2)}, u32[]{:S(2)}) collective-permute-start(bf16[48,384]{1,0:T(8,128)(2,1)S(1)} %get-tuple-element.26), channel_id=1, source_target_pairs={{8,0},{16,8},{24,16},{32,24},{40,32},{48,40},{56,48},{64,56},{72,6... | collective-permute-start | bytes 110600 | tf_op jit(solution)/shard_map/ppermute | solution.py:447
  35.5 2.6 %shard_map.106 = (bf16[384,384]{1,0:T(8,128)(2,1)S(1)}, f32[384,384]{1,0:T(8,128)S(1)}, f32[384,128]{1,0:T(8,128)S(1)}, f32[384,384]{1,0:T(8,128)S(1)}, bf16[384,384]{1,0:T(8,128)(2,1)S(1)}) custom-call(bf16[400,384]{1,0:T(8,128)(2,1)S(1)} %get-tuple-element.25.own, bf16[1,3456,384]{2,1,0:T(8,128)(2,1)S(1)} %get-tuple-element.44.weight.first_weight), custom_call_target="tpu_custom_call" | custom-call | flops 1200000000 | bytes 3000000 | tf_op jit(solution)/shard_map/pallas_call | solution.py:425
  38.1 4.1 %collective-permute-start.3 = (bf16[384,384]{1,0:T(8,128)(2,1)S(1)}, bf16[384,384]{1,0:T(8,128)(2,1)S(1)}, u32[]{:S(2)}, u32[]{:S(2)}) collective-permute-start(bf16[384,384]{1,0:T(8,128)(2,1)S(1)} %get-tuple-element.32.inner), channel_id=1, source_target_pairs={{0,64},{64,128},{128,192},{192,0},{1,65},{65,129},{129,193},{193,1... | collective-permute-start | bytes 884744 | tf_op jit(solution)/shard_map/ppermute | solution.py:447
  42.2 2.6 %collective-permute-start.4 = (bf16[384,384]{1,0:T(8,128)(2,1)S(1)}, bf16[384,384]{1,0:T(8,128)(2,1)S(1)}, u32[]{:S(2)}, u32[]{:S(2)}) collective-permute-start(bf16[384,384]{1,0:T(8,128)(2,1)S(1)} %get-tuple-element.32.inner), channel_id=1, source_target_pairs={{0,128},{64,192},{128,0},{192,64},{1,129},{65,193},{129,1},{193,65... | collective-permute-start | bytes 884744 | tf_op jit(solution)/shard_map/ppermute | solution.py:447
  44.8 1.1 %collective-permute-start.5 = (bf16[384,384]{1,0:T(8,128)(2,1)S(1)}, bf16[384,384]{1,0:T(8,128)(2,1)S(1)}, u32[]{:S(2)}, u32[]{:S(2)}) collective-permute-start(bf16[384,384]{1,0:T(8,128)(2,1)S(1)} %get-tuple-element.32.inner), channel_id=1, source_target_pairs={{0,192},{64,0},{128,64},{192,128},{1,193},{65,1},{129,65},{193,129... | collective-permute-start | bytes 884744 | tf_op jit(solution)/shard_map/ppermute | solution.py:447
  45.8 0.0 collective-permute-done.1.above
  45.9 0.0 collective-permute-done.2.below
  45.9 0.0 copy-done
  45.9 0.0 copy-done.3
  45.9 6.3 %shard_map.107 = (bf16[400,256]{1,0:T(8,128)(2,1)S(1)}, bf16[400,128]{1,0:T(8,128)(2,1)S(1)}, bf16[400,128]{1,0:T(8,128)(2,1)S(1)}, bf16[400,128]{1,0:T(8,128)(2...) custom-call(bf16[48,384]{1,0:T(8,128)(2,1)S(1)} %collective-permute-done.1.above, ...), custom_call_target="tpu_custom_call" | custom-call | flops 3500000000 | bytes 8750000 | tf_op jit(solution)/shard_map/pallas_call | solution.py:425
  52.2 0.5 collective-permute-start.6
  52.7 0.8 collective-permute-start.7
  53.5 0.0 collective-permute-done.3.refs_0_
  53.5 1.7 %collective-permute-start.8 = (bf16[400,128]{1,0:T(8,128)(2,1)S(1)}, bf16[400,128]{1,0:T(8,128)(2,1)S(1)}, u32[]{:S(2)}, u32[]{:S(2)}) collective-permute-start(bf16[400,128]{1,0:T(8,128)(2,1)S(1)} %get-tuple-element.36), channel_id=1, source_target_pairs={{0,192},{64,0},{128,64},{192,128},{1,193},{65,1},{129,65},{193,129... | collective-permute-start | bytes 307208 | tf_op jit(solution)/shard_map/ppermute | solution.py:447
  55.2 2.5 %shard_map.110.refs_3_ = f32[512,384]{1,0:T(8,128)S(1)} custom-call(bf16[416,384]{1,0:T(8,128)(2,1)S(1)} %get-tuple-element.37.grad_ref, f32[400,384]{1,0:T(8,128)S(1)} %get-tuple-element.38.mid_ref, bf16[1,3456,384]{2,1,0:T(8,128)(2,1)S(1)} %get-tuple-element.44.weight.first_weight, bf16[512,400]{1,0:T(8,128)(2,1)S(1)} %get-tuple-element.39.chosen), custom_call_target="tpu_custom_call" | custom-call | flops 1200000000 | bytes 3000000 | tf_op jit(solution)/shard_map/pallas_call | solution.py:425
  57.7 0.9 shard_map.108.summed_ref
  58.6 0.0 collective-permute-done.4.refs_1_
  58.6 0.0 collective-permute-done.5.refs_2_
  58.6 0.3 shard_map.109.turned
  58.9 0.0 copy-start.1
  58.9 0.0 copy-start.2
  58.9 2.2 %collective-permute-done.6.refs_0_ = bf16[400,128]{1,0:T(8,128)(2,1)S(1)} collective-permute-done((bf16[400,128]{1,0:T(8,128)(2,1)S(1)}, bf16[400,128]{1,0:T(8,128)(2,1)S(1)}, u32[]{:S(2)}, u32[]{:S(2)}) %collective-permute-start.6) | collective-permute-done | bytes 102432 | tf_op jit(solution)/shard_map/ppermute | solution.py:447
  61.1 0.3 collective-permute-done.7.refs_1_
  61.3 0.0 collective-permute-done.8.refs_2_
  61.3 3.0 %shard_map.111 = bf16[64,16,384]{2,1,0:T(8,128)(2,1)} custom-call(f32[384,1152]{1,0:T(8,128)S(1)} %shard_map.108.summed_ref, bf16[3,384,384]{2,1,0:T(8,128)(2,1)S(1)} %shard_map.109.turned, bf16[400,128]{1,0:T(8,128)(2,1)S(1)} %collective-permute-done.6.refs_0_, bf16[400,128]{1,0:T(8,128)(2,1)S(1)} %collective-permute-done.7.refs_1_, ...), custom_call_target="tpu_custom_call" | custom-call | flops 1500000000 | bytes 3750000 | tf_op jit(solution)/shard_map/pallas_call | solution.py:425
  64.4 7.7 %all-to-all-start.1 = ((bf16[64,16,384]{2,1,0:T(8,128)(2,1)}), bf16[64,16,384]{2,1,0:T(8,128)(2,1)S(1)}, u32[]{:S(2)}, u32[]{:S(2)}) async-start(bf16[64,16,384]{2,1,0:T(8,128)(2,1)} %shard_map.111), calls=%async_computation.1 | async-start | bytes 1572864 | tf_op jit(solution)/shard_map/all_to_all | solution.py:571
  72.1 0.7 constant_dynamic-slice_fusion
  72.8 22.2 %all-to-all-done.1.arrived = bf16[64,16,384]{2,1,0:T(8,128)(2,1)S(1)} async-done(((bf16[64,16,384]{2,1,0:T(8,128)(2,1)}), bf16[64,16,384]{2,1,0:T(8,128)(2,1)S(1)}, u32[]{:S(2)}, u32[]{:S(2)}) %all-to-all-start.1) | async-done | bytes 786464 | tf_op jit(solution)/shard_map/all_to_all | solution.py:571
  95.0 0.0 copy-done.1
  95.0 0.0 copy-done.2
  95.0 1.2 %shard_map.112 = (f32[40,768]{1,0:T(8,128)}, f32[54,2,384]{2,1,0:T(2,128)}) custom-call(bf16[64,16,384]{2,1,0:T(8,128)(2,1)S(1)} %all-to-all-done.1.arrived, f32[40,128]{1,0:T(8,128)S(1)} %copy-done.2, bf16[768,384]{1,0:T(8,128)(2,1)S(1)} %copy-done.1), custom_call_target="tpu_custom_call" | custom-call | flops 80000000 | bytes 200000 | tf_op jit(solution)/shard_map/pallas_call | solution.py:425
  (2 shorter events, 0.0 us)
Async XLA Ops:
  2.6 20.1 %collective-permute-start = (bf16[200,384]{1,0:T(8,128)(2,1)S(1)}, bf16[200,384]{1,0:T(8,128)(2,1)S(1)}, u32[]{:S(2)}, u32[]{:S(2)}) collective-permute-start(bf16[200,384]{1,0:T(8,128)(2,1)S(1)} %reshape.15.own_aim), channel_id=1, source_target_pairs={{0,4},{4,0},{1,5},{5,1},{2,6},{6,2},{3,7},{7,3},{8,12},{12,8},{9,1... | collective-permute-start | bytes 460808 | tf_op jit(solution)/shard_map/ppermute | solution.py:447
  8.2 21.9 %all-to-all-start = ((bf16[64,8,256]{2,1,0:T(8,128)(2,1)}), bf16[64,8,256]{2,1,0:T(8,128)(2,1)S(1)}, u32[]{:S(2)}, u32[]{:S(2)}) async-start(bf16[64,8,256]{2,1,0:T(8,128)(2,1)} %bitcast.6), calls=%async_computation | async-start | bytes 524288 | tf_op jit(solution)/shard_map/all_to_all | solution.py:468
  18.1 4.6 %copy-start.4 = (bf16[384]{0:T(512)(128)(2,1)S(1)}, bf16[384]{0:T(512)(128)(2,1)}, u32[]{:S(2)}) copy-start(bf16[384]{0:T(512)(128)(2,1)} %param.13) | copy-start | bytes 2308
  30.1 15.8 %copy-start = (bf16[1,3456,384]{2,1,0:T(8,128)(2,1)S(1)}, bf16[1,3456,384]{2,1,0:T(8,128)(2,1)}, u32[]{:S(2)}) copy-start(bf16[1,3456,384]{2,1,0:T(8,128)(2,1)} %get-tuple-element.43.weight) | copy-start | bytes 7962628
  30.1 15.8 %copy-start.3 = (bf16[384,256]{1,0:T(8,128)(2,1)S(1)}, bf16[384,256]{1,0:T(8,128)(2,1)}, u32[]{:S(2)}) copy-start(bf16[384,256]{1,0:T(8,128)(2,1)} %head.1) | copy-start | bytes 589828
  31.2 14.7 %collective-permute-start.1 = (bf16[48,384]{1,0:T(8,128)(2,1)S(1)}, bf16[48,384]{1,0:T(8,128)(2,1)S(1)}, u32[]{:S(2)}, u32[]{:S(2)}) collective-permute-start(bf16[48,384]{1,0:T(8,128)(2,1)S(1)} %get-tuple-element.24), channel_id=1, source_target_pairs={{0,8},{8,16},{16,24},{24,32},{32,40},{40,48},{48,56},{56,64},{64,7... | collective-permute-start | bytes 110600 | tf_op jit(solution)/shard_map/ppermute | solution.py:447
  34.2 11.6 %collective-permute-start.2 = (bf16[48,384]{1,0:T(8,128)(2,1)S(1)}, bf16[48,384]{1,0:T(8,128)(2,1)S(1)}, u32[]{:S(2)}, u32[]{:S(2)}) collective-permute-start(bf16[48,384]{1,0:T(8,128)(2,1)S(1)} %get-tuple-element.26), channel_id=1, source_target_pairs={{8,0},{16,8},{24,16},{32,24},{40,32},{48,40},{56,48},{64,56},{72,6... | collective-permute-start | bytes 110600 | tf_op jit(solution)/shard_map/ppermute | solution.py:447
  38.1 15.4 %collective-permute-start.3 = (bf16[384,384]{1,0:T(8,128)(2,1)S(1)}, bf16[384,384]{1,0:T(8,128)(2,1)S(1)}, u32[]{:S(2)}, u32[]{:S(2)}) collective-permute-start(bf16[384,384]{1,0:T(8,128)(2,1)S(1)} %get-tuple-element.32.inner), channel_id=1, source_target_pairs={{0,64},{64,128},{128,192},{192,0},{1,65},{65,129},{129,193},{193,1... | collective-permute-start | bytes 884744 | tf_op jit(solution)/shard_map/ppermute | solution.py:447
  42.2 16.4 %collective-permute-start.4 = (bf16[384,384]{1,0:T(8,128)(2,1)S(1)}, bf16[384,384]{1,0:T(8,128)(2,1)S(1)}, u32[]{:S(2)}, u32[]{:S(2)}) collective-permute-start(bf16[384,384]{1,0:T(8,128)(2,1)S(1)} %get-tuple-element.32.inner), channel_id=1, source_target_pairs={{0,128},{64,192},{128,0},{192,64},{1,129},{65,193},{129,1},{193,65... | collective-permute-start | bytes 884744 | tf_op jit(solution)/shard_map/ppermute | solution.py:447
  44.8 13.8 %collective-permute-start.5 = (bf16[384,384]{1,0:T(8,128)(2,1)S(1)}, bf16[384,384]{1,0:T(8,128)(2,1)S(1)}, u32[]{:S(2)}, u32[]{:S(2)}) collective-permute-start(bf16[384,384]{1,0:T(8,128)(2,1)S(1)} %get-tuple-element.32.inner), channel_id=1, source_target_pairs={{0,192},{64,0},{128,64},{192,128},{1,193},{65,1},{129,65},{193,129... | collective-permute-start | bytes 884744 | tf_op jit(solution)/shard_map/ppermute | solution.py:447
  52.2 8.9 %collective-permute-start.6 = (bf16[400,128]{1,0:T(8,128)(2,1)S(1)}, bf16[400,128]{1,0:T(8,128)(2,1)S(1)}, u32[]{:S(2)}, u32[]{:S(2)}) collective-permute-start(bf16[400,128]{1,0:T(8,128)(2,1)S(1)} %get-tuple-element.34), channel_id=1, source_target_pairs={{0,64},{64,128},{128,192},{192,0},{1,65},{65,129},{129,193},{193,1... | collective-permute-start | bytes 307208 | tf_op jit(solution)/shard_map/ppermute | solution.py:447
  52.7 8.7 %collective-permute-start.7 = (bf16[400,128]{1,0:T(8,128)(2,1)S(1)}, bf16[400,128]{1,0:T(8,128)(2,1)S(1)}, u32[]{:S(2)}, u32[]{:S(2)}) collective-permute-start(bf16[400,128]{1,0:T(8,128)(2,1)S(1)} %get-tuple-element.35), channel_id=1, source_target_pairs={{0,128},{64,192},{128,0},{192,64},{1,129},{65,193},{129,1},{193,65... | collective-permute-start | bytes 307208 | tf_op jit(solution)/shard_map/ppermute | solution.py:447
  53.5 7.9 %collective-permute-start.8 = (bf16[400,128]{1,0:T(8,128)(2,1)S(1)}, bf16[400,128]{1,0:T(8,128)(2,1)S(1)}, u32[]{:S(2)}, u32[]{:S(2)}) collective-permute-start(bf16[400,128]{1,0:T(8,128)(2,1)S(1)} %get-tuple-element.36), channel_id=1, source_target_pairs={{0,192},{64,0},{128,64},{192,128},{1,193},{65,1},{129,65},{193,129... | collective-permute-start | bytes 307208 | tf_op jit(solution)/shard_map/ppermute | solution.py:447
  58.9 36.1 %copy-start.1 = (bf16[768,384]{1,0:T(8,128)(2,1)S(1)}, bf16[768,384]{1,0:T(8,128)(2,1)}, u32[]{:S(2)}) copy-start(bf16[768,384]{1,0:T(8,128)(2,1)} %in_weight.3) | copy-start | bytes 1769476
  58.9 36.1 %copy-start.2 = (f32[40,128]{1,0:T(8,128)S(1)}, f32[40,128]{1,0:T(8,128)}, u32[]{:S(2)}) copy-start(f32[40,128]{1,0:T(8,128)} %get-tuple-element.40.where_ref) | copy-start | bytes 61444
  64.4 30.6 %all-to-all-start.1 = ((bf16[64,16,384]{2,1,0:T(8,128)(2,1)}), bf16[64,16,384]{2,1,0:T(8,128)(2,1)S(1)}, u32[]{:S(2)}, u32[]{:S(2)}) async-start(bf16[64,16,384]{2,1,0:T(8,128)(2,1)} %shard_map.111), calls=%async_computation.1 | async-start | bytes 1572864 | tf_op jit(solution)/shard_map/all_to_all | solution.py:571
